TPU v7x, 32 devices: a whole 2x2x4 slice. The times are simulated.
32 devices in a mesh: rows: 8 (over y, x, core), blk: 4 (over z).
Axes of the slice: x: 2, y: 2, z: 4, core: 2. Of those that a mesh axis runs over, the one named last changes fastest.
Arguments:
- tokens: bfloat16 [16, 1024, 768], P('rows', 'blk'), may hold values from -6 to 6
- segments: int32 [16, 1024], P('rows', 'blk'), may hold values from 0 to 6, as said below
- query_weight: bfloat16 [768, 768], replicated, may hold values from -0.3125 to 0.3125
- query_bias: float32 [768], replicated, may hold values from -3 to 3
- key_weight: bfloat16 [768, 768], replicated, may hold values from -0.21875 to 0.21875
- value_weight: bfloat16 [768, 768], replicated, may hold values from -0.21875 to 0.21875
- value_bias: float32 [768], replicated, may hold values from -0.125 to 0.125
- out_weight: bfloat16 [768, 768], replicated, may hold values from -3 to 3
- out_bias: float32 [768], replicated, may hold values from -0.625 to 0.625
- first_gain: float32 [768], replicated, may hold values from 0.5 to 1.5
- first_shift: float32 [768], replicated, may hold values from -0.625 to 0.625
- up_weight: bfloat16 [768, 3072], replicated, may hold values from -0.21875 to 0.21875
- up_bias: float32 [3072], replicated, may hold values from -0.625 to 0.625
- down_weight: bfloat16 [3072, 768], replicated, may hold values from -0.109375 to 0.109375
- down_bias: float32 [768], replicated, may hold values from -0.625 to 0.625
- second_gain: float32 [768], replicated, may hold values from 0.5 to 1.5
- second_shift: float32 [768], replicated, may hold values from -0.625 to 0.625
- cotangent: bfloat16 [16, 1024, 768], P('rows', 'blk'), may hold values from -6 to 6
Outputs:
- layer_output: bfloat16 [16, 1024, 768], P('rows', 'blk')
- pooled: float32 [16, 6, 1728], P('rows')
- grad_tokens: bfloat16 [16, 1024, 768], P('rows', 'blk')
- grad_query_weight: float32 [768, 768], replicated
- grad_query_bias: float32 [768], replicated
- grad_key_weight: float32 [768, 768], replicated
- grad_value_weight: float32 [768, 768], replicated
- grad_value_bias: float32 [768], replicated
- grad_out_weight: float32 [768, 768], replicated
- grad_out_bias: float32 [768], replicated
- grad_first_gain: float32 [768], replicated
- grad_first_shift: float32 [768], replicated
- grad_up_weight: float32 [768, 3072], replicated
- grad_up_bias: float32 [3072], replicated
- grad_down_weight: float32 [3072, 768], replicated
- grad_down_bias: float32 [768], replicated
- grad_second_gain: float32 [768], replicated
- grad_second_shift: float32 [768], replicated
Inputs may be any that keep to these rules, and one draw needn't show every extreme that they name: `segments`: in every sequence the ids never fall until padding begins; padding (0) fills the sequence's end, possibly empty; every id 1 to 6 appears in every sequence, each on consecutive tokens.
All inputs are finite; a program needn't handle non-finite values.
Results may differ from a plain program's by a relative error of at most 0.019.
Values may be sent and summed in bfloat16 or wider, within the bound.
No kernel may reach another device: no remote copies, remote signals or barrier semaphores. Data moves between devices by JAX's collectives and lax.ppermute only.
A program may use at most 192 MiB of HBM per device.

v0:
```python
from functools import partial

import jax
import jax.numpy as jnp
from jax import lax
from jax.sharding import PartitionSpec as P

D = 768
H = 12
HD = 64
NSEG = 6


query_scale = 0.125
norm_eps = 1e-12
pool_eps = 1e-06


def matmul(left, right):
    return jnp.dot(left, right, preferred_element_type=jnp.float32)


def layer_norm(rows_in, gain_vec, shift_vec):
    row_mean = jnp.mean(rows_in, axis=-1, keepdims=True)
    centred = rows_in - row_mean
    inverse = lax.rsqrt(jnp.mean(centred * centred, axis=-1, keepdims=True) + norm_eps)
    normed = centred * inverse
    return (normed * gain_vec + shift_vec, normed, inverse)


def norm_backward(upstream, normed, inverse, gain_vec):
    scaled = upstream * gain_vec
    first_mean = jnp.mean(scaled, axis=-1, keepdims=True)
    second_mean = jnp.mean(scaled * normed, axis=-1, keepdims=True)
    return inverse * (scaled - first_mean - normed * second_mean)


def block_weights(query_heads, key_heads, seg_query, seg_keys):
    scores = jnp.einsum(
        "sqhd,skhd->shqk", query_heads, key_heads, preferred_element_type=jnp.float32
    )
    allowed = seg_query[:, None, :, None] == seg_keys[:, None, None, :]
    return jnp.where(allowed, jnp.exp(scores), 0.0)


def matryoshka(averages):
    pieces = []
    for prefix in (D, D * 2 // 3, D // 3, D // 6, D // 12):
        leading = averages[..., :prefix]
        centred = leading - jnp.mean(leading, axis=-1, keepdims=True)
        pieces.append(
            centred * lax.rsqrt(jnp.mean(centred * centred, axis=-1, keepdims=True) + pool_eps)
        )
    return jnp.concatenate(pieces, axis=-1)


def local(
    tokens,
    segments,
    query_weight,
    query_bias,
    key_weight,
    value_weight,
    value_bias,
    out_weight,
    out_bias,
    first_gain,
    first_shift,
    up_weight,
    up_bias,
    down_weight,
    down_bias,
    second_gain,
    second_shift,
    cotangent,
):
    num_seq, tok_rows, width = tokens.shape
    total_rows = num_seq * tok_rows
    flat_in = tokens.reshape(total_rows, width)
    queries = (query_scale * (matmul(flat_in, query_weight) + query_bias)).astype(jnp.bfloat16)
    key_rows = matmul(flat_in, key_weight).astype(jnp.bfloat16)
    value_rows = (matmul(flat_in, value_weight) + value_bias).astype(jnp.bfloat16)
    head_shape = (num_seq, tok_rows, H, HD)
    query_heads = queries.reshape(head_shape)
    seg_query = segments.astype(jnp.bfloat16)
    key_send = key_rows.reshape(1, num_seq, tok_rows, width)
    value_send = value_rows.reshape(1, num_seq, tok_rows, width)
    seg_send = seg_query.reshape(1, num_seq, tok_rows)

    def forward_block(state, block_data):
        numer_sum, total_sum = state
        key_block, value_block, seg_block = block_data
        weights = block_weights(query_heads, key_block.reshape(head_shape), seg_query, seg_block)
        total_sum = total_sum + jnp.sum(weights, axis=3)
        numer_sum = numer_sum + jnp.einsum(
            "shqk,skhd->sqhd",
            weights.astype(jnp.bfloat16),
            value_block.reshape(head_shape),
            preferred_element_type=jnp.float32,
        )
        return ((numer_sum, total_sum), None)

    initial = (jnp.zeros(head_shape, jnp.float32), jnp.zeros((num_seq, H, tok_rows), jnp.float32))
    numer_sum, total_sum = lax.scan(
        forward_block,
        initial,
        (
            lax.all_gather(key_send, "blk", axis=0, tiled=True),
            lax.all_gather(value_send, "blk", axis=0, tiled=True),
            lax.all_gather(seg_send, "blk", axis=0, tiled=True),
        ),
    )[0]
    totals_q = jnp.transpose(total_sum, (0, 2, 1))[..., None]
    attended = numer_sum / totals_q
    attended_low = attended.reshape(total_rows, width).astype(jnp.bfloat16)
    branch = matmul(attended_low, out_weight) + out_bias
    hidden, normed_one, inverse_one = layer_norm(
        flat_in.astype(jnp.float32) + branch, first_gain, first_shift
    )
    hidden_low = hidden.astype(jnp.bfloat16)
    preact = matmul(hidden_low, up_weight) + up_bias
    activation_full, gelu_pull = jax.vjp(partial(jax.nn.gelu, approximate=False), preact)
    activation = activation_full.astype(jnp.bfloat16)
    feed_out = matmul(activation, down_weight) + down_bias
    outputs, normed_two, inverse_two = layer_norm(hidden + feed_out, second_gain, second_shift)
    out_seq = outputs.reshape(num_seq, tok_rows, width)
    labels = jnp.arange(1, NSEG + 1, dtype=jnp.int32)
    onehot = (segments[:, None, :] == labels[None, :, None]).astype(jnp.float32)
    seg_sums = jnp.einsum(
        "snt,std->snd",
        onehot,
        out_seq,
        precision=lax.Precision.HIGHEST,
        preferred_element_type=jnp.float32,
    )
    seg_counts = jnp.sum(onehot, axis=2)
    seg_sums, seg_counts = (
        lax.psum(seg_sums.astype(jnp.bfloat16), "blk").astype(jnp.float32),
        lax.psum(seg_counts.astype(jnp.bfloat16), "blk").astype(jnp.float32),
    )
    pooled = matryoshka(seg_sums / seg_counts[..., None])
    upstream = cotangent.reshape(total_rows, width).astype(jnp.float32)
    grad_second_gain = jnp.sum(upstream * normed_two, axis=0)
    grad_second_shift = jnp.sum(upstream, axis=0)
    d_resid_two = norm_backward(upstream, normed_two, inverse_two, second_gain)
    d_feed = d_resid_two.astype(jnp.bfloat16)
    grad_down_weight = jnp.einsum(
        "rf,rd->fd", activation, d_feed, preferred_element_type=jnp.float32
    )
    grad_down_bias = jnp.sum(d_feed.astype(jnp.float32), axis=0)
    d_activation = jnp.einsum("rd,fd->rf", d_feed, down_weight, preferred_element_type=jnp.float32)
    d_preact = gelu_pull(d_activation)[0].astype(jnp.bfloat16)
    grad_up_weight = jnp.einsum(
        "rd,rf->df", hidden_low, d_preact, preferred_element_type=jnp.float32
    )
    grad_up_bias = jnp.sum(d_preact.astype(jnp.float32), axis=0)
    d_hidden = d_resid_two + jnp.einsum(
        "rf,df->rd", d_preact, up_weight, preferred_element_type=jnp.float32
    )
    grad_first_gain = jnp.sum(d_hidden * normed_one, axis=0)
    grad_first_shift = jnp.sum(d_hidden, axis=0)
    d_resid_one = norm_backward(d_hidden, normed_one, inverse_one, first_gain)
    d_branch = d_resid_one.astype(jnp.bfloat16)
    grad_out_weight = jnp.einsum(
        "rd,re->de", attended_low, d_branch, preferred_element_type=jnp.float32
    )
    grad_out_bias = jnp.sum(d_branch.astype(jnp.float32), axis=0)
    d_attended = jnp.einsum(
        "re,de->rd", d_branch, out_weight, preferred_element_type=jnp.float32
    ).reshape(head_shape)
    d_total = -jnp.sum(d_attended * attended, axis=3) / totals_q[..., 0]
    d_total_by_head = jnp.transpose(d_total, (0, 2, 1))
    d_total_heads = d_total_by_head[..., None]
    d_numer = (d_attended / totals_q).astype(jnp.bfloat16)
    back_keys = (
        lax.all_gather(key_send, "blk", axis=0, tiled=True),
        lax.all_gather(value_send, "blk", axis=0, tiled=True),
        lax.all_gather(seg_send, "blk", axis=0, tiled=True),
    )
    zero_heads = jnp.zeros(head_shape, jnp.float32)

    def backward_block(query_grad, block_data):
        key_block, value_block, seg_block = block_data
        key_heads = key_block.reshape(head_shape)
        value_heads = value_block.reshape(head_shape)
        weights = block_weights(query_heads, key_heads, seg_query, seg_block)
        d_prob = jnp.einsum(
            "sqhd,skhd->shqk", d_numer, value_heads, preferred_element_type=jnp.float32
        )
        d_scores = (weights * (d_prob + d_total_heads)).astype(jnp.bfloat16)
        query_grad = query_grad + jnp.einsum(
            "shqk,skhd->sqhd", d_scores, key_heads, preferred_element_type=jnp.float32
        )
        key_grad = jnp.einsum(
            "shqk,sqhd->skhd", d_scores, query_heads, preferred_element_type=jnp.float32
        )
        value_grad = jnp.einsum(
            "shqk,sqhd->skhd",
            weights.astype(jnp.bfloat16),
            d_numer,
            preferred_element_type=jnp.float32,
        )
        joined = jnp.concatenate(
            [
                key_grad.reshape(num_seq, tok_rows, width),
                value_grad.reshape(num_seq, tok_rows, width),
            ],
            axis=-1,
        )
        return (query_grad, joined)

    query_grad, pair_terms = lax.scan(backward_block, zero_heads, back_keys)
    pair_sums = lax.psum_scatter(
        pair_terms.astype(jnp.bfloat16), "blk", scatter_dimension=0, tiled=True
    ).astype(jnp.float32)[0]
    d_key = pair_sums[..., :width].reshape(total_rows, width).astype(jnp.bfloat16)
    d_value = pair_sums[..., width:].reshape(total_rows, width).astype(jnp.bfloat16)
    d_query = query_grad.reshape(total_rows, width).astype(jnp.bfloat16) * query_scale
    grad_query_weight = jnp.einsum(
        "rd,re->de", flat_in, d_query, preferred_element_type=jnp.float32
    )
    grad_query_bias = jnp.sum(d_query.astype(jnp.float32), axis=0)
    grad_key_weight = jnp.einsum("rd,re->de", flat_in, d_key, preferred_element_type=jnp.float32)
    grad_value_weight = jnp.einsum(
        "rd,re->de", flat_in, d_value, preferred_element_type=jnp.float32
    )
    grad_value_bias = jnp.sum(d_value.astype(jnp.float32), axis=0)
    d_input = d_resid_one + jnp.einsum(
        "re,de->rd", d_query, query_weight, preferred_element_type=jnp.float32
    )
    d_input = d_input + jnp.einsum(
        "re,de->rd", d_key, key_weight, preferred_element_type=jnp.float32
    )
    d_input = d_input + jnp.einsum(
        "re,de->rd", d_value, value_weight, preferred_element_type=jnp.float32
    )
    grad_tokens = d_input.astype(jnp.bfloat16).reshape(num_seq, tok_rows, width)
    (
        grad_query_weight,
        grad_query_bias,
        grad_key_weight,
        grad_value_weight,
        grad_value_bias,
        grad_out_weight,
        grad_out_bias,
        grad_first_gain,
        grad_first_shift,
        grad_up_weight,
        grad_up_bias,
        grad_down_weight,
        grad_down_bias,
        grad_second_gain,
        grad_second_shift,
    ) = lax.psum(
        (
            grad_query_weight,
            grad_query_bias,
            grad_key_weight,
            grad_value_weight,
            grad_value_bias,
            grad_out_weight,
            grad_out_bias,
            grad_first_gain,
            grad_first_shift,
            grad_up_weight,
            grad_up_bias,
            grad_down_weight,
            grad_down_bias,
            grad_second_gain,
            grad_second_shift,
        ),
        ("rows", "blk"),
    )
    layer_output = out_seq.astype(jnp.bfloat16)
    return (
        layer_output,
        pooled,
        grad_tokens,
        grad_query_weight,
        grad_query_bias,
        grad_key_weight,
        grad_value_weight,
        grad_value_bias,
        grad_out_weight,
        grad_out_bias,
        grad_first_gain,
        grad_first_shift,
        grad_up_weight,
        grad_up_bias,
        grad_down_weight,
        grad_down_bias,
        grad_second_gain,
        grad_second_shift,
    )


def solution(mesh):
    return jax.shard_map(
        local,
        mesh=mesh,
        in_specs=(
            P("rows", "blk", None),
            P("rows", "blk"),
            P(),
            P(),
            P(),
            P(),
            P(),
            P(),
            P(),
            P(),
            P(),
            P(),
            P(),
            P(),
            P(),
            P(),
            P(),
            P("rows", "blk", None),
        ),
        out_specs=(
            P("rows", "blk", None),
            P("rows", None, None),
            P("rows", "blk", None),
            P(),
            P(),
            P(),
            P(),
            P(),
            P(),
            P(),
            P(),
            P(),
            P(),
            P(),
            P(),
            P(),
            P(),
            P(),
        ),
        check_vma=False,
    )
```

profile of v0, /device:TPU:0, one launch (start us, length us, event | category | flops | bytes accessed | tf_op | source)
XLA Modules:
  0.0 849.4 jit_solution(11641422914640945987)
XLA Ops:
  7.3 3.3 add_convert_fusion.2
  22.3 13.2 %all-gather.1 = bf16[4,2,256]{2,1,0:T(2,128)(2,1)S(1)} all-gather(bf16[1,2,256]{2,1,0:T(2,128)(2,1)S(1)} %convert_bitcast_fusion), channel_id=2, replica_groups=mesh['rows'=8,'blk'=4] {'blk'}, dimensions={0}, use_global_device_ids=true | all-gather | bytes 5120 | tf_op jit(solution)/shard_map/all_gather | solution.py:110
  35.5 41.5 %all-gather.5.cloned.1.call-done = bf16[4,2,256,768]{3,2,1,0:T(8,128)(2,1)} async-done(((bf16[1,2,256,768]{3,2,1,0:T(8,128)(2,1)}), bf16[4,2,256,768]{3,2,1,0:T(8,128)(2,1)}) %all-gather.5.cloned.1.call-update) | async-done | bytes 3145744 | tf_op jit(solution)/shard_map/all_gather | solution.py:109
  77.0 4.7 copy.75
  81.7 59.6 %all-gather.7.cloned.1.call-done = bf16[4,2,256,768]{3,2,1,0:T(8,128)(2,1)} async-done(((bf16[1,2,256,768]{3,2,1,0:T(8,128)(2,1)}), bf16[4,2,256,768]{3,2,1,0:T(8,128)(2,1)}) %all-gather.7.cloned.1.call-update) | async-done | bytes 3145744 | tf_op jit(solution)/shard_map/all_gather | solution.py:108
  141.3 4.7 copy.76
  146.0 24.6 %while.26 = (s32[]{:T(128)}, f32[2,256,12,64]{1,3,2,0:T(8,128)}, f32[2,12,256]{2,1,0:T(8,128)}, bf16[4,2,256,768]{2,3,1,0:T(8,128)(2,1)}, bf16[2,256]{1,0:T(2,12...) while((s32[]{:T(128)}, f32[2,256,12,64]{1,3,2,0:T(8,128)}, ...), condition=%wide.region_2.3_spmd.clone, body=%wide.region_0.2_spmd.clone.sunk | while | flops 409868288 | bytes 34509036 | solution.py:104
  171.4 4.3 fusion.53
  177.3 20.4 %multiply_convert_fusion = (bf16[512,3072]{1,0:T(8,128)(2,1)S(1)}, f32[512,3072]{1,0:T(8,128)}, f32[512,3072]{1,0:T(8,128)}) fusion(f32[3072]{0:T(1024)S(1)} %copy-done.47, bf16[768,3072]{1,0:T(8,128)(2,1)} %param.33, f32[512,768]{1,0:T(8,128)S(1)} %get-tuple-element.371, f32[768]{0:T(1024)S(1)} %copy-done.51, f32[768]{0:T(1024)S(1)} %copy-done.43, ...), kind=kOutput, calls=%fused_computation.32 | convolution fusion | flops 2521694208 | bytes 22042624 | tf_op jit(solution)/shard_map/dot_general | solution.py:20
  204.6 9.9 %convert_reduce_fusion = (f32[3072]{0:T(1024)}, bf16[512,3072]{1,0:T(8,128)(2,1)}) fusion(f32[512,3072]{1,0:T(8,128)} %get-tuple-element.356, bf16[3072,768]{1,0:T(8,128)(2,1)S(1)} %bitcast.240, f32[512,768]{1,0:T(8,128)S(1)} %get-tuple-element.348, f32[512,3072]{1,0:T(8,128)} %get-tuple-element.372, f32[3072]{0:T(1024)S(1)} %copy-done.47), kind=kOutput, calls=%fused_computation.30 | convolution fusion | flops 2443047936 | bytes 22044672 | tf_op jit(solution)/shard_map/rd,fd->rf/dot_general | solution.py:151
  214.5 5.7 multiply_reduce_fusion
  230.2 35.2 %while.27 = (s32[]{:T(128)}, f32[2,256,12,64]{1,3,2,0:T(8,128)S(1)}, bf16[4,2,256,1536]{2,3,1,0:T(8,128)(2,1)}, bf16[4,2,256,768]{2,3,1,0:T(8,128)(2,1)}, bf16[2...) while((s32[]{:T(128)}, ...), condition=%wide.region_26.27_spmd.clone, body=%wide.region_25.26_spmd.clone.sunk | while | flops 1020133376 | bytes 45248656 | solution.py:212
  273.4 5.4 fusion.40
  278.9 5.5 fusion.47
  284.4 90.6 %reduce-scatter.2.cloned.1.call-done = bf16[1,2,256,1536]{2,3,1,0:T(8,128)(2,1)} async-done(((bf16[4,2,256,1536]{2,3,1,0:T(8,128)(2,1)}), bf16[1,2,256,1536]{2,3,1,0:T(8,128)(2,1)}) %reduce-scatter.2.cloned.1.call-update) | async-done | bytes 1572880 | tf_op jit(solution)/shard_map/reduce_scatter | solution.py:213
  376.3 3.6 convolution_bitcast_fusion.1
  384.1 19.3 %all-reduce.2 = (bf16[2,6]{1,0:T(2,128)(2,1)S(1)}, bf16[2,6,768]{2,1,0:T(8,128)(2,1)S(1)}) all-reduce(bf16[2,6]{1,0:T(2,128)(2,1)S(1)} %fusion.33, bf16[2,6,768]{2,1,0:T(8,128)(2,1)S(1)} %convolution_convert_fusion.1), channel_id=1, replica_groups=mesh['rows'=8,'blk'=4] {'blk'}, use_global_device_ids=true, to_apply=%region_9.10 | all-reduce | flops 9228 | bytes 36912 | tf_op jit(solution)/shard_map/psum | solution.py:139
  406.9 3.7 fusion.59
  414.6 41.4 %all-reduce = (f32[768]{0:T(1024)}, f32[768]{0:T(1024)}, f32[768]{0:T(1024)}, f32[768]{0:T(1024)}, f32[768]{0:T(1024)}, /*index=5*/f32[3072]{0:T(1024)}, f32[768]{0:T(1024)}, f32[768]{0:T(1024)}, f32[768]{0:T(1024)}) all-reduce(f32[768]{0:T(1024)S(1)} %reduce_sum.293, ...), channel_id=1, replica_groups=mesh['rows'=8,'blk'=4] {'rows','blk'}, use_global_device_ids=true, to_apply=%region_30.31 | all-reduce | flops 9216 | bytes 73728 | tf_op jit(solution)/shard_map/psum | solution.py:254
  460.1 359.8 %all-reduce.5.cloned.1.call-done = (f32[768,768]{0,1:T(8,128)}, f32[768,768]{0,1:T(8,128)}, f32[768,768]{0,1:T(8,128)}, f32[768,768]{1,0:T(8,128)}, f32[768,3072]{1,0:T(8,128)}, /*index=5*/f32[3072,768]{1,0:T(8,128)}) async-done(((f32[768,768]{0,1:T(8,128)}, f32[768,768]{0,1:T(8,128)}, f32[768,768]{0,1:T(8,128)}, f32[768,768]{1,0:T(8,128)}, f32[768,3072]{1,0:T(8,128)}, /*index=5*/f32[3072,768]{1,0:T(8,128)}), ...) | async-done | bytes 28311568 | tf_op jit(solution)/shard_map/psum | solution.py:254
  819.9 3.2 copy.91
  825.0 3.2 copy.93
  829.6 9.3 %copy.137 = f32[768,3072]{1,0:T(8,128)} copy(f32[768,3072]{1,0:T(8,128)} %get-tuple-element.580) | data formatting | bytes 18874368
  839.0 3.7 copy.138
  (298 shorter events, 117.9 us)
Async XLA Ops:
  7.2 168.7 %copy-start = (bf16[768,768]{1,0:T(8,128)(2,1)S(1)}, bf16[768,768]{1,0:T(8,128)(2,1)}, u32[]{:S(2)}) copy-start(bf16[768,768]{1,0:T(8,128)(2,1)} %param.29) | copy-start | bytes 3538948
  7.2 69.8 %all-gather.5.cloned.1.call-start = ((), (), s32[]{:S(2)}) async-start(), calls=%async_computation.1 | async-start | bytes 3932160 | tf_op jit(solution)/shard_map/all_gather | solution.py:109
  10.6 4.7 copy-start.48
  10.6 130.7 %all-gather.7.cloned.1.call-start = ((), (), s32[]{:S(2)}) async-start(), calls=%async_computation.2 | async-start | bytes 3932160 | tf_op jit(solution)/shard_map/all_gather | solution.py:108
  13.7 361.3 %reduce-scatter.2.cloned.1.call-start = ((), (), s32[]{:S(2)}) async-start(), calls=%async_computation.3 | async-start | bytes 7864320 | tf_op jit(solution)/shard_map/reduce_scatter | solution.py:213
  175.9 21.8 %slice-start.3 = ((s8[4718592]{0:T(1024)(128)(4,1)}), s8[4194304]{0:T(1024)(128)(4,1)S(1)}, s32[]{:S(2)}) async-start(s8[4718592]{0:T(1024)(128)(4,1)} %bitcast.239), calls=%async_computation.8 | async-start | bytes 8388608
  176.9 43.4 %copy-start.16 = (f32[512,768]{1,0:T(8,128)}, f32[512,768]{1,0:T(8,128)S(1)}, u32[]{:S(2)}) copy-start(f32[512,768]{1,0:T(8,128)S(1)} %get-tuple-element.371) | copy-start | bytes 4718596
  177.2 43.0 %copy-start.39 = (f32[512]{0:T(512)}, f32[512]{0:T(512)S(1)}, u32[]{:S(2)}) copy-start(f32[512]{0:T(512)S(1)} %add_rsqrt_fusion.1) | copy-start | bytes 6148
  177.2 20.5 %slice-start.4 = ((s8[4718592]{0:T(1024)(128)(4,1)}), s8[524288]{0:T(1024)(128)(4,1)S(1)}, s32[]{:S(2)}) async-start(s8[4718592]{0:T(1024)(128)(4,1)} %bitcast.239), calls=%async_computation.9 | async-start | bytes 1048576
  177.3 20.5 %copy-start.50 = (f32[768]{0:T(1024)S(1)}, f32[768]{0:T(1024)}, u32[]{:S(2)}) copy-start(f32[768]{0:T(1024)} %param.36) | copy-start | bytes 9220
  202.1 12.4 %slice-start.5 = ((s8[4718592]{0:T(1024)(128)(4,1)}), s8[4194304]{0:T(1024)(128)(4,1)S(1)}, s32[]{:S(2)}) async-start(s8[4718592]{0:T(1024)(128)(4,1)} %bitcast.241), calls=%async_computation.10 | async-start | bytes 8388608
  204.6 9.9 %copy-start.14 = (f32[512,768]{1,0:T(8,128)}, f32[512,768]{1,0:T(8,128)S(1)}, u32[]{:S(2)}) copy-start(f32[512,768]{1,0:T(8,128)S(1)} %get-tuple-element.348) | copy-start | bytes 4718596
  204.6 9.9 %slice-start.6 = ((s8[4718592]{0:T(1024)(128)(4,1)}), s8[524288]{0:T(1024)(128)(4,1)S(1)}, s32[]{:S(2)}) async-start(s8[4718592]{0:T(1024)(128)(4,1)} %bitcast.241), calls=%async_computation.11 | async-start | bytes 1048576
  265.4 554.5 %all-reduce.5.cloned.1.call-start = ((), (), s32[]{:S(2)}) async-start(), calls=%async_computation.4 | async-start | bytes 56623104 | tf_op jit(solution)/shard_map/psum | solution.py:254
  273.4 5.4 copy-start.17
  273.4 5.4 copy-start.40
  273.4 5.4 copy-start.44
  273.4 5.4 copy-start.52
  273.4 5.4 copy-start.53
  376.3 5.8 copy-start.9
  406.9 5.9 copy-start.10
  828.2 10.7 %slice-start = ((s8[9437184]{0:T(1024)(128)(4,1)}), s8[4194304]{0:T(1024)(128)(4,1)S(1)}, s32[]{:S(2)}) async-start(s8[9437184]{0:T(1024)(128)(4,1)} %bitcast.215), calls=%async_computation.5 | async-start | bytes 8388608
  829.6 9.3 %slice-start.1 = ((s8[9437184]{0:T(1024)(128)(4,1)}), s8[4194304]{0:T(1024)(128)(4,1)S(1)}, s32[]{:S(2)}) async-start(s8[9437184]{0:T(1024)(128)(4,1)} %bitcast.215), calls=%async_computation.6 | async-start | bytes 8388608
  829.6 9.3 %slice-start.2 = ((s8[9437184]{0:T(1024)(128)(4,1)}), s8[1048576]{0:T(1024)(128)(4,1)S(1)}, s32[]{:S(2)}) async-start(s8[9437184]{0:T(1024)(128)(4,1)} %bitcast.215), calls=%async_computation.7 | async-start | bytes 2097152
  (53 other events, 121.5 us)
Sparse Core Ops, SparseCore 0:
  10.7 66.2 all-gather.4
  79.1 62.1 all-gather.6
  265.5 109.3 reduce-scatter.1
  382.4 437.4 all-reduce.4
where the time goes:
time: 853 us; the launch traced here: 849 us
  waiting for transfers between devices  552 us (65%)
  matrix products  114 us (13%)
  blocking collectives  73.8 us (9%)
  local copies, waits for them, and re-layouts  70.2 us (8%)
  other arithmetic  23.7 us (3%)
  between operations  14.8 us (2%)
    psum x1, waiting for transfers between devices, local(): lax.psum((grad_query_weight, grad_query_bias, grad_key_weight, grad_value...  360 us
    reduce_scatter x1, waiting for transfers between devices, local(): lax.psum_scatter(pair_terms.astype(jnp.bfloat16), 'blk', scatter_dimensio...  90.6 us
    all_gather x1, waiting for transfers between devices, local(): lax.all_gather(key_send, 'blk', axis=0, tiled=True)  59.6 us
    all_gather x1, waiting for transfers between devices, local(): lax.all_gather(value_send, 'blk', axis=0, tiled=True)  41.5 us
    psum x1, blocking collectives, local(): lax.psum((grad_query_weight, grad_query_bias, grad_key_weight, grad_value...  41.4 us
    unnamed x129, local copies, waits for them, and re-layouts  40.2 us
    dot_general x6, matrix products, matmul(): return jnp.dot(left, right, preferred_element_type=jnp.float32)  33.6 us
    psum x1, blocking collectives, local(): lax.psum(seg_counts.astype(jnp.bfloat16), 'blk').astype(jnp.float32)  19.3 us
  transfers between devices with their start and end apart: 4, of which 4 were waited for; matrix products, arithmetic and copies ran while one was open for 6% of the time, Pallas kernels for 0%

commit v1 on v0

v1 whole, which is shorter than its diff:
```python
from functools import partial

import jax
import jax.numpy as jnp
from jax import lax
from jax.sharding import PartitionSpec as P

D = 768
H = 12
HD = 64
NSEG = 6

query_scale = 0.125
norm_eps = 1e-12
pool_eps = 1e-06
bf16 = jnp.bfloat16
f32 = jnp.float32


def matmul(left, right):
    return jnp.dot(left, right, preferred_element_type=f32)


def layer_norm(rows_in, gain_vec, shift_vec):
    row_mean = jnp.mean(rows_in, axis=-1, keepdims=True)
    centred = rows_in - row_mean
    inverse = lax.rsqrt(jnp.mean(centred * centred, axis=-1, keepdims=True) + norm_eps)
    normed = centred * inverse
    return (normed * gain_vec + shift_vec, normed, inverse)


def norm_backward(upstream, normed, inverse, gain_vec):
    scaled = upstream * gain_vec
    first_mean = jnp.mean(scaled, axis=-1, keepdims=True)
    second_mean = jnp.mean(scaled * normed, axis=-1, keepdims=True)
    return inverse * (scaled - first_mean - normed * second_mean)


def matryoshka(averages):
    pieces = []
    for prefix in (D, D * 2 // 3, D // 3, D // 6, D // 12):
        leading = averages[..., :prefix]
        centred = leading - jnp.mean(leading, axis=-1, keepdims=True)
        pieces.append(
            centred * lax.rsqrt(jnp.mean(centred * centred, axis=-1, keepdims=True) + pool_eps)
        )
    return jnp.concatenate(pieces, axis=-1)


def swap(value, axis, size, distance):
    return lax.ppermute(value, axis, [(i, i ^ distance) for i in range(size)])


def part_of(value, index, count):
    rows = value.shape[0] // count
    return lax.dynamic_slice_in_dim(value, index * rows, rows, 0)


def ordered(bit, mine, theirs):
    return jnp.where(
        bit == 0,
        jnp.concatenate([mine, theirs], 0),
        jnp.concatenate([theirs, mine], 0),
    )


class Links:
    def __init__(self, n_rows, n_blk):
        self.size = {"rows": n_rows, "blk": n_blk}
        self.at = {"rows": lax.axis_index("rows"), "blk": lax.axis_index("blk")}
        row_bits = [("rows", 1 << k) for k in range(n_rows.bit_length() - 1)]
        self.near, self.far = row_bits[:1], row_bits[1:]
        self.blk_bits = [("blk", 1 << k) for k in range(n_blk.bit_length() - 1)]

    def bit(self, stage):
        axis, distance = stage
        return (self.at[axis] // distance) % 2

    def swap(self, value, stage):
        axis, distance = stage
        return swap(value, axis, self.size[axis], distance)

    def halve(self, value, stage):
        bit = self.bit(stage)
        received = self.swap(part_of(value, 1 - bit, 2), stage)
        return (part_of(value, bit, 2).astype(f32) + received.astype(f32)).astype(bf16)

    def double(self, value, stage):
        return ordered(self.bit(stage), value, self.swap(value, stage))

    def all_reduce(self, value):
        for stage in self.near:
            value = self.halve(value, stage)
        half = value.shape[0] // 2
        left, right = value[:half], value[half:]
        for stage, other in zip(self.far, self.far[::-1]):
            left, right = self.halve(left, stage), self.halve(right, other)
        half = left.shape[0]
        value = jnp.concatenate([left, right], 0)
        for stage in self.blk_bits:
            value = self.halve(value, stage)
        for stage in self.blk_bits[::-1]:
            value = self.double(value, stage)
        left, right = value[:half], value[half:]
        for stage, other in zip(self.far[::-1], self.far):
            left, right = self.double(left, stage), self.double(right, other)
        value = jnp.concatenate([left, right], 0)
        for stage in self.near:
            value = self.double(value, stage)
        return value.astype(f32)

    def sum_small(self, value):
        for stage in self.blk_bits + self.near + self.far:
            value = value + self.swap(value, stage)
        return value


def local(
    n_rows,
    n_blk,
    tokens,
    segments,
    query_weight,
    query_bias,
    key_weight,
    value_weight,
    value_bias,
    out_weight,
    out_bias,
    first_gain,
    first_shift,
    up_weight,
    up_bias,
    down_weight,
    down_bias,
    second_gain,
    second_shift,
    cotangent,
):
    links = Links(n_rows, n_blk)
    pair, cross = ("blk", 1), ("blk", 2)
    blk_at = links.at["blk"]
    seq_at = blk_at // 2
    num_seq, tok_rows, width = tokens.shape
    ff = up_weight.shape[1]
    total_rows = 2 * tok_rows

    own = lax.dynamic_index_in_dim(tokens, seq_at, 0, keepdims=False)
    far_block = links.swap(lax.dynamic_index_in_dim(tokens, 1 - seq_at, 0, keepdims=False), cross)
    near_block = links.swap(own, pair)
    last_block = links.swap(far_block, pair)
    seg_pair = jnp.stack([segments, links.swap(segments, pair)])
    seg_cross = links.swap(seg_pair, cross)
    seg_mine = lax.dynamic_index_in_dim(seg_pair, seq_at, 1, keepdims=False)
    seg_far = lax.dynamic_index_in_dim(seg_cross, seq_at, 1, keepdims=False)
    seg_keys = jnp.concatenate([seg_mine[0], seg_far[0], seg_mine[1], seg_far[1]], 0)
    seg_query = seg_keys[:total_rows]
    cot_own = lax.dynamic_index_in_dim(cotangent, seq_at, 0, keepdims=False)
    cot_far = links.swap(lax.dynamic_index_in_dim(cotangent, 1 - seq_at, 0, keepdims=False), cross)
    upstream = jnp.concatenate([cot_own, cot_far], 0).astype(f32)

    flat_all = jnp.concatenate([own, far_block, near_block, last_block], 0)
    flat_in = flat_all[:total_rows]
    queries = (query_scale * (matmul(flat_in, query_weight) + query_bias)).astype(bf16)
    keys = matmul(flat_all, key_weight).astype(bf16)
    values = (matmul(flat_all, value_weight) + value_bias).astype(bf16)
    q_heads = queries.reshape(total_rows, H, HD)
    k_heads = keys.reshape(-1, H, HD)
    v_heads = values.reshape(-1, H, HD)
    allowed = seg_query[:, None] == seg_keys[None, :]

    def weights_of():
        scores = jnp.einsum("qhd,khd->hqk", q_heads, k_heads, preferred_element_type=f32)
        return jnp.where(allowed[None], jnp.exp(scores), 0.0)

    expo = weights_of()
    totals = jnp.transpose(jnp.sum(expo, axis=2))[..., None]
    numer = jnp.einsum("hqk,khd->qhd", expo.astype(bf16), v_heads, preferred_element_type=f32)
    attended = numer / totals
    attended_low = attended.reshape(total_rows, width).astype(bf16)
    branch = matmul(attended_low, out_weight) + out_bias
    hidden, normed_one, inverse_one = layer_norm(
        flat_in.astype(f32) + branch, first_gain, first_shift
    )
    hidden_low = hidden.astype(bf16)
    preact = matmul(hidden_low, up_weight) + up_bias
    activation_full, gelu_pull = jax.vjp(partial(jax.nn.gelu, approximate=False), preact)
    activation = activation_full.astype(bf16)
    feed_out = matmul(activation, down_weight) + down_bias
    outputs, normed_two, inverse_two = layer_norm(hidden + feed_out, second_gain, second_shift)

    labels = jnp.arange(1, NSEG + 1, dtype=jnp.int32)
    onehot = (seg_query[None, :] == labels[:, None]).astype(f32)
    seg_sums = jnp.dot(onehot, outputs, precision=lax.Precision.HIGHEST)
    counts = jnp.sum((seg_keys[None, :] == labels[:, None]).astype(f32), axis=1)
    seg_sums = seg_sums + links.swap(seg_sums, pair)
    pooled_one = seg_sums / counts[:, None]
    pooled_two = links.swap(pooled_one, cross)
    pooled = matryoshka(ordered(seq_at, pooled_one[None], pooled_two[None]))

    out_low = outputs.astype(bf16)
    out_back = links.swap(out_low[tok_rows:], cross)
    layer_output = ordered(seq_at, out_low[:tok_rows][None], out_back[None])

    grad_second_gain = jnp.sum(upstream * normed_two, axis=0)
    grad_second_shift = jnp.sum(upstream, axis=0)
    d_resid_two = norm_backward(upstream, normed_two, inverse_two, second_gain)
    d_feed = d_resid_two.astype(bf16)
    grad_down_weight = jnp.einsum("rf,rd->fd", activation, d_feed, preferred_element_type=f32)
    grad_down_bias = jnp.sum(d_feed.astype(f32), axis=0)
    d_activation = jnp.einsum("rd,fd->rf", d_feed, down_weight, preferred_element_type=f32)
    d_preact = gelu_pull(d_activation)[0].astype(bf16)
    up_parts = [
        jnp.einsum(
            "rd,rf->df", hidden_low, d_preact[:, k * width : (k + 1) * width],
            preferred_element_type=f32,
        ).astype(bf16)
        for k in range(ff // width)
    ]
    grad_up_bias = jnp.sum(d_preact.astype(f32), axis=0)
    d_hidden = d_resid_two + jnp.einsum(
        "rf,df->rd", d_preact, up_weight, preferred_element_type=f32
    )
    grad_first_gain = jnp.sum(d_hidden * normed_one, axis=0)
    grad_first_shift = jnp.sum(d_hidden, axis=0)
    d_resid_one = norm_backward(d_hidden, normed_one, inverse_one, first_gain)
    d_branch = d_resid_one.astype(bf16)
    grad_out_weight = jnp.einsum("rd,re->de", attended_low, d_branch, preferred_element_type=f32)
    grad_out_bias = jnp.sum(d_branch.astype(f32), axis=0)
    d_attended = jnp.einsum(
        "re,de->rd", d_branch, out_weight, preferred_element_type=f32
    ).reshape(total_rows, H, HD)
    d_total = -jnp.sum(d_attended * attended, axis=2, keepdims=True) / totals
    d_numer = (d_attended / totals).astype(bf16)

    expo = weights_of()
    d_prob = jnp.einsum("qhd,khd->hqk", d_numer, v_heads, preferred_element_type=f32)
    d_scores = (expo * (d_prob + jnp.transpose(d_total, (1, 0, 2)))).astype(bf16)
    d_query = jnp.einsum("hqk,khd->qhd", d_scores, k_heads, preferred_element_type=f32)
    d_query = d_query.reshape(total_rows, width).astype(bf16) * query_scale
    d_key = jnp.einsum("hqk,qhd->khd", d_scores, q_heads, preferred_element_type=f32)
    d_key = d_key.reshape(-1, width).astype(bf16)
    d_value = jnp.einsum("hqk,qhd->khd", expo.astype(bf16), d_numer, preferred_element_type=f32)
    d_value = d_value.reshape(-1, width).astype(bf16)

    def outer(left, right):
        return jnp.einsum("rd,re->de", left, right, preferred_element_type=f32).astype(bf16)

    attn_parts = [
        outer(flat_in, d_query),
        outer(flat_all, d_key),
        outer(flat_all, d_value),
        grad_out_weight.astype(bf16),
    ]
    grad_query_bias = jnp.sum(d_query.astype(f32), axis=0)
    grad_value_bias = jnp.sum(d_value.astype(f32), axis=0)

    def back(left, weight):
        return jnp.einsum("re,de->rd", left, weight, preferred_element_type=f32)

    d_mine = (
        d_resid_one
        + back(d_query, query_weight)
        + back(d_key[:total_rows], key_weight)
        + back(d_value[:total_rows], value_weight)
    )
    d_pair = back(d_key[total_rows:], key_weight) + back(d_value[total_rows:], value_weight)
    d_mine = (d_mine + links.swap(d_pair.astype(bf16), pair).astype(f32)).astype(bf16)
    d_back = links.swap(d_mine[tok_rows:], cross)
    grad_tokens = ordered(seq_at, d_mine[:tok_rows][None], d_back[None])

    vectors = [
        grad_query_bias, grad_value_bias, grad_out_bias, grad_first_gain, grad_first_shift,
        grad_down_bias, grad_second_gain, grad_second_shift,
    ]
    small = jnp.concatenate([v[None] for v in vectors] + [grad_up_bias.reshape(-1, width)], 0)
    small = links.sum_small(small)
    down_sum = links.all_reduce(grad_down_weight.astype(bf16))
    up_sum = links.all_reduce(jnp.concatenate(up_parts, 0))
    attn_sum = links.all_reduce(jnp.concatenate(attn_parts, 0))
    up_sum = jnp.concatenate(jnp.split(up_sum, ff // width, 0), 1)
    query_sum, key_sum, value_sum, out_sum = jnp.split(attn_sum, 4, 0)
    return (
        layer_output,
        pooled,
        grad_tokens,
        query_sum,
        small[0],
        key_sum,
        value_sum,
        small[1],
        out_sum,
        small[2],
        small[3],
        small[4],
        up_sum,
        small[8:].reshape(-1),
        down_sum,
        small[5],
        small[6],
        small[7],
    )


def solution(mesh):
    row_split = P("rows", "blk", None)
    return jax.shard_map(
        partial(local, mesh.shape["rows"], mesh.shape["blk"]),
        mesh=mesh,
        in_specs=(row_split, P("rows", "blk")) + (P(),) * 15 + (row_split,),
        out_specs=(row_split, P("rows", None, None), row_split) + (P(),) * 15,
        check_vma=False,
    )
```

time: 853 us -> 465 us (0.55)
  waiting for transfers between devices: 552 us -> 157 us
  blocking collectives: 73.8 us -> 0 us
  starting transfers between devices: 0.16 us -> 66.6 us
  local copies, waits for them, and re-layouts: 70.2 us -> 30.8 us
  matrix products: 114 us -> 148 us
  other arithmetic: 23.7 us -> 56.5 us
  between operations: 14.8 us -> 2.41 us
    psum x1 -> x0, waiting for transfers between devices: 360 us -> none  [local(): lax.psum((grad_query_weight, grad_query_bias, grad_key_weight, grad_value...]
    ppermute x0 -> x58, waiting for transfers between devices: none -> 157 us  [swap(): return lax.ppermute(value, axis, [(i, i ^ distance) for i in range(size)])]
    all_gather x2 -> x0, waiting for transfers between devices: 101 us -> none  [the longest x1 59.6 us: local(): lax.all_gather(key_send, 'blk', axis=0, tiled=True)]
    reduce_scatter x1 -> x0, waiting for transfers between devices: 90.6 us -> none  [local(): lax.psum_scatter(pair_terms.astype(jnp.bfloat16), 'blk', scatter_dimensio...]
    ppermute x0 -> x58, starting transfers between devices: none -> 66.6 us  [swap(): return lax.ppermute(value, axis, [(i, i ^ distance) for i in range(size)])]
    psum x2 -> x0, blocking collectives: 60.6 us -> none  [the longest x1 41.4 us: local(): lax.psum((grad_query_weight, grad_query_bias, grad_key_weight, grad_value...]
    unnamed x129 -> x95, local copies, waits for them, and re-layouts: 40.2 us -> 5.54 us
    dot_general x47 -> x30, matrix products: 114 us -> 148 us  [the longest x6 32.4 us: matmul(): return jnp.dot(left, right, preferred_element_type=f32)]
  transfers between devices with their start and end apart: 4 -> 58, of which waited for: 4 -> 29; matrix products, arithmetic and copies ran while one was open for 6% -> 30% of each run, Pallas kernels for 0% -> 0%
where the time goes in v1:
time: 465 us; the launch traced here: 461 us
  waiting for transfers between devices  157 us (34%)
  matrix products  148 us (32%)
  starting transfers between devices  66.6 us (14%)
  other arithmetic  56.5 us (12%)
  local copies, waits for them, and re-layouts  30.8 us (7%)
    ppermute x58, waiting for transfers between devices, swap(): return lax.ppermute(value, axis, [(i, i ^ distance) for i in range(size)])  157 us
    ppermute x58, starting transfers between devices, swap(): return lax.ppermute(value, axis, [(i, i ^ distance) for i in range(size)])  66.6 us
    dot_general x6, matrix products, matmul(): return jnp.dot(left, right, preferred_element_type=f32)  32.4 us
    dot_general x1, matrix products, local(): jnp.einsum('qhd,khd->hqk', d_numer, v_heads, preferred_element_type=f32)  16 us
    select_n x20, other arithmetic, ordered(): jnp.where(bit == 0, jnp.concatenate([mine, theirs], 0), jnp.concatenate([...  14.1 us
    convert_element_type x3, other arithmetic, all_reduce(): return value.astype(f32)  14 us
    dot_general x1, matrix products, local(): jnp.einsum('hqk,khd->qhd', expo.astype(bf16), v_heads, preferred_element_...  12.4 us
    dot_general x1, matrix products, local(): jnp.einsum('hqk,qhd->khd', expo.astype(bf16), d_numer, preferred_element_...  12.4 us
  transfers between devices with their start and end apart: 58, of which 29 were waited for; matrix products, arithmetic and copies ran while one was open for 30% of the time, Pallas kernels for 0%

profile of v1, /device:TPU:0, one launch (start us, length us, event | category | flops | bytes accessed | tf_op | source)
XLA Modules:
  0.0 460.9 jit_solution(16058197965833795822)
XLA Ops:
  13.8 28.8 %collective-permute-done.4 = s32[2,2,256]{2,1,0:T(2,128)S(1)} collective-permute-done((s32[2,2,256]{2,1,0:T(2,128)S(1)}, s32[2,2,256]{2,1,0:T(2,128)S(1)}, u32[]{:S(2)}, u32[]{:S(2)}) %collective-permute-start.4) | collective-permute-done | bytes 4128 | tf_op jit(solution)/shard_map/ppermute | solution.py:51
  46.4 7.7 %collective-permute-done.2 = bf16[256,768]{1,0:T(8,128)(2,1)} collective-permute-done((bf16[256,768]{1,0:T(8,128)(2,1)}, bf16[256,768]{1,0:T(8,128)(2,1)}, u32[]{:S(2)}, u32[]{:S(2)}) %collective-permute-start.2) | collective-permute-done | bytes 393248 | tf_op jit(solution)/shard_map/ppermute | solution.py:51
  56.9 11.5 %fusion = (f32[12,512]{1,0:T(8,128)S(1)}, f32[12,512,1024]{2,1,0:T(8,128)}) fusion(pred[512,1024]{1,0:T(8,128)(4,1)S(1)} %broadcast_compare_fusion, bf16[512,12,64]{0,2,1:T(8,128)(2,1)S(1)} %bitcast.93, bf16[1024,12,64]{0,2,1:T(8,128)(2,1)S(1)} %bitcast.101), kind=kOutput, calls=%fused_computation.2 | convolution fusion | flops 817883136 | bytes 28073984 | tf_op jit(solution)/shard_map/qhd,khd->hqk/dot_general | solution.py:173
  71.3 12.4 %fusion.75 = (bf16[512,12,64]{0,2,1:T(8,128)(2,1)}, f32[512,12,64]{0,2,1:T(8,128)}) fusion(f32[512,12]{0,1:T(8,128)S(1)} %bitcast.108, bf16[1024,12,64]{0,2,1:T(8,128)(2,1)S(1)} %bitcast.97, f32[12,512,1024]{2,1,0:T(8,128)} %get-tuple-element.134, pred[512,1024]{1,0:T(8,128)(4,1)S(1)} %broadcast_compare_fusion), kind=kOutput, calls=%fused_computation.264 | convolution fusion | flops 818675712 | bytes 29646848 | tf_op jit(solution)/shard_map/hqk,khd->qhd/dot_general | solution.py:178
  87.2 19.1 %multiply_convert_fusion.1 = (bf16[512,3072]{1,0:T(8,128)(2,1)S(1)}, f32[512,3072]{1,0:T(8,128)}, f32[512,3072]{1,0:T(8,128)}) fusion(f32[3072]{0:T(1024)S(1)} %copy-done.36, bf16[512,768]{1,0:T(8,128)(2,1)S(1)} %fusion.27, bf16[768,3072]{1,0:T(8,128)(2,1)} %param.29), kind=kOutput, calls=%fused_computation.9 | convolution fusion | flops 2519728128 | bytes 21245952 | tf_op jit(solution)/shard_map/dot_general | solution.py:21
  115.9 8.6 %convert_reduce_fusion = (f32[3072]{0:T(1024)}, bf16[512,3072]{1,0:T(8,128)(2,1)S(1)}) fusion(f32[512,3072]{1,0:T(8,128)} %get-tuple-element.95, bf16[3072,768]{1,0:T(8,128)(2,1)S(1)} %bitcast.130, f32[512,768]{1,0:T(8,128)S(1)} %get-tuple-element.89, f32[512,3072]{1,0:T(8,128)} %get-tuple-element.139, f32[3072]{0:T(1024)S(1)} %copy-done.36), kind=kOutput, calls=%fused_computation.7 | convolution fusion | flops 2443047936 | bytes 22044672 | tf_op jit(solution)/shard_map/rd,fd->rf/dot_general | solution.py:211
  132.0 6.3 %multiply_reduce_fusion = (f32[768]{0:T(1024)}, f32[512]{0:T(512)S(1)}, f32[512]{0:T(512)S(1)}, f32[768]{0:T(1024)}, f32[512,768]{1,0:T(8,128)S(1)}) fusion(f32[512,768]{1,0:T(8,128)S(1)} %get-tuple-element.138, f32[512]{0:T(512)S(1)} %add_rsqrt_fusion.1, f32[512]{0:T(512)S(1)} %broadcast_multiply_fusion.5, f32[768]{0:T(1024)S(1)} %copy-done.31, ...), kind=kOutput, calls=%fused_computation.58 | convolution fusion | flops 2419848704 | bytes 12600320 | tf_op jit(solution)/shard_map/rf,df->rd/dot_general | solution.py:221
  146.3 12.4 %convert_reduce_fusion.1 = (f32[12,64]{1,0:T(8,128)}, bf16[12,64,1024]{2,1,0:T(8,128)(2,1)}) fusion(f32[12,512,1024]{2,1,0:T(8,128)} %get-tuple-element.134, pred[512,1024]{1,0:T(8,128)(4,1)S(1)} %broadcast_compare_fusion, f32[512,12,64]{0,2,1:T(8,128)S(1)} %bitcast.90, f32[512,12]{0,1:T(8,128)S(1)} %bitcast.109), kind=kOutput, calls=%fused_computation.35 | convolution fusion | flops 821034240 | bytes 28863488 | tf_op jit(solution)/shard_map/hqk,qhd->khd/dot_general | solution.py:243
  159.2 16.0 %multiply_convert_fusion = bf16[12,512,1024]{2,1,0:T(8,128)(2,1)} fusion(f32[12,512,1024]{2,1,0:T(8,128)} %get-tuple-element.134, f32[12,512]{1,0:T(8,128)S(1)} %divide_bitcast_fusion, pred[512,1024]{1,0:T(8,128)(4,1)S(1)} %broadcast_compare_fusion, bf16[1024,12,64]{0,2,1:T(8,128)(2,1)} %bitcast.98, f32[512,12,64]{0,2,1:T(8,128)S(1)} %bitcast.92, ...), kind=kOutput, calls=%fused_computation | convolution fusion | flops 831258624 | bytes 41467904 | tf_op jit(solution)/shard_map/qhd,khd->hqk/dot_general | solution.py:237
  175.1 10.5 %convert_reduce_fusion.5 = (f32[12,64]{1,0:T(8,128)}, bf16[12,64,512]{2,1,0:T(8,128)(2,1)}) fusion(bf16[1024,12,64]{0,2,1:T(8,128)(2,1)} %bitcast.102, bf16[12,512,1024]{2,1,0:T(8,128)(2,1)} %multiply_convert_fusion), kind=kOutput, calls=%fused_computation.60 | convolution fusion | flops 806878464 | bytes 14945280 | tf_op jit(solution)/shard_map/hqk,khd->qhd/dot_general | solution.py:239
  185.7 6.9 %convolution_convert_fusion.1 = bf16[12,64,1024]{2,1,0:T(8,128)(2,1)S(1)} fusion(bf16[512,12,64]{0,2,1:T(8,128)(2,1)S(1)} %bitcast.94, bf16[12,512,1024]{2,1,0:T(8,128)(2,1)} %multiply_convert_fusion), kind=kOutput, calls=%fused_computation.48 | convolution fusion | flops 806092800 | bytes 14942208 | tf_op jit(solution)/shard_map/hqk,qhd->khd/dot_general | solution.py:241
  249.1 10.2 %collective-permute-done.45 = bf16[384,768]{1,0:T(8,128)(2,1)S(1)} collective-permute-done((bf16[384,768]{1,0:T(8,128)(2,1)S(1)}, bf16[384,768]{1,0:T(8,128)(2,1)S(1)}, u32[]{:S(2)}, u32[]{:S(2)}) %collective-permute-start.45) | collective-permute-done | bytes 589856 | tf_op jit(solution)/shard_map/ppermute | solution.py:51
  261.0 10.9 %collective-permute-done.31 = bf16[384,768]{1,0:T(8,128)(2,1)S(1)} collective-permute-done((bf16[384,768]{1,0:T(8,128)(2,1)S(1)}, bf16[384,768]{1,0:T(8,128)(2,1)S(1)}, u32[]{:S(2)}, u32[]{:S(2)}) %collective-permute-start.31) | collective-permute-done | bytes 589856 | tf_op jit(solution)/shard_map/ppermute | solution.py:51
  276.3 8.3 %collective-permute-done.12 = bf16[384,768]{1,0:T(8,128)(2,1)S(1)} collective-permute-done((bf16[384,768]{1,0:T(8,128)(2,1)S(1)}, bf16[384,768]{1,0:T(8,128)(2,1)S(1)}, u32[]{:S(2)}, u32[]{:S(2)}) %collective-permute-start.12) | collective-permute-done | bytes 589856 | tf_op jit(solution)/shard_map/ppermute | solution.py:51
  290.0 4.6 collective-permute-done.46
  303.8 7.4 %collective-permute-done.49 = bf16[192,768]{1,0:T(8,128)(2,1)S(1)} collective-permute-done((bf16[192,768]{1,0:T(8,128)(2,1)S(1)}, bf16[192,768]{1,0:T(8,128)(2,1)S(1)}, u32[]{:S(2)}, u32[]{:S(2)}) %collective-permute-start.49) | collective-permute-done | bytes 294944 | tf_op jit(solution)/shard_map/ppermute | solution.py:51
  325.9 11.2 %collective-permute-done.17 = bf16[96,768]{1,0:T(8,128)(2,1)S(1)} collective-permute-done((bf16[96,768]{1,0:T(8,128)(2,1)S(1)}, bf16[96,768]{1,0:T(8,128)(2,1)S(1)}, u32[]{:S(2)}, u32[]{:S(2)}) %collective-permute-start.17) | collective-permute-done | bytes 147488 | tf_op jit(solution)/shard_map/ppermute | solution.py:51
  340.3 4.6 collective-permute-done.18
  348.3 6.5 %collective-permute-done.19 = bf16[192,768]{1,0:T(8,128)(2,1)S(1)} collective-permute-done((bf16[192,768]{1,0:T(8,128)(2,1)S(1)}, bf16[192,768]{1,0:T(8,128)(2,1)S(1)}, u32[]{:S(2)}, u32[]{:S(2)}) %collective-permute-start.19) | collective-permute-done | bytes 294944 | tf_op jit(solution)/shard_map/ppermute | solution.py:51
  373.6 9.4 %collective-permute-done.23 = bf16[384,768]{1,0:T(8,128)(2,1)S(1)} collective-permute-done((bf16[384,768]{1,0:T(8,128)(2,1)S(1)}, bf16[384,768]{1,0:T(8,128)(2,1)S(1)}, u32[]{:S(2)}, u32[]{:S(2)}) %collective-permute-start.23) | collective-permute-done | bytes 589856 | tf_op jit(solution)/shard_map/ppermute | solution.py:51
  386.1 7.9 %collective-permute-done.39 = bf16[192,768]{1,0:T(8,128)(2,1)S(1)} collective-permute-done((bf16[192,768]{1,0:T(8,128)(2,1)S(1)}, bf16[192,768]{1,0:T(8,128)(2,1)S(1)}, u32[]{:S(2)}, u32[]{:S(2)}) %collective-permute-start.39) | collective-permute-done | bytes 294944 | tf_op jit(solution)/shard_map/ppermute | solution.py:51
  411.9 6.5 %collective-permute-done.5 = bf16[256,768]{1,0:T(8,128)(2,1)S(1)} collective-permute-done((bf16[256,768]{1,0:T(8,128)(2,1)S(1)}, bf16[256,768]{1,0:T(8,128)(2,1)S(1)}, u32[]{:S(2)}, u32[]{:S(2)}) %collective-permute-start.5) | collective-permute-done | bytes 393248 | tf_op jit(solution)/shard_map/ppermute | solution.py:51
  447.7 6.3 %pad_maximum_fusion = f32[768,3072]{1,0:T(8,128)} fusion(f32[768,768]{1,0:T(8,128)S(1)} %get-tuple-element.97, f32[768,768]{1,0:T(8,128)} %get-tuple-element.98, f32[768,768]{1,0:T(8,128)} %get-tuple-element.99, f32[768,768]{1,0:T(8,128)S(1)} %get-tuple-element.96), kind=kLoop, calls=%fused_computation.5 | loop fusion | flops 7077888 | bytes 18874368 | tf_op jit(solution)/shard_map/concatenate | solution.py:281
  454.0 6.4 %fusion.10 = f32[3072,768]{1,0:T(8,128)} fusion(bf16[1536,768]{1,0:T(8,128)(2,1)} %collective-permute-done.57, bf16[768,768]{1,0:T(8,128)(2,1)S(1)} %maximum_select_fusion.8, bf16[768,768]{1,0:T(8,128)(2,1)S(1)} %maximum_select_fusion.7, pred[]{:T(512)S(6)} %eq.132), kind=kLoop, calls=%fused_computation.31 | loop fusion | flops 33030144 | bytes 14155777 | tf_op jit(solution)/shard_map/convert_element_type | solution.py:110
  (373 shorter events, 217.8 us)
Async XLA Ops:
  5.7 36.9 %collective-permute-start = (bf16[256,768]{1,0:T(8,128)(2,1)S(1)}, bf16[256,768]{1,0:T(8,128)(2,1)}, u32[]{:S(2)}, u32[]{:S(2)}) collective-permute-start(bf16[256,768]{1,0:T(8,128)(2,1)S(1)} %get-tuple-element.122), channel_id=1, source_target_pairs={{0,2},{1,3},{2,0},{3,1},{4,6},{5,7},{6,4},{7,5},{8,10},{9,11},{10,... | collective-permute-start | bytes 1179656 | tf_op jit(solution)/shard_map/ppermute | solution.py:51
  8.3 38.1 %collective-permute-start.1 = (bf16[256,768]{1,0:T(8,128)(2,1)}, bf16[256,768]{1,0:T(8,128)(2,1)}, u32[]{:S(2)}, u32[]{:S(2)}) collective-permute-start(bf16[256,768]{1,0:T(8,128)(2,1)} %get-tuple-element.121), channel_id=1, source_target_pairs={{0,1},{1,0},{2,3},{3,2},{4,5},{5,4},{6,7},{7,6},{8,9},{9,8},{10,11... | collective-permute-start | bytes 1179656 | tf_op jit(solution)/shard_map/ppermute | solution.py:51
  10.8 100.2 %collective-permute-start.8 = (bf16[256,768]{1,0:T(8,128)(2,1)}, bf16[256,768]{1,0:T(8,128)(2,1)}, u32[]{:S(2)}, u32[]{:S(2)}) collective-permute-start(bf16[256,768]{1,0:T(8,128)(2,1)} %get-tuple-element.118), channel_id=1, source_target_pairs={{0,2},{1,3},{2,0},{3,1},{4,6},{5,7},{6,4},{7,5},{8,10},{9,11},{10,... | collective-permute-start | bytes 1179656 | tf_op jit(solution)/shard_map/ppermute | solution.py:51
  10.9 31.7 %collective-permute-start.4 = (s32[2,2,256]{2,1,0:T(2,128)S(1)}, s32[2,2,256]{2,1,0:T(2,128)S(1)}, u32[]{:S(2)}, u32[]{:S(2)}) collective-permute-start(s32[2,2,256]{2,1,0:T(2,128)S(1)} %pad_add_fusion), channel_id=1, source_target_pairs={{0,2},{1,3},{2,0},{3,1},{4,6},{5,7},{6,4},{7,5},{8,10},{9,11},{10,... | collective-permute-start | bytes 12296 | tf_op jit(solution)/shard_map/ppermute | solution.py:51
  195.8 26.4 %collective-permute-start.6 = (f32[6,768]{1,0:T(8,128)}, f32[6,768]{1,0:T(8,128)}, u32[]{:S(2)}, u32[]{:S(2)}) collective-permute-start(f32[6,768]{1,0:T(8,128)} %fusion.28), channel_id=1, source_target_pairs={{0,1},{1,0},{2,3},{3,2},{4,5},{5,4},{6,7},{7,6},{8,9},{9,8},{10,11... | collective-permute-start | bytes 55304 | tf_op jit(solution)/shard_map/ppermute | solution.py:51
  201.9 27.6 %collective-permute-start.25 = (f32[12,768]{1,0:T(8,128)}, f32[12,768]{1,0:T(8,128)S(1)}, u32[]{:S(2)}, u32[]{:S(2)}) collective-permute-start(f32[12,768]{1,0:T(8,128)} %concatenate.227), channel_id=1, source_target_pairs={{0,1},{1,0},{2,3},{3,2},{4,5},{5,4},{6,7},{7,6},{8,9},{9,8},{10,11... | collective-permute-start | bytes 110600 | tf_op jit(solution)/shard_map/ppermute | solution.py:51
  211.0 134.1 %collective-permute-start.9 = (bf16[512,768]{1,0:T(8,128)(2,1)}, bf16[512,768]{1,0:T(8,128)(2,1)S(1)}, u32[]{:S(2)}, u32[]{:S(2)}) collective-permute-start(bf16[512,768]{1,0:T(8,128)(2,1)} %add_convert_fusion.6), channel_id=1, source_target_pairs={{0,1},{1,0},{2,3},{3,2},{4,5},{5,4},{6,7},{7,6},{8,9},{9,8},{10,11... | collective-permute-start | bytes 2359304 | tf_op jit(solution)/shard_map/ppermute | solution.py:51
  244.6 29.1 %collective-permute-start.47 = (bf16[384,768]{1,0:T(8,128)(2,1)S(1)}, bf16[384,768]{1,0:T(8,128)(2,1)S(1)}, u32[]{:S(2)}, u32[]{:S(2)}) collective-permute-start(bf16[384,768]{1,0:T(8,128)(2,1)S(1)} %constant_dynamic-slice_fusion.4), channel_id=1, source_target_pairs={{0,16},{4,20},{8,24},{12,28},{16,0},{20,4},{24,8},{28,12},{1,17},{... | collective-permute-start | bytes 1769480 | tf_op jit(solution)/shard_map/ppermute | solution.py:51
  247.1 24.9 %collective-permute-start.31 = (bf16[384,768]{1,0:T(8,128)(2,1)S(1)}, bf16[384,768]{1,0:T(8,128)(2,1)S(1)}, u32[]{:S(2)}, u32[]{:S(2)}) collective-permute-start(bf16[384,768]{1,0:T(8,128)(2,1)S(1)} %constant_dynamic-slice_fusion.12), channel_id=1, source_target_pairs={{0,8},{4,12},{8,0},{12,4},{16,24},{20,28},{24,16},{28,20},{1,9},{5... | collective-permute-start | bytes 1769480 | tf_op jit(solution)/shard_map/ppermute | solution.py:51
  247.7 26.8 %collective-permute-start.33 = (bf16[384,768]{1,0:T(8,128)(2,1)S(1)}, bf16[384,768]{1,0:T(8,128)(2,1)S(1)}, u32[]{:S(2)}, u32[]{:S(2)}) collective-permute-start(bf16[384,768]{1,0:T(8,128)(2,1)S(1)} %constant_dynamic-slice_fusion.10), channel_id=1, source_target_pairs={{0,16},{4,20},{8,24},{12,28},{16,0},{20,4},{24,8},{28,12},{1,17},{... | collective-permute-start | bytes 1769480 | tf_op jit(solution)/shard_map/ppermute | solution.py:51
  259.3 25.3 %collective-permute-start.12 = (bf16[384,768]{1,0:T(8,128)(2,1)S(1)}, bf16[384,768]{1,0:T(8,128)(2,1)S(1)}, u32[]{:S(2)}, u32[]{:S(2)}) collective-permute-start(bf16[384,768]{1,0:T(8,128)(2,1)S(1)} %constant_dynamic-slice_fusion.18), channel_id=1, source_target_pairs={{0,8},{4,12},{8,0},{12,4},{16,24},{20,28},{24,16},{28,20},{1,9},{5... | collective-permute-start | bytes 1769480 | tf_op jit(solution)/shard_map/ppermute | solution.py:51
  274.5 21.7 %collective-permute-start.48 = (bf16[192,768]{1,0:T(8,128)(2,1)S(1)}, bf16[192,768]{1,0:T(8,128)(2,1)S(1)}, u32[]{:S(2)}, u32[]{:S(2)}) collective-permute-start(bf16[192,768]{1,0:T(8,128)(2,1)S(1)} %constant_dynamic-slice_fusion.3), channel_id=1, source_target_pairs={{0,8},{4,12},{8,0},{12,4},{16,24},{20,28},{24,16},{28,20},{1,9},{5... | collective-permute-start | bytes 884744 | tf_op jit(solution)/shard_map/ppermute | solution.py:51
  315.4 21.8 %collective-permute-start.36 = (bf16[96,768]{1,0:T(8,128)(2,1)S(1)}, bf16[96,768]{1,0:T(8,128)(2,1)S(1)}, u32[]{:S(2)}, u32[]{:S(2)}) collective-permute-start(bf16[96,768]{1,0:T(8,128)(2,1)S(1)} %constant_dynamic-slice_fusion.8), channel_id=1, source_target_pairs={{0,2},{1,3},{2,0},{3,1},{4,6},{5,7},{6,4},{7,5},{8,10},{9,11},{10,... | collective-permute-start | bytes 442376 | tf_op jit(solution)/shard_map/ppermute | solution.py:51
  324.0 22.1 %collective-permute-start.51 = (bf16[96,768]{1,0:T(8,128)(2,1)S(1)}, bf16[96,768]{1,0:T(8,128)(2,1)S(1)}, u32[]{:S(2)}, u32[]{:S(2)}) collective-permute-start(bf16[96,768]{1,0:T(8,128)(2,1)S(1)} %add_convert_fusion.22), channel_id=1, source_target_pairs={{0,2},{1,3},{2,0},{3,1},{4,6},{5,7},{6,4},{7,5},{8,10},{9,11},{10,... | collective-permute-start | bytes 442376 | tf_op jit(solution)/shard_map/ppermute | solution.py:51
  346.1 23.1 %collective-permute-start.52 = (bf16[192,768]{1,0:T(8,128)(2,1)S(1)}, bf16[192,768]{1,0:T(8,128)(2,1)S(1)}, u32[]{:S(2)}, u32[]{:S(2)}) collective-permute-start(bf16[192,768]{1,0:T(8,128)(2,1)S(1)} %maximum_select_fusion.22), channel_id=1, source_target_pairs={{0,1},{1,0},{2,3},{3,2},{4,5},{5,4},{6,7},{7,6},{8,9},{9,8},{10,11... | collective-permute-start | bytes 884744 | tf_op jit(solution)/shard_map/ppermute | solution.py:51
  369.7 26.8 %collective-permute-start.53 = (bf16[192,768]{1,0:T(8,128)(2,1)S(1)}, bf16[192,768]{1,0:T(8,128)(2,1)S(1)}, u32[]{:S(2)}, u32[]{:S(2)}) collective-permute-start(bf16[192,768]{1,0:T(8,128)(2,1)S(1)} %get-tuple-element.123), channel_id=1, source_target_pairs={{0,16},{4,20},{8,24},{12,28},{16,0},{20,4},{24,8},{28,12},{1,17},{... | collective-permute-start | bytes 884744 | tf_op jit(solution)/shard_map/ppermute | solution.py:51
  371.3 26.2 %collective-permute-start.55 = (bf16[192,768]{1,0:T(8,128)(2,1)S(1)}, bf16[192,768]{1,0:T(8,128)(2,1)S(1)}, u32[]{:S(2)}, u32[]{:S(2)}) collective-permute-start(bf16[192,768]{1,0:T(8,128)(2,1)S(1)} %get-tuple-element.124), channel_id=1, source_target_pairs={{0,8},{4,12},{8,0},{12,4},{16,24},{20,28},{24,16},{28,20},{1,9},{5... | collective-permute-start | bytes 884744 | tf_op jit(solution)/shard_map/ppermute | solution.py:51
  372.8 21.2 %collective-permute-start.39 = (bf16[192,768]{1,0:T(8,128)(2,1)S(1)}, bf16[192,768]{1,0:T(8,128)(2,1)S(1)}, u32[]{:S(2)}, u32[]{:S(2)}) collective-permute-start(bf16[192,768]{1,0:T(8,128)(2,1)S(1)} %get-tuple-element.125), channel_id=1, source_target_pairs={{0,16},{4,20},{8,24},{12,28},{16,0},{20,4},{24,8},{28,12},{1,17},{... | collective-permute-start | bytes 884744 | tf_op jit(solution)/shard_map/ppermute | solution.py:51
  386.1 47.1 %collective-permute-start.24 = (bf16[1536,768]{1,0:T(8,128)(2,1)}, bf16[1536,768]{1,0:T(8,128)(2,1)}, u32[]{:S(2)}, u32[]{:S(2)}) collective-permute-start(bf16[1536,768]{1,0:T(8,128)(2,1)} %pad_maximum_fusion.3), channel_id=1, source_target_pairs={{0,4},{4,0},{8,12},{12,8},{16,20},{20,16},{24,28},{28,24},{1,5},{5... | collective-permute-start | bytes 7077896 | tf_op jit(solution)/shard_map/ppermute | solution.py:51
  396.5 21.9 %collective-permute-start.5 = (bf16[256,768]{1,0:T(8,128)(2,1)S(1)}, bf16[256,768]{1,0:T(8,128)(2,1)S(1)}, u32[]{:S(2)}, u32[]{:S(2)}) collective-permute-start(bf16[256,768]{1,0:T(8,128)(2,1)S(1)} %copy-done.26), channel_id=1, source_target_pairs={{0,2},{1,3},{2,0},{3,1},{4,6},{5,7},{6,4},{7,5},{8,10},{9,11},{10,... | collective-permute-start | bytes 1179656 | tf_op jit(solution)/shard_map/ppermute | solution.py:51
  401.8 23.6 %collective-permute-start.10 = (bf16[256,768]{1,0:T(8,128)(2,1)}, bf16[256,768]{1,0:T(8,128)(2,1)}, u32[]{:S(2)}, u32[]{:S(2)}) collective-permute-start(bf16[256,768]{1,0:T(8,128)(2,1)} %get-tuple-element.116), channel_id=1, source_target_pairs={{0,2},{1,3},{2,0},{3,1},{4,6},{5,7},{6,4},{7,5},{8,10},{9,11},{10,... | collective-permute-start | bytes 1179656 | tf_op jit(solution)/shard_map/ppermute | solution.py:51
  406.1 21.7 %collective-permute-start.56 = (bf16[384,768]{1,0:T(8,128)(2,1)}, bf16[384,768]{1,0:T(8,128)(2,1)}, u32[]{:S(2)}, u32[]{:S(2)}) collective-permute-start(bf16[384,768]{1,0:T(8,128)(2,1)} %maximum_select_fusion.19), channel_id=1, source_target_pairs={{0,16},{4,20},{8,24},{12,28},{16,0},{20,4},{24,8},{28,12},{1,17},{... | collective-permute-start | bytes 1769480 | tf_op jit(solution)/shard_map/ppermute | solution.py:51
  418.4 22.6 %collective-permute-start.43 = (bf16[1536,768]{1,0:T(8,128)(2,1)}, bf16[1536,768]{1,0:T(8,128)(2,1)}, u32[]{:S(2)}, u32[]{:S(2)}) collective-permute-start(bf16[1536,768]{1,0:T(8,128)(2,1)} %pad_maximum_fusion.4), channel_id=1, source_target_pairs={{0,4},{4,0},{8,12},{12,8},{16,20},{20,16},{24,28},{28,24},{1,5},{5... | collective-permute-start | bytes 7077896 | tf_op jit(solution)/shard_map/ppermute | solution.py:51
  433.1 20.9 %collective-permute-start.57 = (bf16[1536,768]{1,0:T(8,128)(2,1)}, bf16[1536,768]{1,0:T(8,128)(2,1)}, u32[]{:S(2)}, u32[]{:S(2)}) collective-permute-start(bf16[1536,768]{1,0:T(8,128)(2,1)} %pad_maximum_fusion.5), channel_id=1, source_target_pairs={{0,4},{4,0},{8,12},{12,8},{16,20},{20,16},{24,28},{28,24},{1,5},{5... | collective-permute-start | bytes 7077896 | tf_op jit(solution)/shard_map/ppermute | solution.py:51
  (81 other events, 862.1 us)

commit v2 on v1

v2 whole, which is shorter than its diff:
```python
from functools import partial

import jax
import jax.numpy as jnp
from jax import lax
from jax.experimental import pallas as pl
from jax.experimental.pallas import tpu as pltpu
from jax.sharding import PartitionSpec as P

f32=jnp.float32; bf16=jnp.bfloat16
norm_eps=1e-12
NSEG=6
HD=64
def dot(a,b): return jnp.dot(a,b,preferred_element_type=f32)
def dot_nt(a,b): return lax.dot_general(a,b,(((1,),(1,)),((),())),preferred_element_type=f32)
def dot_tn(a,b): return lax.dot_general(a,b,(((0,),(0,)),((),())),preferred_element_type=f32)

def gelu_pair(x):
    t = 1.0 / (1.0 + (0.3275911 * 0.7071067811865476) * jnp.abs(x))
    e = jnp.exp(-0.5 * x * x)
    half = (0.5*0.254829592) + t*((0.5*-0.284496736) + t*((0.5*1.421413741) + t*((0.5*-1.453152027) + t*(0.5*1.061405429))))
    tail = half * t * e
    cdf = jnp.where(x > 0, 1.0 - tail, tail)
    return x * cdf, cdf + x * e * 0.3989422804014327

def in_hbm(*arrays):
    return tuple(pltpu.with_memory_space_constraint(a, pltpu.HBM) for a in arrays)

def wide(rows):
    return jnp.concatenate([rows[i:i+1,:] for i in range(rows.shape[0])], axis=1)

def same_segment(left, right):
    lab = lax.broadcasted_iota(jnp.int32, (8, 1), 0)
    hot = lambda s: (lab == s).astype(f32).astype(bf16)
    return (dot_tn(hot(left), hot(right)) - 1.0) * 1e30

OUT_B, G1, B1, DOWN_B, G2, B2, UP_B = range(7)
RB = 128

def rows_norm(r):
    m = jnp.mean(r, axis=-1, keepdims=True)
    c = r - m
    inv = lax.rsqrt(jnp.mean(c*c, axis=-1, keepdims=True) + norm_eps)
    return c * inv, inv

def norm_back(g, xh, inv):
    return inv * (g - jnp.mean(g, axis=-1, keepdims=True) - xh * jnp.mean(g*xh, axis=-1, keepdims=True))

def col_sum(v): return jnp.sum(v, axis=0, keepdims=True)

def mid_kernel(order_ref, att_ref, xa_ref, xb_ref, cota_ref, cotb_ref, itot_ref, seg_ref, ob_ref, g1_ref, b1_ref, db_ref, g2_ref, b2_ref, ub_ref, wo_hbm, wu_hbm, wd_hbm,
               out_ref, segsum_ref, small_ref, dres_ref, dn_ref, dt_ref, gout_ref, gsend_hbm, gkeep_hbm,
               wo, wu, wd, hid, hl, xh1, rs1, act, gp, feed, dfl, dhid, stage, wsem, gsem):
    R, W = att_ref.shape
    nc = wu.shape[0]
    def rows_of(a, b, i):
        h = a.shape[0] // RB
        return a[pl.ds(i*RB,RB),:] if i < h else b[pl.ds((i-h)*RB,RB),:]
    def copies(k):
        c = order_ref[k]
        return (pltpu.make_async_copy(wu_hbm.at[:, pl.ds(c*W, W)], wu.at[k], wsem.at[1+k]),
                pltpu.make_async_copy(wd_hbm.at[pl.ds(c*W, W), :], wd.at[k], wsem.at[1+nc+k]))
    cwo = pltpu.make_async_copy(wo_hbm, wo, wsem.at[0]); cwo.start()
    for k in range(nc):
        for cp in copies(k): cp.start()
    NB = R // RB
    vecs = (ob_ref, g1_ref, b1_ref, db_ref, g2_ref, b2_ref)
    row = lambda i: wide(vecs[i][...])
    lanes = W // 128
    cwo.wait()
    for i in range(NB):
        s = pl.ds(i*RB, RB)
        r = rows_of(xa_ref, xb_ref, i).astype(f32) + dot(att_ref[s, :].astype(bf16), wo[...]) + row(OUT_B)
        xh, inv = rows_norm(r)
        xh1[s,:] = xh
        rs1[s,:] = inv
        h = xh * row(G1) + row(B1)
        hid[s,:] = h
        hl[s,:] = h.astype(bf16)
    for k in range(nc):
        for cp in copies(k): cp.wait()
        ub = wide(ub_ref[pl.ds(order_ref[k]*lanes, lanes), :])
        for j in range(W//256):
            cs = slice(j*256, (j+1)*256)
            pre = dot(hl[...], wu[k, :, cs]) + ub[:, cs]
            a_, g_ = gelu_pair(pre)
            act[k, :, cs] = a_.astype(bf16)
            gp[k, :, cs] = g_.astype(gp.dtype)
        part = dot(act[k], wd[k])
        if k == 0: feed[...] = part
        else: feed[...] += part
    lab = lax.broadcasted_iota(jnp.int32, (8, 1), 0) + 1
    zero = jnp.zeros((1,W),f32)
    segsum = jnp.zeros((8, W), f32)
    sg = ss = sdb = zero
    for i in range(NB):
        s = pl.ds(i*RB, RB)
        xh, inv = rows_norm(hid[s,:] + feed[s,:] + row(DOWN_B))
        o = xh * row(G2) + row(B2)
        oh = o.astype(bf16)
        out_ref[s,:] = oh
        ol = (o - oh.astype(f32)).astype(bf16)
        hot = (lab == seg_ref[:, i*RB:(i+1)*RB]).astype(f32).astype(bf16)
        segsum = segsum + dot(hot, oh) + dot(hot, ol)
        u = rows_of(cota_ref, cotb_ref, i).astype(f32)
        sg = sg + col_sum(u*xh)
        ss = ss + col_sum(u)
        d = norm_back(u * row(G2), xh, inv)
        dhid[s,:] = d
        dl = d.astype(bf16)
        dfl[s,:] = dl
        sdb = sdb + col_sum(dl.astype(f32))
    segsum_ref[...] = segsum
    small_ref[pl.ds(DOWN_B,1), :] = sdb
    small_ref[pl.ds(G2,1), :] = sg
    small_ref[pl.ds(B2,1), :] = ss
    half = nc // 2
    def push(slot, k, kind):
        dst = gsend_hbm if k < half else gkeep_hbm
        return pltpu.make_async_copy(stage.at[slot], dst.at[pl.ds((2*(k % half) + kind)*W, W), :], gsem.at[slot])
    for k in range(nc):
        stage[k] = dot_tn(act[k], dfl[...]).astype(bf16)
        push(k, k, 0).start()
        da = dot_nt(dfl[...], wd[k])
        dp = (da * gp[k].astype(f32)).astype(bf16)
        act[k] = dp
        small_ref[pl.ds(UP_B + order_ref[k],1), :] = col_sum(dp.astype(f32))
        stage[nc+k] = dot_tn(hl[...], dp).astype(bf16)
        push(nc+k, k, 1).start()
        dhid[...] += dot_nt(dp, wu[k])
    sg = ss = sdb = zero
    for i in range(NB):
        s = pl.ds(i*RB, RB)
        dh = dhid[s,:]
        xh = xh1[s,:]
        sg = sg + col_sum(dh*xh)
        ss = ss + col_sum(dh)
        d = norm_back(dh * row(G1), xh, rs1[s,:])
        dres_ref[s,:] = d
        dl = d.astype(bf16)
        dfl[s,:] = dl
        sdb = sdb + col_sum(dl.astype(f32))
    small_ref[pl.ds(OUT_B,1), :] = sdb
    small_ref[pl.ds(G1,1), :] = sg
    small_ref[pl.ds(B1,1), :] = ss
    gout_ref[...] = dot_tn(att_ref[...].astype(bf16), dfl[...]).astype(bf16)
    l0 = lax.broadcasted_iota(jnp.int32, (128,128), 0) // HD
    l1 = lax.broadcasted_iota(jnp.int32, (128,128), 1) // HD
    same = (l0 == l1).astype(f32).astype(bf16)
    for i in range(NB):
        s = pl.ds(i*RB, RB)
        da = dot_nt(dfl[s,:], wo[...])
        it = itot_ref[s,:]
        dn_ref[s,:] = (da * it).astype(bf16)
        p = da * att_ref[s,:]
        ph = p.astype(bf16)
        plow = (p - ph.astype(f32)).astype(bf16)
        for j in range(W//128):
            cs = slice(j*128,(j+1)*128)
            dt_ref[s, cs] = -(dot(ph[:,cs], same) + dot(plow[:,cs], same)) * it[:,cs]
    for k in range(nc):
        push(k, k, 0).wait()
        push(nc+k, k, 1).wait()

def mid(order, att, x, cot, itot, seg_row, vecs, wo, wu, wd):
    R, W = att.shape
    nc = wu.shape[1] // W
    any_ = pl.BlockSpec(memory_space=pltpu.HBM)
    vm = pl.BlockSpec(memory_space=pltpu.VMEM)
    sm = pl.BlockSpec(memory_space=pltpu.SMEM)
    sd = jax.ShapeDtypeStruct
    return pl.pallas_call(
        mid_kernel,
        in_specs=[sm]+[vm]*14+[any_]*3,
        out_specs=[vm]*7+[any_, any_],
        out_shape=[sd((R,W),bf16), sd((8,W),f32), sd((UP_B+nc+6,W),f32), sd((R,W),f32), sd((R,W),bf16), sd((R,W),f32),
                   sd((W,W),bf16), sd((nc*W,W),bf16), sd((nc*W,W),bf16)],
        scratch_shapes=[pltpu.VMEM((W,W),bf16), pltpu.VMEM((nc,W,W),bf16), pltpu.VMEM((nc,W,W),bf16),
                        pltpu.VMEM((R,W),f32), pltpu.VMEM((R,W),bf16), pltpu.VMEM((R,W),f32), pltpu.VMEM((R,1),f32),
                        pltpu.VMEM((nc,R,W),bf16), pltpu.VMEM((nc,R,W),f32), pltpu.VMEM((R,W),f32), pltpu.VMEM((R,W),bf16), pltpu.VMEM((R,W),f32),
                        pltpu.VMEM((2*nc,W,W),bf16), pltpu.SemaphoreType.DMA((1+2*nc,)), pltpu.SemaphoreType.DMA((2*nc,))],
        compiler_params=pltpu.CompilerParams(vmem_limit_bytes=60*1024*1024),
        name="mid",
    )(order, *in_hbm(att, *x, *cot, itot), seg_row, *vecs, wo, wu, wd)

GW = 256
def head_pair_lanes():
    return lax.broadcasted_iota(jnp.int32, (1,128), 1) < HD

def gather_rows(refs, dst, sem):
    at, copies = 0, []
    for i, ref in enumerate(refs):
        copies.append(pltpu.make_async_copy(ref, dst.at[pl.ds(at, ref.shape[0]), :], sem.at[i]))
        at += ref.shape[0]
    return copies

def attn_fwd_kernel(n_parts, *refs):
    parts = refs[:n_parts]
    (wq_ref, wk_ref, wv_ref, qb_ref, vb_ref, sk_ref,
     q_ref, k_ref, v_ref, att_ref, itot_ref, bias, x_ref, sem) = refs[n_parts:]
    R = q_ref.shape[0]
    @pl.when(pl.program_id(0) == 0)
    def _():
        copies = gather_rows(parts, x_ref, sem)
        for c in copies: c.start()
        bias[...] = same_segment(sk_ref[:, 0:R], sk_ref[...])
        for c in copies: c.wait()
    lanes = GW // 128
    at = pl.ds(pl.program_id(0)*lanes, lanes)
    qb, vb = wide(qb_ref[at, :]), wide(vb_ref[at, :])
    q = (0.125*(dot(x_ref[0:R,:], wq_ref[...]) + qb)).astype(bf16)
    k = dot(x_ref[...], wk_ref[...]).astype(bf16)
    v = (dot(x_ref[...], wv_ref[...]) + vb).astype(bf16)
    q_ref[...] = q; k_ref[...] = k; v_ref[...] = v
    first = head_pair_lanes()
    for p in range(GW//128):
        cs = slice(p*128,(p+1)*128)
        qp, kp, vp = q[:,cs], k[:,cs], v[:,cs]
        one = jnp.ones_like(vp); zero=jnp.zeros_like(qp)
        res = []
        for h in range(2):
            mine = first if h==0 else jnp.logical_not(first)
            s = dot_nt(jnp.where(mine, qp, zero), kp)
            e = jnp.exp(s + bias[...]).astype(bf16)
            res.append(dot(e, jnp.where(mine, vp, one)))
        num = jnp.where(first, res[0], res[1])
        tot = pltpu.roll(jnp.where(first, res[1], res[0]), HD, 1)
        it = 1.0 / tot
        att_ref[:,cs] = num * it
        itot_ref[:,cs] = it

def attn_fwd(parts, wq, wk, wv, qb, vb, sk, R):
    W = wq.shape[0]
    N = sum(p.shape[0] for p in parts)
    sd = jax.ShapeDtypeStruct
    full = lambda a: pl.BlockSpec(a.shape, lambda j: (0,0))
    col = lambda r: pl.BlockSpec((r,GW), lambda j: (0,j))
    return pl.pallas_call(
        partial(attn_fwd_kernel, len(parts)), grid=(W//GW,),
        in_specs=[pl.BlockSpec(memory_space=pltpu.HBM)]*len(parts)+[col(W), col(W), col(W), full(qb), full(vb), full(sk)],
        out_specs=[col(R), col(N), col(N), col(R), col(R)],
        out_shape=[sd((R,W),bf16), sd((N,W),bf16), sd((N,W),bf16), sd((R,W),f32), sd((R,W),f32)],
        scratch_shapes=[pltpu.VMEM((R,N),f32), pltpu.VMEM((N,W),bf16), pltpu.SemaphoreType.DMA((len(parts),))],
        compiler_params=pltpu.CompilerParams(vmem_limit_bytes=24*1024*1024, dimension_semantics=("arbitrary",)),
        name="attn_fwd",
    )(*parts, *in_hbm(wq, wk, wv), qb, vb, sk)

def attn_bwd_kernel(q_ref, k_ref, v_ref, dn_ref, dt_ref, sk_ref, dq_ref, dk_ref, dv_ref, bias):
    @pl.when(pl.program_id(0) == 0)
    def _():
        bias[...] = same_segment(sk_ref[...], sk_ref[:, 0:q_ref.shape[0]])
    first = head_pair_lanes()
    lane = lax.broadcasted_iota(jnp.int32, (1,128), 1)
    for p in range(q_ref.shape[1]//128):
        cs = slice(p*128,(p+1)*128)
        qp, kp, vp, dnp = q_ref[:,cs], k_ref[:,cs], v_ref[:,cs], dn_ref[:,cs]
        dtr = pltpu.roll(dt_ref[:,cs], HD, 1)
        hi = dtr.astype(bf16)
        rest = dtr - hi.astype(f32)
        mid_ = rest.astype(bf16)
        low = (rest - mid_.astype(f32)).astype(bf16)
        res=[]
        for h in range(2):
            mine = first if h==0 else jnp.logical_not(first)
            o = HD if h==0 else 0
            ex = jnp.where(lane==o, hi, jnp.where(lane==o+1, mid_, jnp.where(lane==o+2, low, jnp.zeros_like(hi))))
            dne = jnp.where(mine, dnp, ex)
            ve = jnp.where(mine, vp, jnp.where((lane>=o)&(lane<o+3), jnp.ones_like(vp), jnp.zeros_like(vp)))
            s = dot_nt(jnp.where(mine, kp, jnp.zeros_like(kp)), qp)
            e = jnp.exp(s + bias[...])
            pr = dot_nt(ve, dne)
            ds = (e * pr).astype(bf16)
            dv = dot(e.astype(bf16), dnp)
            dk = dot(ds, qp)
            dq = dot_tn(ds, kp)
            res.append((dq,dk,dv))
        dq_ref[:,cs] = (jnp.where(first, res[0][0], res[1][0]).astype(bf16).astype(f32)*0.125).astype(bf16)
        dk_ref[:,cs] = jnp.where(first, res[0][1], res[1][1]).astype(bf16)
        dv_ref[:,cs] = jnp.where(first, res[0][2], res[1][2]).astype(bf16)

def attn_bwd(q,k,v,dn,dt,sk,start,count):
    R,W=q.shape; N=k.shape[0]
    sd = jax.ShapeDtypeStruct
    full = lambda a: pl.BlockSpec(a.shape, lambda j: (0,0))
    GB=128
    col = lambda r: pl.BlockSpec((r,GB), lambda j: (0,j+start))
    out = lambda r: pl.BlockSpec((r,GB), lambda j: (0,j))
    return pl.pallas_call(
        attn_bwd_kernel, grid=(count,),
        in_specs=[col(R), col(N), col(N), col(R), col(R), full(sk)],
        out_specs=[out(R), out(N), out(N)],
        out_shape=[sd((R,GB*count),bf16), sd((N,GB*count),bf16), sd((N,GB*count),bf16)],
        scratch_shapes=[pltpu.VMEM((N,R),f32)],
        compiler_params=pltpu.CompilerParams(vmem_limit_bytes=20*1024*1024, dimension_semantics=("arbitrary",)),
        name="attn_bwd",
    )(*in_hbm(q,k,v,dn,dt),sk)

def proj_bwd_kernel(n_parts, *refs):
    tokens = refs[:n_parts]
    (bit_ref, dqa_ref, dqb_ref, dka_ref, dkb_ref, dva_ref, dvb_ref, wq_ref, wk_ref, wv_ref, dres_ref, gout_ref,
     mine_ref, pair_ref, bsum_ref, gsend_hbm, gkeep_hbm, stage, x_ref, sem, xsem) = refs[n_parts:]
    copies = gather_rows(tokens, x_ref, xsem)
    for c in copies: c.start()
    R, CA = dqa_ref.shape
    W = x_ref.shape[1]
    bit = bit_ref[0]
    parts = (slice(0,CA), slice(CA,W))
    def push(i, start):
        src = gout_ref if i == 3 else stage.at[i]
        def go(dst):
            cp = pltpu.make_async_copy(src, dst.at[pl.ds((i%2)*W, W), :], sem.at[i])
            cp.start() if start else cp.wait()
        @pl.when(bit == i//2)
        def _(): go(gkeep_hbm)
        @pl.when(bit != i//2)
        def _(): go(gsend_hbm)
    push(3, True)
    for c in copies: c.wait()
    for i, refs in ((2,(dva_ref,dvb_ref)), (1,(dka_ref,dkb_ref)), (0,(dqa_ref,dqb_ref))):
        for ref, cs in zip(refs, parts):
            n = ref.shape[0]
            stage[i, :, cs] = dot_tn(x_ref[0:n,:], ref[...]).astype(bf16)
        push(i, True)
    def back(refs, w_ref, rows):
        return dot_nt(refs[0][rows,:], w_ref[:,parts[0]]) + dot_nt(refs[1][rows,:], w_ref[:,parts[1]])
    top, rest = slice(0,R), slice(R,2*R)
    pair_ref[...] = (back((dka_ref,dkb_ref), wk_ref, rest) + back((dva_ref,dvb_ref), wv_ref, rest)).astype(bf16)
    mine_ref[...] = (dres_ref[...] + back((dqa_ref,dqb_ref), wq_ref, top) + back((dka_ref,dkb_ref), wk_ref, top)
                     + back((dva_ref,dvb_ref), wv_ref, top))
    for ref, cs in zip((dqa_ref,dqb_ref), parts): bsum_ref[0:1,cs] = col_sum(ref[...].astype(f32))
    for ref, cs in zip((dva_ref,dvb_ref), parts): bsum_ref[1:2,cs] = col_sum(ref[...].astype(f32))
    for i in range(4): push(i, False)

def proj_bwd(bit, grads, tokens, wq, wk, wv, dres, gout):
    R, W = dres.shape
    any_ = pl.BlockSpec(memory_space=pltpu.HBM)
    vm = pl.BlockSpec(memory_space=pltpu.VMEM)
    sm = pl.BlockSpec(memory_space=pltpu.SMEM)
    sd = jax.ShapeDtypeStruct
    return pl.pallas_call(
        partial(proj_bwd_kernel, len(tokens)),
        in_specs=[any_]*len(tokens)+[sm]+[vm]*11, out_specs=[vm,vm,vm,any_,any_],
        out_shape=[sd((R,W),f32), sd((R,W),bf16), sd((2,W),f32), sd((2*W,W),bf16), sd((2*W,W),bf16)],
        scratch_shapes=[pltpu.VMEM((3,W,W),bf16), pltpu.VMEM((2*R,W),bf16), pltpu.SemaphoreType.DMA((4,)), pltpu.SemaphoreType.DMA((len(tokens),))],
        compiler_params=pltpu.CompilerParams(vmem_limit_bytes=32*1024*1024),
        name="proj_bwd",
    )(*tokens, bit, *in_hbm(*grads, wq, wk, wv, dres, gout))

def emit_kernel(up_from, n_prev, place_ref, own_m, own_r, oth_m, oth_r, *refs):
    outs, stage, sem = refs[n_prev:-2], refs[-2], refs[-1]
    n, W = own_m.shape
    bit = place_ref[0]
    mine, theirs = place_ref[1], place_ref[2]
    pieces = ((bit, mine, own_m), (bit, 1 - mine, own_r), (1 - bit, theirs, oth_m), (1 - bit, 1 - theirs, oth_r))
    def send(i, start):
        half, block, ref = pieces[i]
        for b in range(2):
            for h in range(2):
                if up_from is None: dst = outs[2*h + b]
                elif b == 0: dst = outs[0].at[pl.ds((2*h + up_from)*W, W), :]
                else: dst = outs[1].at[:, pl.ds((2*h + up_from)*W, W)]
                @pl.when((half == h) & (block == b))
                def _():
                    cp = pltpu.make_async_copy(stage.at[i], dst, sem.at[i])
                    cp.start() if start else cp.wait()
    for i, (half, block, ref) in enumerate(pieces):
        stage[i] = ref[...].astype(f32)
        send(i, True)
    for i in range(len(pieces)): send(i, False)

def emit(place, pieces, out_shape, up_from=None, prev=()):
    n, W = pieces[0].shape
    any_ = pl.BlockSpec(memory_space=pltpu.HBM)
    vm = pl.BlockSpec(memory_space=pltpu.VMEM)
    sm = pl.BlockSpec(memory_space=pltpu.SMEM)
    return pl.pallas_call(
        partial(emit_kernel, up_from, len(prev)),
        in_specs=[sm]+[vm]*4+[any_]*len(prev), out_specs=[any_]*len(out_shape),
        out_shape=[jax.ShapeDtypeStruct(s, f32) for s in out_shape],
        input_output_aliases={5+i: i for i in range(len(prev))},
        scratch_shapes=[pltpu.VMEM((4,n,W),f32), pltpu.SemaphoreType.DMA((4,))],
        compiler_params=pltpu.CompilerParams(vmem_limit_bytes=24*1024*1024),
        name="emit",
    )(place, *pieces, *prev)

def split_kernel(groups, bit_ref, keep_hbm, recv_hbm, *refs):
    outs, (a, b, o, sem) = refs[:2*groups], refs[2*groups:]
    n, W = outs[0].shape
    bit = bit_ref[0]
    def load(i):
        half = bit if i % 2 else 1 - bit
        src = pl.ds(((i//2)*2 + half)*n, n)
        return (pltpu.make_async_copy(keep_hbm.at[src, :], a.at[i], sem.at[0, i]),
                pltpu.make_async_copy(recv_hbm.at[src, :], b.at[i], sem.at[1, i]))
    for i in range(2*groups):
        for c in load(i): c.start()
    for i in range(2*groups):
        for c in load(i): c.wait()
        o[i] = (a[i].astype(f32) + b[i].astype(f32)).astype(bf16)
        pltpu.make_async_copy(o.at[i], outs[i], sem.at[2, i]).start()
    for i in range(2*groups): pltpu.make_async_copy(o.at[i], outs[i], sem.at[2, i]).wait()

def split_add(bit, keep, recv, groups):
    n, W = keep.shape[0] // (2*groups), keep.shape[1]
    any_ = pl.BlockSpec(memory_space=pltpu.HBM)
    return pl.pallas_call(
        partial(split_kernel, groups),
        in_specs=[pl.BlockSpec(memory_space=pltpu.SMEM), any_, any_], out_specs=[any_]*(2*groups),
        out_shape=[jax.ShapeDtypeStruct((n,W),bf16)]*(2*groups),
        scratch_shapes=[pltpu.VMEM((2*groups,n,W),bf16)]*3+[pltpu.SemaphoreType.DMA((3,2*groups))],
        compiler_params=pltpu.CompilerParams(vmem_limit_bytes=24*1024*1024),
        name="split_add",
    )(bit, keep, recv)

D = 768
pool_eps = 1e-06


def matryoshka(averages):
    pieces = []
    for prefix in (D, D * 2 // 3, D // 3, D // 6, D // 12):
        leading = averages[..., :prefix]
        centred = leading - jnp.mean(leading, axis=-1, keepdims=True)
        pieces.append(
            centred * lax.rsqrt(jnp.mean(centred * centred, axis=-1, keepdims=True) + pool_eps)
        )
    return jnp.concatenate(pieces, axis=-1)


def part_of(value, index, count):
    rows = value.shape[0] // count
    return lax.dynamic_slice_in_dim(value, index * rows, rows, 0)


def ordered(bit, mine, theirs):
    first = lax.broadcasted_iota(jnp.int32, (2,) + (1,) * mine.ndim, 0) == bit
    return jnp.where(first, mine[None], theirs[None]).reshape((-1,) + mine.shape[1:])


def sum_of(arrays):
    total = arrays[0].astype(f32)
    for array in arrays[1:]:
        total = total + array.astype(f32)
    return total.astype(bf16)


fence = lax.optimization_barrier


class Links:
    def __init__(self, n_rows, n_blk):
        self.size = {"rows": n_rows, "blk": n_blk}
        self.at = {"rows": lax.axis_index("rows"), "blk": lax.axis_index("blk")}
        self.near = ("rows", 0, 0)
        self.near_bit = self.at["rows"] % 2
        far = list(range(1, n_rows.bit_length() - 1))
        self.far = [("rows", a, b) for a, b in zip(far, far[::-1])]
        self.plain_far = [("rows", a, a) for a in far]
        self.blk_bits = [("blk", k, k) for k in range(n_blk.bit_length() - 1)]

    def bit(self, stage, flip=False):
        axis, even, odd = stage
        at = self.at[axis]
        if even == odd:
            return (at >> even) % 2
        near = 1 - self.near_bit if flip else self.near_bit
        return jnp.where(near == 0, (at >> even) % 2, (at >> odd) % 2)

    def swap(self, value, stage):
        axis, even, odd = stage
        pairs = [(i, i ^ (1 << (odd if i % 2 and even != odd else even))) for i in range(self.size[axis])]
        return lax.ppermute(value, axis, pairs)

    def halve(self, addends, stages):
        for stage in stages:
            bit = self.bit(stage)
            send = sum_of([part_of(a, 1 - bit, 2) for a in addends])
            addends = [part_of(a, bit, 2) for a in addends] + [self.swap(send, stage)]
        return addends

    def double(self, value, stages):
        for stage in stages[::-1]:
            value = ordered(self.bit(stage), value, self.swap(value, stage))
        return value

    def last(self, value):
        return value, self.swap(value, self.far[0]), self.swap(value, self.near)

    def finish(self, group):
        return (*group, self.swap(group[1], self.near))


def local(
    n_rows,
    n_blk,
    tokens,
    segments,
    query_weight,
    query_bias,
    key_weight,
    value_weight,
    value_bias,
    out_weight,
    out_bias,
    first_gain,
    first_shift,
    up_weight,
    up_bias,
    down_weight,
    down_bias,
    second_gain,
    second_shift,
    cotangent,
):
    links = Links(n_rows, n_blk)
    pair, cross = links.blk_bits
    seq_at = links.at["blk"] // 2
    near_bit = links.near_bit
    num_seq, tok_rows, width = tokens.shape
    ff = up_weight.shape[1]
    chunks = ff // width
    total_rows = 2 * tok_rows

    own = lax.dynamic_index_in_dim(tokens, seq_at, 0, keepdims=False)
    other = lax.dynamic_index_in_dim(tokens, 1 - seq_at, 0, keepdims=False)
    piece = tok_rows // 2
    far_a = links.swap(other[:piece], cross)
    far_b = links.swap(other[piece:], cross)
    near_block = links.swap(own, pair)
    seg_pair = jnp.stack([segments, links.swap(segments, pair)])
    seg_cross = links.swap(seg_pair, cross)
    last_a = links.swap(far_a, pair)
    last_b = links.swap(far_b, pair)
    seg_mine = lax.dynamic_index_in_dim(seg_pair, seq_at, 1, keepdims=False)
    seg_far = lax.dynamic_index_in_dim(seg_cross, seq_at, 1, keepdims=False)
    seg_keys = jnp.concatenate([seg_mine[0], seg_far[0], seg_mine[1], seg_far[1]], 0)
    seg_query = seg_keys[:total_rows]
    blocks = [own, far_a, far_b, near_block, last_a, last_b]
    cot_other = lax.dynamic_index_in_dim(cotangent, 1 - seq_at, 0, keepdims=False)
    cot_own = lax.dynamic_index_in_dim(cotangent, seq_at, 0, keepdims=False)
    cot_other, cot_own, *blocks = fence((cot_other, cot_own, *blocks))
    cot_far = links.swap(cot_other, cross)

    queries, keys, values, attended, inv_totals = attn_fwd(
        blocks, query_weight, key_weight, value_weight, query_bias.reshape(-1, 128),
        value_bias.reshape(-1, 128), seg_keys[None, :], total_rows,
    )
    vectors = [
        v.reshape(-1, 128)
        for v in (out_bias, first_gain, first_shift, down_bias, second_gain, second_shift, up_bias)
    ]
    half = chunks // 2
    order = jnp.concatenate(
        [(1 - near_bit) * half + jnp.arange(half), near_bit * half + jnp.arange(half)]
    ).astype(jnp.int32)
    far_block = jnp.concatenate(blocks[1:3], 0)
    out_low, seg_sums, small, d_resid, d_numer, d_total, grad_out, ffn_send, ffn_keep = mid(
        order, attended, (own, far_block), (cot_own, cot_far), inv_totals, seg_query[None, :],
        vectors, out_weight, up_weight, down_weight,
    )
    seg_row = seg_keys[None, :]
    back_in = (queries, keys, values, d_numer, d_total)
    first, rest = links.far[:1], links.far[1:]
    first_bit = links.bit(first[0]).reshape(1).astype(jnp.int32)
    ffn_recv = links.swap(ffn_send, links.near)
    grads_a = attn_bwd(*back_in, seg_row, 0, 2)
    ffn_keep, ffn_recv, grads_a, back_in = fence((ffn_keep, ffn_recv, grads_a, back_in))

    send_one, keep_one, send_two, keep_two = split_add(first_bit, ffn_keep, ffn_recv, 2)
    send_one, back_in = fence((send_one, back_in))
    one = [keep_one, links.swap(send_one, first[0])]
    grads_b = attn_bwd(*back_in, seg_row, 2, width // 128 - 2)
    one, send_two, grads_a, grads_b = fence((one, send_two, grads_a, grads_b))

    one = [sum_of(links.halve(one, rest))]
    two = [keep_two, links.swap(send_two, first[0])]
    out_back = links.swap(out_low[tok_rows:], cross)
    grads = [g for pair_of in zip(grads_a, grads_b) for g in pair_of]
    d_mine, d_pair, bias_sums, attn_send, attn_keep = proj_bwd(
        near_bit.reshape(1), grads, blocks, query_weight, key_weight,
        value_weight, d_resid, grad_out,
    )
    one, two, out_back, d_mine, d_pair, bias_sums, attn_send, attn_keep = fence(
        (one, two, out_back, d_mine, d_pair, bias_sums, attn_send, attn_keep)
    )

    attn_recv = links.swap(attn_send, links.near)
    two = [sum_of(links.halve(two, rest))]
    one = links.halve(one, [pair])
    layer_output = ordered(seq_at, out_low[:tok_rows][None], out_back[None])
    seg_sums = seg_sums[:NSEG]
    seg_recv = links.swap(seg_sums, pair)
    small = jnp.concatenate([small[: UP_B + chunks], bias_sums], 0)
    one, two, attn_recv, attn_keep, small, seg_sums, seg_recv, layer_output = fence(
        (one, two, attn_recv, attn_keep, small, seg_sums, seg_recv, layer_output)
    )

    send_three, keep_three = split_add(first_bit, attn_keep, attn_recv, 1)
    three = [keep_three, links.swap(send_three, first[0])]
    one = [sum_of(links.halve(one, [cross]))]
    two = links.halve(two, [pair])
    labels = jnp.arange(1, NSEG + 1, dtype=jnp.int32)
    counts = jnp.sum((seg_keys[None, :] == labels[:, None]).astype(f32), axis=1)
    pooled_one = (seg_sums + seg_recv) / counts[:, None]
    pooled_two = links.swap(pooled_one, cross)
    small = small + links.swap(small, pair)
    one, two, three, small, pooled_one, pooled_two = fence((one, two, three, small, pooled_one, pooled_two))

    three = [sum_of(links.halve(three, rest))]
    one = links.double(one[0], [cross])
    two = [sum_of(links.halve(two, [cross]))]
    small = small + links.swap(small, cross)
    pooled = matryoshka(ordered(seq_at, pooled_one[None], pooled_two[None]))
    one, two, three, small, pooled = fence((one, two, three, small, pooled))

    one = links.double(one, [pair])
    two = links.double(two[0], [cross])
    three = links.halve(three, [pair])
    small = small + links.swap(small, links.near)
    one, two, three, small = fence((one, two, three, small))

    one = links.double(one, rest)
    two = links.double(two, [pair])
    three = [sum_of(links.halve(three, [cross]))]
    for stage in links.plain_far:
        small = small + links.swap(small, stage)
    one, two, three, small, d_pair = fence((one, two, three, small, d_pair))

    one = links.last(one)
    two = links.double(two, rest)
    three = links.double(three[0], [cross])
    d_pair = links.swap(d_pair, pair)
    one, two, three, d_pair, d_mine = fence((one, two, three, d_pair, d_mine))

    two = links.last(two)
    three = links.double(three, [pair])
    one = links.finish(one)
    d_mine = (d_mine + d_pair.astype(f32)).astype(bf16)
    one, two, three, d_mine = fence((one, two, three, d_mine))

    place = jnp.stack([near_bit, links.bit(first[0]), links.bit(first[0], True)]).astype(jnp.int32)
    three = links.double(three, rest)
    two = links.finish(two)
    d_back = links.swap(d_mine[tok_rows:], cross)
    ffn_sums = emit(place, one, ((ff, width), (width, ff)), 0)
    two, three, d_mine, ffn_sums = fence((two, three, d_mine, ffn_sums))

    three = links.last(three)
    down_sum, up_sum = emit(place, two, ((ff, width), (width, ff)), 1, ffn_sums)
    three, d_mine, d_back, down_sum, up_sum = fence((three, d_mine, d_back, down_sum, up_sum))

    three = links.finish(three)
    grad_tokens = ordered(seq_at, d_mine[:tok_rows][None], d_back[None])
    query_sum, key_sum, value_sum, out_sum = emit(place, three, ((width, width),) * 4)
    return (
        layer_output,
        pooled,
        grad_tokens,
        query_sum,
        small[UP_B + chunks],
        key_sum,
        value_sum,
        small[UP_B + chunks + 1],
        out_sum,
        small[OUT_B],
        small[G1],
        small[B1],
        up_sum,
        small[UP_B : UP_B + chunks].reshape(-1),
        down_sum,
        small[DOWN_B],
        small[G2],
        small[B2],
    )


def solution(mesh):
    row_split = P("rows", "blk", None)
    return jax.shard_map(
        partial(local, mesh.shape["rows"], mesh.shape["blk"]),
        mesh=mesh,
        in_specs=(row_split, P("rows", "blk")) + (P(),) * 15 + (row_split,),
        out_specs=(row_split, P("rows", None, None), row_split) + (P(),) * 15,
        check_vma=False,
    )
```

time: 465 us -> 330 us (0.71)
  matrix products: 148 us -> 0 us
  Pallas kernels: 0 us -> 106 us
  waiting for transfers between devices: 157 us -> 111 us
  other arithmetic: 56.5 us -> 19.5 us
  starting transfers between devices: 66.6 us -> 57.5 us
    dot_general x30 -> x0, matrix products: 148 us -> none  [the longest x6 32.4 us: matmul(): return jnp.dot(left, right, preferred_element_type=f32)]
    pallas_call x0 -> x10, Pallas kernels: none -> 106 us  [the longest x1 31.8 us: mid(): pl.pallas_call(mid_kernel, in_specs=[sm] + [vm] * 14 + [any_] * 3, out_sp...]
    ppermute x58 -> x50, waiting for transfers between devices: 157 us -> 111 us  [swap(): return lax.ppermute(value, axis, pairs)]
    unnamed x95 -> x106, local copies, waits for them, and re-layouts: 5.54 us -> 21.3 us
    concatenate x9 -> x3, other arithmetic: 13 us -> 1.42 us  [the longest x1 0.82 us: local(): far_block = jnp.concatenate(blocks[1:3], 0)]
    convert_element_type x25 -> x13, other arithmetic: 18.5 us -> 7.15 us  [the longest x12 6.1 us: sum_of(): return total.astype(bf16)]
    ppermute x58 -> x50, starting transfers between devices: 66.6 us -> 57.5 us  [swap(): return lax.ppermute(value, axis, pairs)]
    split x2 -> x0, local copies, waits for them, and re-layouts: 6.94 us -> none  [the longest x1 3.82 us: local(): query_sum, key_sum, value_sum, out_sum = jnp.split(attn_sum, 4, 0)]
  transfers between devices with their start and end apart: 58 -> 50, of which waited for: 29 -> 23; matrix products, arithmetic and copies ran while one was open for 30% -> 8% of each run, Pallas kernels for 0% -> 19%
where the time goes in v2:
time: 330 us; the launch traced here: 325 us
  waiting for transfers between devices  111 us (34%)
  Pallas kernels  106 us (32%)
  starting transfers between devices  57.5 us (17%)
  local copies, waits for them, and re-layouts  30 us (9%)
  other arithmetic  19.5 us (6%)
    ppermute x50, waiting for transfers between devices, swap(): return lax.ppermute(value, axis, pairs)  111 us
    ppermute x50, starting transfers between devices, swap(): return lax.ppermute(value, axis, pairs)  57.5 us
    pallas_call x1, Pallas kernels, mid(): pl.pallas_call(mid_kernel, in_specs=[sm] + [vm] * 14 + [any_] * 3, out_sp...  31.8 us
    pallas_call x2, Pallas kernels, attn_bwd(): pl.pallas_call(attn_bwd_kernel, grid=(count,), in_specs=[col(R), col(N),...  22.5 us
    unnamed x106, local copies, waits for them, and re-layouts  21.3 us
    pallas_call x1, Pallas kernels, attn_fwd(): pl.pallas_call(partial(attn_fwd_kernel, len(parts)), grid=(W // GW,), in_...  15.6 us
    pallas_call x3, Pallas kernels, emit(): pl.pallas_call(partial(emit_kernel, up_from, len(prev)), in_specs=[sm] +...  14.7 us
    pallas_call x1, Pallas kernels, proj_bwd(): pl.pallas_call(partial(proj_bwd_kernel, len(tokens)), in_specs=[any_] * l...  14.5 us
  transfers between devices with their start and end apart: 50, of which 23 were waited for; matrix products, arithmetic and copies ran while one was open for 8% of the time, Pallas kernels for 19%

profile of v2, /device:TPU:0, one launch (start us, length us, event | category | flops | bytes accessed | tf_op | source)
XLA Modules:
  0.0 325.4 jit_solution(3937051448202566220)
XLA Ops:
  1.8 4.1 %collective-permute-start = (bf16[128,768]{1,0:T(8,128)(2,1)S(1)}, bf16[128,768]{1,0:T(8,128)(2,1)S(1)}, u32[]{:S(2)}, u32[]{:S(2)}) collective-permute-start(bf16[128,768]{1,0:T(8,128)(2,1)S(1)} %get-tuple-element.319), channel_id=1, source_target_pairs={{0,2},{1,3},{2,0},{3,1},{4,6},{5,7},{6,4},{7,5},{8,10},{9,11},{10,... | collective-permute-start | bytes 589832 | tf_op jit(solution)/shard_map/ppermute | solution.py:472
  10.6 14.5 %collective-permute-done.5 = s32[2,256]{1,0:T(2,128)S(1)} collective-permute-done((s32[2,256]{1,0:T(2,128)S(1)}, s32[2,256]{1,0:T(2,128)S(1)}, u32[]{:S(2)}, u32[]{:S(2)}) %collective-permute-start.5) | collective-permute-done | bytes 2080 | tf_op jit(solution)/shard_map/ppermute | solution.py:472
  25.0 2.7 collective-permute-start.6
  30.4 5.2 %collective-permute-done.3.refs_4_ = bf16[128,768]{1,0:T(8,128)(2,1)S(1)} collective-permute-done((bf16[128,768]{1,0:T(8,128)(2,1)S(1)}, bf16[128,768]{1,0:T(8,128)(2,1)S(1)}, u32[]{:S(2)}, u32[]{:S(2)}) %collective-permute-start.3) | collective-permute-done | bytes 196640 | tf_op jit(solution)/shard_map/ppermute | solution.py:472
  38.6 15.6 %attn_fwd.1 = (bf16[512,768]{1,0:T(8,128)(2,1)S(1)}, bf16[1024,768]{1,0:T(8,128)(2,1)S(1)}, bf16[1024,768]{1,0:T(8,128)(2,1)S(1)}, f32[512,768]{1,0:T(8,128)S(1)}, f32[512,768]{1,0:T(8,128)S(1)}) custom-call(bf16[256,768]{1,0:T(8,128)(2,1)S(1)} %dynamic-slice_bitcast_fusion.refs_0_.xa_ref, bf16[128,768]{1,0:T(8,128)(2,1)S(1)} %collective-permute-done.refs_1_, ...), custom_call_target="tpu_custom_call" | custom-call | tf_op jit(solution)/shard_map/attn_fwd/pallas_call | solution.py:238
  60.8 31.8 %mid.1 = (bf16[512,768]{1,0:T(8,128)(2,1)}, f32[8,768]{1,0:T(8,128)}, f32[16,768]{1,0:T(8,128)}, f32[512,768]{1,0:T(8,128)}, bf16[512,768]{1,0:T(8,128)(2,1)}, /...) custom-call(s32[4]{0:T(128)} %pad_add_fusion.3.order_ref, ...), custom_call_target="tpu_custom_call" | custom-call | tf_op jit(solution)/shard_map/mid/pallas_call | solution.py:172
  92.7 8.3 %attn_bwd.2 = (bf16[512,256]{1,0:T(8,128)(2,1)S(1)}, bf16[1024,256]{1,0:T(8,128)(2,1)S(1)}, bf16[1024,256]{1,0:T(8,128)(2,1)S(1)}) custom-call(bf16[512,768]{1,0:T(8,128)(2,1)} %copy-done.5, bf16[1024,768]{1,0:T(8,128)(2,1)} %copy-done.2, bf16[1024,768]{1,0:T(8,128)(2,1)} %copy-done.3, bf16[512,768]{1,0:T(8,128)(2,1)} %get-tuple-element.199.dn_ref, ...), custom_call_target="tpu_custom_call" | custom-call | tf_op jit(solution)/shard_map/attn_bwd/pallas_call | solution.py:288
  103.4 3.9 %split_add.2 = (bf16[768,768]{1,0:T(8,128)(2,1)S(1)}, bf16[768,768]{1,0:T(8,128)(2,1)S(1)}, bf16[768,768]{1,0:T(8,128)(2,1)}, bf16[768,768]{1,0:T(8,128)(2,1)S(1)}) custom-call(s32[1]{0:T(128)} %bitcast.bit_ref, bf16[3072,768]{1,0:T(8,128)(2,1)S(1)} %copy-done.4, bf16[3072,768]{1,0:T(8,128)(2,1)} %collective-permute-done.8.recv_hbm), custom_call_target="tpu_custom_call" | custom-call | tf_op jit(solution)/shard_map/split_add/pallas_call | solution.py:406
  108.9 14.2 %attn_bwd.3 = (bf16[512,512]{1,0:T(8,128)(2,1)S(1)}, bf16[1024,512]{1,0:T(8,128)(2,1)S(1)}, bf16[1024,512]{1,0:T(8,128)(2,1)S(1)}) custom-call(bf16[512,768]{1,0:T(8,128)(2,1)} %copy-done.5, bf16[1024,768]{1,0:T(8,128)(2,1)} %copy-done.2, bf16[1024,768]{1,0:T(8,128)(2,1)} %copy-done.3, bf16[512,768]{1,0:T(8,128)(2,1)} %get-tuple-element.199.dn_ref, ...), custom_call_target="tpu_custom_call" | custom-call | tf_op jit(solution)/shard_map/attn_bwd/pallas_call | solution.py:288
  130.1 2.9 collective-permute-start.12
  134.8 14.5 %proj_bwd.1 = (f32[512,768]{1,0:T(8,128)S(1)}, bf16[512,768]{1,0:T(8,128)(2,1)S(1)}, f32[2,768]{1,0:T(2,128)S(1)}, bf16[1536,768]{1,0:T(8,128)(2,1)}, bf16[1536,768]{1,0:T(8,128)(2,1)S(1)}) custom-call(bf16[256,768]{1,0:T(8,128)(2,1)S(1)} %copy-done.1, bf16[128,768]{1,0:T(8,128)(2,1)S(1)} %collective-permute-done.refs_1_, ...), custom_call_target="tpu_custom_call" | custom-call | tf_op jit(solution)/shard_map/proj_bwd/pallas_call | solution.py:340
  158.1 4.6 %collective-permute-done.14 = bf16[384,768]{1,0:T(8,128)(2,1)S(1)} collective-permute-done((bf16[384,768]{1,0:T(8,128)(2,1)S(1)}, bf16[384,768]{1,0:T(8,128)(2,1)S(1)}, u32[]{:S(2)}, u32[]{:S(2)}) %collective-permute-start.14) | collective-permute-done | bytes 589856 | tf_op jit(solution)/shard_map/ppermute | solution.py:472
  166.3 2.8 split_add.3
  177.8 4.8 %collective-permute-done.17 = bf16[96,768]{1,0:T(8,128)(2,1)S(1)} collective-permute-done((bf16[96,768]{1,0:T(8,128)(2,1)S(1)}, bf16[96,768]{1,0:T(8,128)(2,1)S(1)}, u32[]{:S(2)}, u32[]{:S(2)}) %collective-permute-start.17) | collective-permute-done | bytes 147488 | tf_op jit(solution)/shard_map/ppermute | solution.py:472
  193.3 7.1 %collective-permute-done.25 = f32[12,768]{1,0:T(8,128)S(1)} collective-permute-done((f32[12,768]{1,0:T(8,128)S(1)}, f32[12,768]{1,0:T(8,128)S(1)}, u32[]{:S(2)}, u32[]{:S(2)}) %collective-permute-start.25) | collective-permute-done | bytes 36896 | tf_op jit(solution)/shard_map/ppermute | solution.py:472
  200.4 5.3 %collective-permute-done.22 = bf16[96,768]{1,0:T(8,128)(2,1)S(1)} collective-permute-done((bf16[96,768]{1,0:T(8,128)(2,1)S(1)}, bf16[96,768]{1,0:T(8,128)(2,1)S(1)}, u32[]{:S(2)}, u32[]{:S(2)}) %collective-permute-start.22) | collective-permute-done | bytes 147488 | tf_op jit(solution)/shard_map/ppermute | solution.py:472
  210.2 11.4 %collective-permute-done.27 = bf16[96,768]{1,0:T(8,128)(2,1)S(1)} collective-permute-done((bf16[96,768]{1,0:T(8,128)(2,1)S(1)}, bf16[96,768]{1,0:T(8,128)(2,1)S(1)}, u32[]{:S(2)}, u32[]{:S(2)}) %collective-permute-start.27) | collective-permute-done | bytes 147488 | tf_op jit(solution)/shard_map/ppermute | solution.py:472
  230.7 3.5 %collective-permute-done.34 = f32[12,768]{1,0:T(8,128)S(1)} collective-permute-done((f32[12,768]{1,0:T(8,128)S(1)}, f32[12,768]{1,0:T(8,128)S(1)}, u32[]{:S(2)}, u32[]{:S(2)}) %collective-permute-start.34) | collective-permute-done | bytes 36896 | tf_op jit(solution)/shard_map/ppermute | solution.py:472
  242.9 17.1 %collective-permute-done.38 = bf16[96,768]{1,0:T(8,128)(2,1)S(1)} collective-permute-done((bf16[96,768]{1,0:T(8,128)(2,1)S(1)}, bf16[96,768]{1,0:T(8,128)(2,1)S(1)}, u32[]{:S(2)}, u32[]{:S(2)}) %collective-permute-start.38) | collective-permute-done | bytes 147488 | tf_op jit(solution)/shard_map/ppermute | solution.py:472
  266.5 6.4 %collective-permute-done.43 = bf16[192,768]{1,0:T(8,128)(2,1)S(1)} collective-permute-done((bf16[192,768]{1,0:T(8,128)(2,1)S(1)}, bf16[192,768]{1,0:T(8,128)(2,1)S(1)}, u32[]{:S(2)}, u32[]{:S(2)}) %collective-permute-start.43) | collective-permute-done | bytes 294944 | tf_op jit(solution)/shard_map/ppermute | solution.py:472
  284.2 4.4 %emit.3 = (f32[3072,768]{1,0:T(8,128)}, f32[768,3072]{1,0:T(8,128)}) custom-call(s32[3]{0:T(128)S(1)} %pad_add_fusion.4.place_ref, bf16[768,768]{1,0:T(8,128)(2,1)S(1)} %bitcast_select_fusion.2.own_m, bf16[768,768]{1,0:T(8,128)(2,1)S(1)} %copy-done.13, bf16[768,768]{1,0:T(8,128)(2,1)S(1)} %copy-done.15, bf16[768,768]{1,0:T(8,128)(2,1)S(1)} %copy-done.19), custom_call_target="tpu_custom_call" | custom-call | tf_op jit(solution)/shard_map/emit/pallas_call | solution.py:376
  294.2 5.1 %emit.4 = (f32[3072,768]{1,0:T(8,128)}, f32[768,3072]{1,0:T(8,128)}) custom-call(s32[3]{0:T(128)S(1)} %pad_add_fusion.4.place_ref, bf16[768,768]{1,0:T(8,128)(2,1)S(1)} %bitcast_select_fusion.1.own_m, bf16[768,768]{1,0:T(8,128)(2,1)S(1)} %collective-permute-done.41.own_r, ...), custom_call_target="tpu_custom_call", output_to_operand_aliasing={{0}: (5, {}), {1}: (6, {})} | custom-call | tf_op jit(solution)/shard_map/emit/pallas_call | solution.py:376
  299.4 13.2 %collective-permute-done.48 = bf16[256,768]{1,0:T(8,128)(2,1)} collective-permute-done((bf16[256,768]{1,0:T(8,128)(2,1)S(1)}, bf16[256,768]{1,0:T(8,128)(2,1)}, u32[]{:S(2)}, u32[]{:S(2)}) %collective-permute-start.48) | collective-permute-done | bytes 393248 | tf_op jit(solution)/shard_map/ppermute | solution.py:472
  319.8 5.1 %emit.5 = (f32[768,768]{1,0:T(8,128)}, f32[768,768]{1,0:T(8,128)}, f32[768,768]{1,0:T(8,128)}, f32[768,768]{1,0:T(8,128)}) custom-call(s32[3]{0:T(128)S(1)} %pad_add_fusion.4.place_ref, bf16[768,768]{1,0:T(8,128)(2,1)S(1)} %bitcast_select_fusion.own_m, bf16[768,768]{1,0:T(8,128)(2,1)} %collective-permute-done.46.own_r, bf16[768,768]{1,0:T(8,128)(2,1)S(1)} %copy-done.17, ...), custom_call_target="tpu_custom_call" | custom-call | tf_op jit(solution)/shard_map/emit/pallas_call | solution.py:376
  (282 shorter events, 114.7 us)
Async XLA Ops:
  1.8 25.9 %collective-permute-start = (bf16[128,768]{1,0:T(8,128)(2,1)S(1)}, bf16[128,768]{1,0:T(8,128)(2,1)S(1)}, u32[]{:S(2)}, u32[]{:S(2)}) collective-permute-start(bf16[128,768]{1,0:T(8,128)(2,1)S(1)} %get-tuple-element.319), channel_id=1, source_target_pairs={{0,2},{1,3},{2,0},{3,1},{4,6},{5,7},{6,4},{7,5},{8,10},{9,11},{10,... | collective-permute-start | bytes 589832 | tf_op jit(solution)/shard_map/ppermute | solution.py:472
  5.9 24.4 %collective-permute-start.1 = (bf16[128,768]{1,0:T(8,128)(2,1)S(1)}, bf16[128,768]{1,0:T(8,128)(2,1)S(1)}, u32[]{:S(2)}, u32[]{:S(2)}) collective-permute-start(bf16[128,768]{1,0:T(8,128)(2,1)S(1)} %get-tuple-element.318), channel_id=1, source_target_pairs={{0,2},{1,3},{2,0},{3,1},{4,6},{5,7},{6,4},{7,5},{8,10},{9,11},{10,... | collective-permute-start | bytes 589832 | tf_op jit(solution)/shard_map/ppermute | solution.py:472
  7.1 30.9 %collective-permute-start.2 = (bf16[256,768]{1,0:T(8,128)(2,1)S(1)}, bf16[256,768]{1,0:T(8,128)(2,1)S(1)}, u32[]{:S(2)}, u32[]{:S(2)}) collective-permute-start(bf16[256,768]{1,0:T(8,128)(2,1)S(1)} %dynamic-slice_bitcast_fusion.refs_0_.xa_ref), channel_id=1, source_target_pairs={{0,1},{1,0},{2,3},{3,2},{4,5},{5,4},{6,7},{7,6},{8,9},{9,8},{10,11... | collective-permute-start | bytes 1179656 | tf_op jit(solution)/shard_map/ppermute | solution.py:472
  9.0 16.0 %collective-permute-start.5 = (s32[2,256]{1,0:T(2,128)S(1)}, s32[2,256]{1,0:T(2,128)S(1)}, u32[]{:S(2)}, u32[]{:S(2)}) collective-permute-start(s32[2,256]{1,0:T(2,128)S(1)} %copy-done.52), channel_id=1, source_target_pairs={{0,1},{1,0},{2,3},{3,2},{4,5},{5,4},{6,7},{7,6},{8,9},{9,8},{10,11... | collective-permute-start | bytes 6152 | tf_op jit(solution)/shard_map/ppermute | solution.py:472
  38.0 22.0 %collective-permute-start.7 = (bf16[256,768]{1,0:T(8,128)(2,1)S(1)}, bf16[256,768]{1,0:T(8,128)(2,1)S(1)}, u32[]{:S(2)}, u32[]{:S(2)}) collective-permute-start(bf16[256,768]{1,0:T(8,128)(2,1)S(1)} %get-tuple-element.170), channel_id=1, source_target_pairs={{0,2},{1,3},{2,0},{3,1},{4,6},{5,7},{6,4},{7,5},{8,10},{9,11},{10,... | collective-permute-start | bytes 1179656 | tf_op jit(solution)/shard_map/ppermute | solution.py:472
  107.3 18.6 %collective-permute-start.9 = (bf16[768,768]{1,0:T(8,128)(2,1)S(1)}, bf16[768,768]{1,0:T(8,128)(2,1)S(1)}, u32[]{:S(2)}, u32[]{:S(2)}) collective-permute-start(bf16[768,768]{1,0:T(8,128)(2,1)S(1)} %get-tuple-element.191), channel_id=1, source_target_pairs={{0,8},{4,20},{8,0},{12,28},{16,24},{20,4},{24,16},{28,12},{1,9},{5... | collective-permute-start | bytes 3538952 | tf_op jit(solution)/shard_map/ppermute | solution.py:472
  125.9 25.3 %collective-permute-start.11 = (bf16[768,768]{1,0:T(8,128)(2,1)}, bf16[768,768]{1,0:T(8,128)(2,1)}, u32[]{:S(2)}, u32[]{:S(2)}) collective-permute-start(bf16[768,768]{1,0:T(8,128)(2,1)} %get-tuple-element.207), channel_id=1, source_target_pairs={{0,8},{4,20},{8,0},{12,28},{16,24},{20,4},{24,16},{28,12},{1,9},{5... | collective-permute-start | bytes 3538952 | tf_op jit(solution)/shard_map/ppermute | solution.py:472
  127.6 21.8 %collective-permute-start.10 = (bf16[384,768]{1,0:T(8,128)(2,1)}, bf16[384,768]{1,0:T(8,128)(2,1)}, u32[]{:S(2)}, u32[]{:S(2)}) collective-permute-start(bf16[384,768]{1,0:T(8,128)(2,1)} %add_convert_fusion.6), channel_id=1, source_target_pairs={{0,16},{4,12},{8,24},{12,4},{16,0},{20,28},{24,8},{28,20},{1,17},{... | collective-permute-start | bytes 1769480 | tf_op jit(solution)/shard_map/ppermute | solution.py:472
  130.1 21.1 %collective-permute-start.12 = (bf16[256,768]{1,0:T(8,128)(2,1)}, bf16[256,768]{1,0:T(8,128)(2,1)}, u32[]{:S(2)}, u32[]{:S(2)}) collective-permute-start(bf16[256,768]{1,0:T(8,128)(2,1)} %get-tuple-element.317), channel_id=1, source_target_pairs={{0,2},{1,3},{2,0},{3,1},{4,6},{5,7},{6,4},{7,5},{8,10},{9,11},{10,... | collective-permute-start | bytes 1179656 | tf_op jit(solution)/shard_map/ppermute | solution.py:472
  170.2 16.4 %collective-permute-start.19 = (bf16[768,768]{1,0:T(8,128)(2,1)}, bf16[768,768]{1,0:T(8,128)(2,1)S(1)}, u32[]{:S(2)}, u32[]{:S(2)}) collective-permute-start(bf16[768,768]{1,0:T(8,128)(2,1)} %get-tuple-element.238), channel_id=1, source_target_pairs={{0,8},{4,20},{8,0},{12,28},{16,24},{20,4},{24,16},{28,12},{1,9},{5... | collective-permute-start | bytes 3538952 | tf_op jit(solution)/shard_map/ppermute | solution.py:472
  188.9 17.1 %collective-permute-start.24 = (bf16[384,768]{1,0:T(8,128)(2,1)S(1)}, bf16[384,768]{1,0:T(8,128)(2,1)S(1)}, u32[]{:S(2)}, u32[]{:S(2)}) collective-permute-start(bf16[384,768]{1,0:T(8,128)(2,1)S(1)} %add_convert_fusion.2), channel_id=1, source_target_pairs={{0,16},{4,12},{8,24},{12,4},{16,0},{20,28},{24,8},{28,20},{1,17},{... | collective-permute-start | bytes 1769480 | tf_op jit(solution)/shard_map/ppermute | solution.py:472
  190.0 15.9 %collective-permute-start.23 = (bf16[96,768]{1,0:T(8,128)(2,1)S(1)}, bf16[96,768]{1,0:T(8,128)(2,1)S(1)}, u32[]{:S(2)}, u32[]{:S(2)}) collective-permute-start(bf16[96,768]{1,0:T(8,128)(2,1)S(1)} %add_convert_fusion.10), channel_id=1, source_target_pairs={{0,2},{1,3},{2,0},{3,1},{4,6},{5,7},{6,4},{7,5},{8,10},{9,11},{10,... | collective-permute-start | bytes 442376 | tf_op jit(solution)/shard_map/ppermute | solution.py:472
  206.2 15.5 %collective-permute-start.26 = (bf16[192,768]{1,0:T(8,128)(2,1)S(1)}, bf16[192,768]{1,0:T(8,128)(2,1)S(1)}, u32[]{:S(2)}, u32[]{:S(2)}) collective-permute-start(bf16[192,768]{1,0:T(8,128)(2,1)S(1)} %bitcast_select_fusion.8), channel_id=1, source_target_pairs={{0,1},{1,0},{2,3},{3,2},{4,5},{5,4},{6,7},{7,6},{8,9},{9,8},{10,11... | collective-permute-start | bytes 884744 | tf_op jit(solution)/shard_map/ppermute | solution.py:472
  206.3 17.5 %collective-permute-start.28 = (bf16[192,768]{1,0:T(8,128)(2,1)S(1)}, bf16[192,768]{1,0:T(8,128)(2,1)S(1)}, u32[]{:S(2)}, u32[]{:S(2)}) collective-permute-start(bf16[192,768]{1,0:T(8,128)(2,1)S(1)} %get-tuple-element.322), channel_id=1, source_target_pairs={{0,1},{1,0},{2,3},{3,2},{4,5},{5,4},{6,7},{7,6},{8,9},{9,8},{10,11... | collective-permute-start | bytes 884744 | tf_op jit(solution)/shard_map/ppermute | solution.py:472
  237.0 23.8 %collective-permute-start.35 = (bf16[768,768]{1,0:T(8,128)(2,1)S(1)}, bf16[768,768]{1,0:T(8,128)(2,1)S(1)}, u32[]{:S(2)}, u32[]{:S(2)}) collective-permute-start(bf16[768,768]{1,0:T(8,128)(2,1)S(1)} %bitcast_select_fusion.2.own_m), channel_id=1, source_target_pairs={{0,8},{4,20},{8,0},{12,28},{16,24},{20,4},{24,16},{28,12},{1,9},{5... | collective-permute-start | bytes 3538952 | tf_op jit(solution)/shard_map/ppermute | solution.py:472
  237.6 23.1 %collective-permute-start.36 = (bf16[768,768]{1,0:T(8,128)(2,1)S(1)}, bf16[768,768]{1,0:T(8,128)(2,1)S(1)}, u32[]{:S(2)}, u32[]{:S(2)}) collective-permute-start(bf16[768,768]{1,0:T(8,128)(2,1)S(1)} %bitcast_select_fusion.2.own_m), channel_id=1, source_target_pairs={{0,4},{4,0},{8,12},{12,8},{16,20},{20,16},{24,28},{28,24},{1,5},{5... | collective-permute-start | bytes 3538952 | tf_op jit(solution)/shard_map/ppermute | solution.py:472
  238.0 22.8 %collective-permute-start.39 = (bf16[512,768]{1,0:T(8,128)(2,1)S(1)}, bf16[512,768]{1,0:T(8,128)(2,1)S(1)}, u32[]{:S(2)}, u32[]{:S(2)}) collective-permute-start(bf16[512,768]{1,0:T(8,128)(2,1)S(1)} %copy-done.39), channel_id=1, source_target_pairs={{0,1},{1,0},{2,3},{3,2},{4,5},{5,4},{6,7},{7,6},{8,9},{9,8},{10,11... | collective-permute-start | bytes 2359304 | tf_op jit(solution)/shard_map/ppermute | solution.py:472
  239.7 20.4 %collective-permute-start.37 = (bf16[384,768]{1,0:T(8,128)(2,1)S(1)}, bf16[384,768]{1,0:T(8,128)(2,1)S(1)}, u32[]{:S(2)}, u32[]{:S(2)}) collective-permute-start(bf16[384,768]{1,0:T(8,128)(2,1)S(1)} %bitcast_select_fusion.4), channel_id=1, source_target_pairs={{0,16},{4,12},{8,24},{12,4},{16,0},{20,28},{24,8},{28,20},{1,17},{... | collective-permute-start | bytes 1769480 | tf_op jit(solution)/shard_map/ppermute | solution.py:472
  240.8 19.2 %collective-permute-start.38 = (bf16[96,768]{1,0:T(8,128)(2,1)S(1)}, bf16[96,768]{1,0:T(8,128)(2,1)S(1)}, u32[]{:S(2)}, u32[]{:S(2)}) collective-permute-start(bf16[96,768]{1,0:T(8,128)(2,1)S(1)} %add_convert_fusion.7), channel_id=1, source_target_pairs={{0,2},{1,3},{2,0},{3,1},{4,6},{5,7},{6,4},{7,5},{8,10},{9,11},{10,... | collective-permute-start | bytes 442376 | tf_op jit(solution)/shard_map/ppermute | solution.py:472
  260.8 16.3 %collective-permute-start.41 = (bf16[768,768]{1,0:T(8,128)(2,1)S(1)}, bf16[768,768]{1,0:T(8,128)(2,1)S(1)}, u32[]{:S(2)}, u32[]{:S(2)}) collective-permute-start(bf16[768,768]{1,0:T(8,128)(2,1)S(1)} %bitcast_select_fusion.1.own_m), channel_id=1, source_target_pairs={{0,8},{4,20},{8,0},{12,28},{16,24},{20,4},{24,16},{28,12},{1,9},{5... | collective-permute-start | bytes 3538952 | tf_op jit(solution)/shard_map/ppermute | solution.py:472
  262.3 14.8 %collective-permute-start.42 = (bf16[768,768]{1,0:T(8,128)(2,1)S(1)}, bf16[768,768]{1,0:T(8,128)(2,1)S(1)}, u32[]{:S(2)}, u32[]{:S(2)}) collective-permute-start(bf16[768,768]{1,0:T(8,128)(2,1)S(1)} %bitcast_select_fusion.1.own_m), channel_id=1, source_target_pairs={{0,4},{4,0},{8,12},{12,8},{16,20},{20,16},{24,28},{28,24},{1,5},{5... | collective-permute-start | bytes 3538952 | tf_op jit(solution)/shard_map/ppermute | solution.py:472
  290.2 22.3 %collective-permute-start.46 = (bf16[768,768]{1,0:T(8,128)(2,1)S(1)}, bf16[768,768]{1,0:T(8,128)(2,1)}, u32[]{:S(2)}, u32[]{:S(2)}) collective-permute-start(bf16[768,768]{1,0:T(8,128)(2,1)S(1)} %bitcast_select_fusion.own_m), channel_id=1, source_target_pairs={{0,8},{4,20},{8,0},{12,28},{16,24},{20,4},{24,16},{28,12},{1,9},{5... | collective-permute-start | bytes 3538952 | tf_op jit(solution)/shard_map/ppermute | solution.py:472
  291.4 21.2 %collective-permute-start.47 = (bf16[768,768]{1,0:T(8,128)(2,1)S(1)}, bf16[768,768]{1,0:T(8,128)(2,1)S(1)}, u32[]{:S(2)}, u32[]{:S(2)}) collective-permute-start(bf16[768,768]{1,0:T(8,128)(2,1)S(1)} %bitcast_select_fusion.own_m), channel_id=1, source_target_pairs={{0,4},{4,0},{8,12},{12,8},{16,20},{20,16},{24,28},{28,24},{1,5},{5... | collective-permute-start | bytes 3538952 | tf_op jit(solution)/shard_map/ppermute | solution.py:472
  291.6 20.9 %collective-permute-start.48 = (bf16[256,768]{1,0:T(8,128)(2,1)S(1)}, bf16[256,768]{1,0:T(8,128)(2,1)}, u32[]{:S(2)}, u32[]{:S(2)}) collective-permute-start(bf16[256,768]{1,0:T(8,128)(2,1)S(1)} %slice.103), channel_id=1, source_target_pairs={{0,2},{1,3},{2,0},{3,1},{4,6},{5,7},{6,4},{7,5},{8,10},{9,11},{10,... | collective-permute-start | bytes 1179656 | tf_op jit(solution)/shard_map/ppermute | solution.py:472
  (79 other events, 606.2 us)

commit v3 on v2

v3 whole, which is shorter than its diff:
```python
from functools import partial

import jax
import jax.numpy as jnp
from jax import lax
from jax.experimental import pallas as pl
from jax.experimental.pallas import tpu as pltpu
from jax.sharding import PartitionSpec as P

f32=jnp.float32; bf16=jnp.bfloat16
norm_eps=1e-12
NSEG=6
HD=64
def dot(a,b): return jnp.dot(a,b,preferred_element_type=f32)
def dot_nt(a,b): return lax.dot_general(a,b,(((1,),(1,)),((),())),preferred_element_type=f32)
def dot_tn(a,b): return lax.dot_general(a,b,(((0,),(0,)),((),())),preferred_element_type=f32)

def gelu_pair(x):
    t = 1.0 / (1.0 + (0.3275911 * 0.7071067811865476) * jnp.abs(x))
    e = jnp.exp(-0.5 * x * x)
    half = (0.5*0.254829592) + t*((0.5*-0.284496736) + t*((0.5*1.421413741) + t*((0.5*-1.453152027) + t*(0.5*1.061405429))))
    tail = half * t * e
    cdf = jnp.where(x > 0, 1.0 - tail, tail)
    return x * cdf, cdf + x * e * 0.3989422804014327

def in_hbm(*arrays):
    return tuple(pltpu.with_memory_space_constraint(a, pltpu.HBM) for a in arrays)

def wide(rows):
    return jnp.concatenate([rows[i:i+1,:] for i in range(rows.shape[0])], axis=1)

VM = pl.BlockSpec(memory_space=pltpu.VMEM)
SM = pl.BlockSpec(memory_space=pltpu.SMEM)
ANY = pl.BlockSpec(memory_space=pl.ANY)
FAR = pl.BlockSpec(memory_space=pltpu.HBM)
MIB = 1024 * 1024


def call(kernel, deps, args, in_specs, out_specs, out_shape, scratch=(), aliases=None, vmem=16, grid=(), name=None):
    n, m = len(deps), len(args)

    def body(*refs):
        kernel(*refs[n : n + m], *refs[n + m + 1 :])

    token, *outs = pl.pallas_call(
        body,
        grid=grid,
        in_specs=[ANY] * n + list(in_specs),
        out_specs=[FAR] + list(out_specs),
        out_shape=[pltpu.HBM((8, 128), f32)] + list(out_shape),
        scratch_shapes=list(scratch),
        input_output_aliases={n + k: 1 + v for k, v in (aliases or {}).items()},
        compiler_params=pltpu.CompilerParams(vmem_limit_bytes=int(vmem * MIB)),
        name=name,
    )(*deps, *args)
    return in_hbm(token)[0], outs


def same_segment(left, right):
    lab = lax.broadcasted_iota(jnp.int32, (8, 1), 0).astype(f32)
    hot = lambda s: (lab == s).astype(f32).astype(bf16)
    return (dot_tn(hot(left), hot(right)) - 1.0) * 1e30

OUT_B, G1, B1, DOWN_B, G2, B2, UP_B = range(7)
RB = 128

def rows_norm(r):
    m = jnp.mean(r, axis=-1, keepdims=True)
    c = r - m
    inv = lax.rsqrt(jnp.mean(c*c, axis=-1, keepdims=True) + norm_eps)
    return c * inv, inv

def norm_back(g, xh, inv):
    return inv * (g - jnp.mean(g, axis=-1, keepdims=True) - xh * jnp.mean(g*xh, axis=-1, keepdims=True))

def col_sum(v): return jnp.sum(v, axis=0, keepdims=True)

def mid_kernel(order_ref, att_ref, xa_ref, xb_ref, xc_ref, cota_hbm, cotb_hbm, itot_hbm, seg_ref, ob_ref, g1_ref, b1_ref, db_ref, g2_ref, b2_ref, ub_ref, wo_hbm, wu_hbm, wd_hbm,
               segsum_ref, small_ref, dres_ref, dn_ref, dt_ref, outo_hbm, outx_hbm, gout_hbm, send_one, send_two, keep_one, keep_two,
               wo, wu, wd, hid, hl, xh1, rs1, act, gp, feed, dfl, dhid, stage, cota_ref, cotb_ref, itot_ref, out_ref, gout_ref,
               wsem, gsem, csem):
    R, W = att_ref.shape
    nc = wu.shape[0]
    def rows_of(refs, i):
        for ref in refs:
            h = ref.shape[0] // RB
            if i < h:
                return ref[pl.ds(i*RB,RB),:]
            i -= h
    def copies(k):
        c = order_ref[k]
        return (pltpu.make_async_copy(wu_hbm.at[:, pl.ds(c*W, W)], wu.at[k], wsem.at[1+k]),
                pltpu.make_async_copy(wd_hbm.at[pl.ds(c*W, W), :], wd.at[k], wsem.at[1+nc+k]))
    cwo = pltpu.make_async_copy(wo_hbm, wo, wsem.at[0]); cwo.start()
    for k in range(nc):
        for cp in copies(k): cp.start()
    late = [pltpu.make_async_copy(src, dst, csem.at[i]) for i, (src, dst) in enumerate(
        ((cota_hbm, cota_ref), (cotb_hbm, cotb_ref), (itot_hbm, itot_ref), (out_ref.at[pl.ds(0, R//2), :], outo_hbm), (gout_ref, gout_hbm),
         (out_ref.at[pl.ds(R//2, R//2), :], outx_hbm)))]
    for c in late[:3]: c.start()
    NB = R // RB
    vecs = (ob_ref, g1_ref, b1_ref, db_ref, g2_ref, b2_ref)
    row = lambda i: wide(vecs[i][...])
    lanes = W // 128
    cwo.wait()
    feed[...] = dot(att_ref[...].astype(bf16), wo[...])
    for i in range(NB):
        s = pl.ds(i*RB, RB)
        r = rows_of((xa_ref, xb_ref, xc_ref), i).astype(f32) + feed[s, :] + row(OUT_B)
        xh, inv = rows_norm(r)
        xh1[s,:] = xh
        rs1[s,:] = inv
        h = xh * row(G1) + row(B1)
        hid[s,:] = h
        hl[s,:] = h.astype(bf16)
    for k in range(nc):
        for cp in copies(k): cp.wait()
        ub = wide(ub_ref[pl.ds(order_ref[k]*lanes, lanes), :])
        for j in range(W//256):
            cs = slice(j*256, (j+1)*256)
            pre = dot(hl[...], wu[k, :, cs]) + ub[:, cs]
            a_, g_ = gelu_pair(pre)
            act[k, :, cs] = a_.astype(bf16)
            gp[k, :, cs] = g_.astype(gp.dtype)
        part = dot(act[k], wd[k])
        if k == 0: feed[...] = part
        else: feed[...] += part
    late[0].wait()
    late[1].wait()
    lab = (lax.broadcasted_iota(jnp.int32, (8, 1), 0) + 1).astype(f32)
    count = jnp.zeros((8, 1), f32)
    zero = jnp.zeros((1,W),f32)
    segsum = jnp.zeros((8, W), f32)
    sg = ss = sdb = zero
    for i in range(NB):
        s = pl.ds(i*RB, RB)
        xh, inv = rows_norm(hid[s,:] + feed[s,:] + row(DOWN_B))
        o = xh * row(G2) + row(B2)
        oh = o.astype(bf16)
        out_ref[s,:] = oh
        ol = (o - oh.astype(f32)).astype(bf16)
        hot = (lab == seg_ref[0:1, i*RB:(i+1)*RB]).astype(f32)
        count = count + jnp.sum(hot, axis=1, keepdims=True)
        hot = hot.astype(bf16)
        segsum = segsum + dot(hot, oh) + dot(hot, ol)
        u = rows_of((cota_ref, cotb_ref), i).astype(f32)
        sg = sg + col_sum(u*xh)
        ss = ss + col_sum(u)
        d = norm_back(u * row(G2), xh, inv)
        dhid[s,:] = d
        dl = d.astype(bf16)
        dfl[s,:] = dl
        sdb = sdb + col_sum(dl.astype(f32))
    late[3].start()
    late[5].start()
    segsum_ref[0:8, :] = segsum
    segsum_ref[8:16, :] = jnp.broadcast_to(count, (8, W))
    small_ref[pl.ds(DOWN_B,1), :] = sdb
    small_ref[pl.ds(G2,1), :] = sg
    small_ref[pl.ds(B2,1), :] = ss
    def push(slot, k, kind):
        dst = (send_one, send_two, keep_one, keep_two)[k]
        return pltpu.make_async_copy(stage.at[slot], dst.at[pl.ds(kind*W, W), :], gsem.at[slot])
    for k in range(nc):
        stage[k] = dot_tn(act[k], dfl[...]).astype(bf16)
        push(k, k, 0).start()
        da = dot_nt(dfl[...], wd[k])
        dp = (da * gp[k].astype(f32)).astype(bf16)
        act[k] = dp
        small_ref[pl.ds(UP_B + order_ref[k],1), :] = col_sum(dp.astype(f32))
        stage[nc+k] = dot_tn(hl[...], dp).astype(bf16)
        push(nc+k, k, 1).start()
        dhid[...] += dot_nt(dp, wu[k])
    sg = ss = sdb = zero
    for i in range(NB):
        s = pl.ds(i*RB, RB)
        dh = dhid[s,:]
        xh = xh1[s,:]
        sg = sg + col_sum(dh*xh)
        ss = ss + col_sum(dh)
        d = norm_back(dh * row(G1), xh, rs1[s,:])
        dres_ref[s,:] = d
        dl = d.astype(bf16)
        dfl[s,:] = dl
        sdb = sdb + col_sum(dl.astype(f32))
    small_ref[pl.ds(OUT_B,1), :] = sdb
    small_ref[pl.ds(G1,1), :] = sg
    small_ref[pl.ds(B1,1), :] = ss
    gout_ref[...] = dot_tn(att_ref[...].astype(bf16), dfl[...]).astype(bf16)
    late[4].start()
    late[2].wait()
    l0 = lax.broadcasted_iota(jnp.int32, (128,128), 0) // HD
    l1 = lax.broadcasted_iota(jnp.int32, (128,128), 1) // HD
    same = (l0 == l1).astype(f32).astype(bf16)
    feed[...] = dot_nt(dfl[...], wo[...])
    for i in range(NB):
        s = pl.ds(i*RB, RB)
        da = feed[s,:]
        it = itot_ref[s,:]
        dn_ref[s,:] = (da * it).astype(bf16)
        p = da * att_ref[s,:]
        ph = p.astype(bf16)
        plow = (p - ph.astype(f32)).astype(bf16)
        for j in range(W//128):
            cs = slice(j*128,(j+1)*128)
            dt_ref[s, cs] = -(dot(ph[:,cs], same) + dot(plow[:,cs], same)) * it[:,cs]
    for c in late[3:]: c.wait()
    for k in range(nc):
        push(k, k, 0).wait()
        push(nc+k, k, 1).wait()

def mid(order, att, x, cot, itot, seg_row, vecs, wo, wu, wd):
    R, W = att.shape
    nc = wu.shape[1] // W
    any_ = pl.BlockSpec(memory_space=pltpu.HBM)
    vm = pl.BlockSpec(memory_space=pltpu.VMEM)
    sm = pl.BlockSpec(memory_space=pltpu.SMEM)
    sd = pltpu.HBM
    return pl.pallas_call(
        mid_kernel,
        in_specs=[sm]+[vm]*4+[any_]*3+[vm]*8+[any_]*3,
        out_specs=[vm]*5+[any_]*7,
        out_shape=[sd((16,W),f32), sd((UP_B+nc+6,W),f32), sd((R,W),f32), sd((R,W),bf16), sd((R,W),f32), sd((R//2,W),bf16), sd((R//2,W),bf16),
                   sd((W,W),bf16)]+[sd((2*W,W),bf16)]*4,
        scratch_shapes=[pltpu.VMEM((W,W),bf16), pltpu.VMEM((nc,W,W),bf16), pltpu.VMEM((nc,W,W),bf16),
                        pltpu.VMEM((R,W),f32), pltpu.VMEM((R,W),bf16), pltpu.VMEM((R,W),f32), pltpu.VMEM((R,1),f32),
                        pltpu.VMEM((nc,R,W),bf16), pltpu.VMEM((nc,R,W),f32), pltpu.VMEM((R,W),f32), pltpu.VMEM((R,W),bf16), pltpu.VMEM((R,W),f32),
                        pltpu.VMEM((2*nc,W,W),bf16), pltpu.VMEM((R//2,W),bf16), pltpu.VMEM((R//2,W),bf16), pltpu.VMEM((R,W),f32),
                        pltpu.VMEM((R,W),bf16), pltpu.VMEM((W,W),bf16),
                        pltpu.SemaphoreType.DMA((1+2*nc,)), pltpu.SemaphoreType.DMA((2*nc,)), pltpu.SemaphoreType.DMA((6,))],
        compiler_params=pltpu.CompilerParams(vmem_limit_bytes=60*1024*1024),
        name="mid",
    )(order, *in_hbm(att, *x, *cot, itot, seg_row, *vecs, wo, wu, wd))

GW = 256
ID_ROWS = 16
def head_pair_lanes():
    return lax.broadcasted_iota(jnp.int32, (1,128), 1) < HD

def gather_rows(refs, dst, sem):
    at, copies = 0, []
    for i, ref in enumerate(refs):
        n = ref.shape[0] // 128 * 128
        copies.append(pltpu.make_async_copy(ref.at[pl.ds(0, n), :], dst.at[pl.ds(at, n), :], sem.at[i]))
        at += n
    return copies

def gather_ids(refs, dst, sem):
    tails = [ref for ref in refs if ref.shape[0] % 128]
    return [
        pltpu.make_async_copy(ref.at[pl.ds(ref.shape[0] - ID_ROWS, ID_ROWS), :], dst.at[i], sem.at[i])
        for i, ref in enumerate(tails)
    ]

def ids_of(ids, width):
    return jnp.concatenate([ids[i, 0:1, 0:width].astype(f32) for i in range(ids.shape[0])], axis=1)

def attend(q, k, v, bias, first):
    nums, tots = [], []
    for p in range(q.shape[1]//128):
        cs = slice(p*128,(p+1)*128)
        qp, kp, vp = q[:,cs], k[:,cs], v[:,cs]
        one = jnp.ones_like(vp); zero=jnp.zeros_like(qp)
        res = []
        for h in range(2):
            mine = first if h==0 else jnp.logical_not(first)
            s = dot_nt(jnp.where(mine, qp, zero), kp)
            e = jnp.exp(s + bias[...]).astype(bf16)
            res.append(dot(e, jnp.where(mine, vp, one)))
        nums.append(jnp.where(first, res[0], res[1]))
        tots.append(jnp.where(first, res[1], res[0]))
    return nums, tots

def attn_some_kernel(n_parts, *refs):
    parts = refs[:n_parts]
    (wq_ref, wk_ref, wv_ref, qb_ref, vb_ref,
     q_ref, k_ref, v_ref, num_ref, tot_ref, bias, x_ref, ids, sem, isem) = refs[n_parts:]
    R, N = q_ref.shape[0], k_ref.shape[0]
    @pl.when(pl.program_id(0) == 0)
    def _():
        marks = gather_ids(parts, ids, isem)
        copies = gather_rows(parts, x_ref, sem)
        for c in marks + copies: c.start()
        for c in marks: c.wait()
        row = ids_of(ids, N // ids.shape[0])
        bias[...] = same_segment(row[:, 0:R], row)
        for c in copies: c.wait()
    lanes = GW // 128
    at = pl.ds(pl.program_id(0)*lanes, lanes)
    qb, vb = wide(qb_ref[at, :]), wide(vb_ref[at, :])
    q = (0.125*(dot(x_ref[0:R,:], wq_ref[...]) + qb)).astype(bf16)
    k = dot(x_ref[...], wk_ref[...]).astype(bf16)
    v = (dot(x_ref[...], wv_ref[...]) + vb).astype(bf16)
    q_ref[...] = q; k_ref[...] = k; v_ref[...] = v
    nums, tots = attend(q, k, v, bias, head_pair_lanes())
    for p in range(lanes):
        num_ref[:, p*128:(p+1)*128] = nums[p]
        tot_ref[:, p*128:(p+1)*128] = tots[p]

def attn_some(parts, wq, wk, wv, qb, vb, R):
    W = wq.shape[0]
    N = sum(p.shape[0] // 128 * 128 for p in parts)
    n_ids = sum(1 for p in parts if p.shape[0] % 128)
    whole = N // n_ids * (n_ids + 1)
    sd = pltpu.HBM
    full = lambda a: pl.BlockSpec(a.shape, lambda j: (0,0))
    col = lambda r: pl.BlockSpec((r,GW), lambda j: (0,j))
    return pl.pallas_call(
        partial(attn_some_kernel, len(parts)), grid=(W//GW,),
        in_specs=[pl.BlockSpec(memory_space=pltpu.HBM)]*len(parts)+[col(W), col(W), col(W), full(qb), full(vb)],
        out_specs=[col(R), col(N), col(N), col(R), col(R)],
        out_shape=[sd((R,W),bf16), sd((whole,W),bf16), sd((whole,W),bf16), sd((R,W),f32), sd((R,W),f32)],
        scratch_shapes=[pltpu.VMEM((R,N),f32), pltpu.VMEM((N,W),bf16), pltpu.VMEM((n_ids,ID_ROWS,W),bf16),
                        pltpu.SemaphoreType.DMA((len(parts),)), pltpu.SemaphoreType.DMA((n_ids,))],
        compiler_params=pltpu.CompilerParams(vmem_limit_bytes=24*1024*1024, dimension_semantics=("arbitrary",)),
        name="attn_some",
    )(*in_hbm(*parts, wq, wk, wv, qb, vb))

def attn_last_kernel(n_parts, n_all, *refs):
    parts = refs[n_all-n_parts:n_all]
    (q_ref, wk_ref, wv_ref, vb_ref, num_ref, tot_ref, _, _,
     k_ref, v_ref, att_ref, itot_ref, sk_ref, bias, x_ref, ids, sem, isem) = refs[n_all:]
    R, N = q_ref.shape[0], k_ref.shape[0]
    whole = sk_ref.shape[1]
    @pl.when(pl.program_id(0) == 0)
    def _():
        marks = gather_ids(refs[:n_all], ids, isem)
        copies = gather_rows(parts, x_ref, sem)
        for c in marks + copies: c.start()
        for c in marks: c.wait()
        row = ids_of(ids, N)
        sk_ref[...] = jnp.broadcast_to(row, sk_ref.shape)
        bias[...] = same_segment(row[:, 0:R], row[:, whole-N:whole])
        for c in copies: c.wait()
    lanes = GW // 128
    vb = wide(vb_ref[pl.ds(pl.program_id(0)*lanes, lanes), :])
    k = dot(x_ref[...], wk_ref[...]).astype(bf16)
    v = (dot(x_ref[...], wv_ref[...]) + vb).astype(bf16)
    k_ref[...] = k; v_ref[...] = v
    nums, tots = attend(q_ref[...], k, v, bias, head_pair_lanes())
    for p in range(lanes):
        cs = slice(p*128, (p+1)*128)
        it = 1.0 / pltpu.roll(tots[p] + tot_ref[:, cs], HD, 1)
        att_ref[:,cs] = (nums[p] + num_ref[:, cs]) * it
        itot_ref[:,cs] = it

def attn_last(here, parts, q, wk, wv, vb, num, tot, k, v):
    R, W = q.shape
    N = sum(p.shape[0] // 128 * 128 for p in parts)
    whole = k.shape[0]
    sd = pltpu.HBM
    every = [*here, *parts]
    n = len(every)
    n_ids = sum(1 for p in every if p.shape[0] % 128)
    any_ = pl.BlockSpec(memory_space=pltpu.HBM)
    full = lambda a: pl.BlockSpec(a.shape, lambda j: (0,0))
    col = lambda r: pl.BlockSpec((r,GW), lambda j: (0,j))
    tail = pl.BlockSpec((N,GW), lambda j: (whole//N-1,j))
    return pl.pallas_call(
        partial(attn_last_kernel, len(parts), n), grid=(W//GW,),
        in_specs=[any_]*n+[col(R), col(W), col(W), full(vb), col(R), col(R), any_, any_],
        out_specs=[tail, tail, col(R), col(R), pl.BlockSpec((8,whole), lambda j: (0,0))],
        out_shape=[sd((whole,W),bf16), sd((whole,W),bf16), sd((R,W),f32), sd((R,W),f32), sd((8,whole),f32)],
        input_output_aliases={n+6: 0, n+7: 1},
        scratch_shapes=[pltpu.VMEM((R,N),f32), pltpu.VMEM((N,W),bf16), pltpu.VMEM((n_ids,ID_ROWS,W),bf16),
                        pltpu.SemaphoreType.DMA((n,)), pltpu.SemaphoreType.DMA((n_ids,))],
        compiler_params=pltpu.CompilerParams(vmem_limit_bytes=20*1024*1024, dimension_semantics=("arbitrary",)),
        name="attn_last",
    )(*in_hbm(*every, q, wk, wv, vb, num, tot), k, v)

def attn_bwd_kernel(q_ref, k_ref, v_ref, dn_ref, dt_ref, sk_ref, dq_ref, dk_ref, dv_ref, bias):
    @pl.when(pl.program_id(0) == 0)
    def _():
        row = sk_ref[0:1, :]
        bias[...] = same_segment(row, row[:, 0:q_ref.shape[0]])
    first = head_pair_lanes()
    lane = lax.broadcasted_iota(jnp.int32, (1,128), 1)
    for p in range(q_ref.shape[1]//128):
        cs = slice(p*128,(p+1)*128)
        qp, kp, vp, dnp = q_ref[:,cs], k_ref[:,cs], v_ref[:,cs], dn_ref[:,cs]
        dtr = pltpu.roll(dt_ref[:,cs], HD, 1)
        hi = dtr.astype(bf16)
        rest = dtr - hi.astype(f32)
        mid_ = rest.astype(bf16)
        low = (rest - mid_.astype(f32)).astype(bf16)
        res=[]
        for h in range(2):
            mine = first if h==0 else jnp.logical_not(first)
            o = HD if h==0 else 0
            ex = jnp.where(lane==o, hi, jnp.where(lane==o+1, mid_, jnp.where(lane==o+2, low, jnp.zeros_like(hi))))
            dne = jnp.where(mine, dnp, ex)
            ve = jnp.where(mine, vp, jnp.where((lane>=o)&(lane<o+3), jnp.ones_like(vp), jnp.zeros_like(vp)))
            s = dot_nt(jnp.where(mine, kp, jnp.zeros_like(kp)), qp)
            e = jnp.exp(s + bias[...])
            pr = dot_nt(ve, dne)
            ds = (e * pr).astype(bf16)
            dv = dot(e.astype(bf16), dnp)
            dk = dot(ds, qp)
            dq = dot_tn(ds, kp)
            res.append((dq,dk,dv))
        dq_ref[:,cs] = (jnp.where(first, res[0][0], res[1][0]).astype(bf16).astype(f32)*0.125).astype(bf16)
        dk_ref[:,cs] = jnp.where(first, res[0][1], res[1][1]).astype(bf16)
        dv_ref[:,cs] = jnp.where(first, res[0][2], res[1][2]).astype(bf16)

def attn_bwd(deps,q,k,v,dn,dt,sk,start,count):
    R,W=q.shape; N=k.shape[0]
    sd = pltpu.HBM
    GB=128
    col = lambda r: pl.BlockSpec((r,GB), lambda j: (0,j+start))
    out = lambda r: pl.BlockSpec((r,GB), lambda j: (0,j))
    return call(
        attn_bwd_kernel, deps, in_hbm(q,k,v,dn,dt,sk),
        [col(R), col(N), col(N), col(R), col(R), pl.BlockSpec(sk.shape, lambda j: (0,0))],
        [out(R), out(N), out(N)],
        [sd((R,GB*count),bf16), sd((N,GB*count),bf16), sd((N,GB*count),bf16)],
        [pltpu.VMEM((N,R),f32)], grid=(count,), vmem=16, name="attn_bwd",
    )

def spans(refs):
    at, out = 0, []
    for r in refs:
        out.append(slice(at, at + r.shape[1]))
        at += r.shape[1]
    return out

def token_grad_kernel(n_grads, *refs):
    grads, (wq_ref, wk_ref, wv_ref, dres_ref, own_ref, away_ref, pa_ref, pb_ref) = refs[:n_grads], refs[n_grads:]
    dq, dk, dv = grads[0::3], grads[1::3], grads[2::3]
    R = dq[0].shape[0]
    parts = spans(dq)
    def back(refs, w_ref, rows):
        total = dot_nt(refs[0][rows,:], w_ref[:,parts[0]])
        for r, cs in zip(refs[1:], parts[1:]): total = total + dot_nt(r[rows,:], w_ref[:,cs])
        return total
    top, rest = slice(0,R), slice(R,2*R)
    pair = (back(dk, wk_ref, rest) + back(dv, wv_ref, rest)).astype(bf16)
    pa_ref[...] = pair[:R//2]
    pb_ref[...] = pair[R//2:]
    mine = (dres_ref[...] + back(dq, wq_ref, top) + back(dk, wk_ref, top)
            + back(dv, wv_ref, top))
    own_ref[...] = mine[:R//2]
    away_ref[...] = mine[R//2:]

def token_grad(deps, grads, wq, wk, wv, dres):
    R, W = dres.shape
    sd = pltpu.HBM
    return call(
        partial(token_grad_kernel, len(grads)), deps, in_hbm(*grads, wq, wk, wv, dres),
        [VM]*(len(grads)+4), [VM]*4, [sd((R//2,W),f32)]*2+[sd((R//2,W),bf16)]*2, vmem=24, name="token_grad",
    )

def weight_grad_kernel(n_parts, n_grads, *refs):
    tokens, grads = refs[:n_parts], refs[n_parts:n_parts+n_grads]
    dq, dk, dv = grads[0::3], grads[1::3], grads[2::3]
    (bit_ref, gout_ref, bsum_ref, gsend_hbm, gkeep_hbm, stage, x_ref, sem, xsem) = refs[n_parts+n_grads:]
    copies = gather_rows(tokens, x_ref, xsem)
    for c in copies: c.start()
    W = x_ref.shape[1]
    bit = bit_ref[0]
    parts = spans(dq)
    def push(i, start):
        src = gout_ref if i == 3 else stage.at[i]
        def go(dst):
            cp = pltpu.make_async_copy(src, dst.at[pl.ds((i%2)*W, W), :], sem.at[i])
            cp.start() if start else cp.wait()
        @pl.when(bit == i//2)
        def _(): go(gkeep_hbm)
        @pl.when(bit != i//2)
        def _(): go(gsend_hbm)
    push(3, True)
    for c in copies: c.wait()
    for i, refs in ((2,dv), (1,dk), (0,dq)):
        for ref, cs in zip(refs, parts):
            n = ref.shape[0]
            stage[i, :, cs] = dot_tn(x_ref[0:n,:], ref[...]).astype(bf16)
        push(i, True)
    for ref, cs in zip(dq, parts): bsum_ref[0:1,cs] = col_sum(ref[...].astype(f32))
    for ref, cs in zip(dv, parts): bsum_ref[1:2,cs] = col_sum(ref[...].astype(f32))
    for i in range(4): push(i, False)

def weight_grad(deps, bits, grads, tokens, gout):
    R = grads[0].shape[0]
    W = gout.shape[0]
    sd = pltpu.HBM
    return call(
        partial(weight_grad_kernel, len(tokens), len(grads)), deps, (*in_hbm(*tokens, *grads), bits, *in_hbm(gout)),
        [FAR]*len(tokens)+[VM]*len(grads)+[SM, VM], [VM,FAR,FAR],
        [sd((2,W),f32), sd((2*W,W),bf16), sd((2*W,W),bf16)],
        [pltpu.VMEM((3,W,W),bf16), pltpu.VMEM((2*R,W),bf16), pltpu.SemaphoreType.DMA((4,)), pltpu.SemaphoreType.DMA((len(tokens),))],
        vmem=22, name="weight_grad",
    )

def emit_kernel(up_from, n_prev, second, bits_ref, *refs):
    n_in = len(second) * 2
    pieces_in, outs, (stage, sem) = refs[:n_in], refs[n_in+n_prev:-2], refs[-2:]
    n, W = pieces_in[0].shape
    bit, mine, theirs = bits_ref[0], bits_ref[1], bits_ref[2]
    pieces = []
    for i, s in enumerate(second):
        pieces.append((bit, 1 - mine if s else mine, pieces_in[2*i]))
        pieces.append((1 - bit, 1 - theirs if s else theirs, pieces_in[2*i+1]))
    def send(i, start):
        half, block, ref = pieces[i]
        for b in range(2):
            for h in range(2):
                if up_from is None: dst = outs[2*h + b]
                elif b == 0: dst = outs[0].at[pl.ds((2*h + up_from)*W, W), :]
                else: dst = outs[1].at[:, pl.ds((2*h + up_from)*W, W)]
                @pl.when((half == h) & (block == b))
                def _():
                    cp = pltpu.make_async_copy(stage.at[i], dst, sem.at[i])
                    cp.start() if start else cp.wait()
    for i, (half, block, ref) in enumerate(pieces):
        stage[i] = ref[...].astype(f32)
        send(i, True)
    for i in range(len(pieces)): send(i, False)

def emit(deps, bits, pieces, second, out_shape, up_from=None, prev=()):
    n, W = pieces[0].shape
    m = len(pieces)
    return call(
        partial(emit_kernel, up_from, len(prev), second), deps, (bits, *pieces, *prev),
        [SM]+[VM]*m+[FAR]*len(prev), [FAR]*len(out_shape), [pltpu.HBM(s, f32) for s in out_shape],
        [pltpu.VMEM((m,n,W),f32), pltpu.SemaphoreType.DMA((m,))],
        {1+m+i: i for i in range(len(prev))}, vmem=18, name="emit",
    )

def split_kernel(index, bits_ref, keep_hbm, recv_hbm, *refs):
    outs, (a, b, o, sem) = refs[:2], refs[2:]
    n, W = outs[0].shape
    bit = bits_ref[index]
    def load(i):
        src = pl.ds((bit if i else 1 - bit)*n, n)
        return (pltpu.make_async_copy(keep_hbm.at[src, :], a.at[i], sem.at[0, i]),
                pltpu.make_async_copy(recv_hbm.at[src, :], b.at[i], sem.at[1, i]))
    for i in range(2):
        for c in load(i): c.start()
    for i in range(2):
        for c in load(i): c.wait()
        o[i] = (a[i].astype(f32) + b[i].astype(f32)).astype(bf16)
        pltpu.make_async_copy(o.at[i], outs[i], sem.at[2, i]).start()
    for i in range(2): pltpu.make_async_copy(o.at[i], outs[i], sem.at[2, i]).wait()

def split_add(deps, bits, index, keep, recv):
    n, W = keep.shape[0] // 2, keep.shape[1]
    if n % 16:
        keep, recv, deps = lax.optimization_barrier((keep, recv, tuple(deps)))
        bit = bits[index]
        halves = [[lax.dynamic_slice_in_dim(a, b * n, n, 0).astype(f32) for a in (keep, recv)] for b in (1 - bit, bit)]
        return deps[0], [(a + b).astype(bf16) for a, b in halves]
    return call(
        partial(split_kernel, index), deps, (bits, *in_hbm(keep), recv), [SM, FAR, ANY], [FAR]*2,
        [pltpu.HBM((n,W),bf16)]*2, [pltpu.VMEM((2,n,W),bf16)]*3+[pltpu.SemaphoreType.DMA((3,2))],
        vmem=14*n*W/MIB+1, name="split_add",
    )

def join_kernel(index, bits_ref, mine_hbm, recv_hbm, out_hbm, both, sem):
    n = mine_hbm.shape[0]
    bit = bits_ref[index]
    loads = [pltpu.make_async_copy(src, both.at[pl.ds(at*n, n), :], sem.at[i])
             for i, (src, at) in enumerate(((mine_hbm, bit), (recv_hbm, 1 - bit)))]
    for c in loads: c.start()
    for c in loads: c.wait()
    out = pltpu.make_async_copy(both, out_hbm, sem.at[2])
    out.start()
    out.wait()

def join(deps, bits, index, mine, recv):
    n, W = mine.shape
    if n % 16:
        mine, recv, deps = lax.optimization_barrier((mine, recv, tuple(deps)))
        return deps[0], [jnp.where(bits[index] == 0, jnp.concatenate([mine, recv], 0), jnp.concatenate([recv, mine], 0))]
    return call(
        partial(join_kernel, index), deps, (bits, mine, recv), [SM, ANY, ANY], [ANY],
        [jax.ShapeDtypeStruct((2*n,W),bf16)], [pltpu.VMEM((2*n,W),bf16), pltpu.SemaphoreType.DMA((3,))],
        vmem=8*n*W/MIB+1, name="join",
    )

def add_kernel(a_ref, b_ref, o_ref):
    o_ref[...] = (a_ref[...].astype(f32) + b_ref[...].astype(f32)).astype(o_ref.dtype)

def add_to(deps, a, b, dtype):
    return call(add_kernel, deps, (a, b), [VM, VM], [VM], [jax.ShapeDtypeStruct(a.shape, dtype)], vmem=8, name="add")

def stack_kernel(*refs):
    out, at = refs[-1], 0
    for r in refs[:-1]:
        out[at:at+r.shape[0], :] = r[...]
        at += r.shape[0]

def stack_rows(deps, arrays):
    rows = sum(a.shape[0] for a in arrays)
    return call(stack_kernel, deps, arrays, [VM]*len(arrays), [VM],
                [jax.ShapeDtypeStruct((rows, arrays[0].shape[1]), f32)], vmem=4, name="stack_rows")

D = 768
pool_eps = 1e-06


def matryoshka(averages):
    pieces = []
    for prefix in (D, D * 2 // 3, D // 3, D // 6, D // 12):
        leading = averages[..., :prefix]
        centred = leading - jnp.mean(leading, axis=-1, keepdims=True)
        pieces.append(
            centred * lax.rsqrt(jnp.mean(centred * centred, axis=-1, keepdims=True) + pool_eps)
        )
    return jnp.concatenate(pieces, axis=-1)


def part_of(value, index, count):
    rows = value.shape[0] // count
    return lax.dynamic_slice_in_dim(value, index * rows, rows, 0)


def ordered(bit, mine, theirs):
    first = lax.broadcasted_iota(jnp.int32, (2,) + (1,) * mine.ndim, 0) == bit
    return jnp.where(first, mine[None], theirs[None]).reshape((-1,) + mine.shape[1:])


def sum_of(arrays):
    total = arrays[0].astype(f32)
    for array in arrays[1:]:
        total = total + array.astype(f32)
    return total.astype(bf16)


fence = lax.optimization_barrier


class Links:
    def __init__(self, n_rows, n_blk):
        self.size = {"rows": n_rows, "blk": n_blk}
        self.at = {"rows": lax.axis_index("rows"), "blk": lax.axis_index("blk")}
        self.near = ("rows", 0, 0)
        self.near_bit = self.at["rows"] % 2
        far = list(range(1, n_rows.bit_length() - 1))
        self.far = [("rows", a, b) for a, b in zip(far, far[::-1])]
        self.plain_far = [("rows", a, a) for a in far]
        self.blk_bits = [("blk", k, k) for k in range(n_blk.bit_length() - 1)]

    def bit(self, stage, flip=False):
        axis, even, odd = stage
        at = self.at[axis]
        if even == odd:
            return (at >> even) % 2
        near = 1 - self.near_bit if flip else self.near_bit
        return jnp.where(near == 0, (at >> even) % 2, (at >> odd) % 2)

    def swap(self, value, stage):
        axis, even, odd = stage
        pairs = [(i, i ^ (1 << (odd if i % 2 and even != odd else even))) for i in range(self.size[axis])]
        return lax.ppermute(value, axis, pairs)


class Steps:
    def __init__(self, links):
        self.links = links
        self.stages = links.far + links.blk_bits
        first = links.far[0]
        bits = [links.near_bit, links.bit(first), links.bit(first, True)]
        self.base = len(bits)
        bits += [links.bit(stage) for stage in self.stages]
        self.bits = jnp.stack(bits).astype(jnp.int32)
        self.swap = links.swap

    def run(self, function, *args):
        return function((), *args)[1]

    def cut(self, addends, stage):
        return self.run(split_add, self.bits, self.base + self.stages.index(stage), *addends)

    def halve(self, addends, stage):
        bit = self.links.bit(stage)
        send = sum_of([part_of(a, 1 - bit, 2) for a in addends])
        keep = sum_of([part_of(a, bit, 2) for a in addends])
        return keep, self.swap(send, stage)

    def total(self, addends, stage):
        value = sum_of(addends)
        return value, self.swap(value, stage)

    def double(self, pieces, stage, following):
        value = ordered(self.links.bit(stage), *pieces)
        return value, self.swap(value, following)

    def last(self, pieces, stage, final):
        value = ordered(self.links.bit(stage), *pieces)
        return value, self.swap(value, final), self.swap(value, self.links.near)

    def finish(self, group):
        return group[0], group[2], group[1], self.swap(group[1], self.links.near)


def local(
    n_rows,
    n_blk,
    tokens,
    segments,
    query_weight,
    query_bias,
    key_weight,
    value_weight,
    value_bias,
    out_weight,
    out_bias,
    first_gain,
    first_shift,
    up_weight,
    up_bias,
    down_weight,
    down_bias,
    second_gain,
    second_shift,
    cotangent,
):
    links = Links(n_rows, n_blk)
    pair, cross = links.blk_bits
    seq_at = links.at["blk"] // 2
    near_bit = links.near_bit
    num_seq, tok_rows, width = tokens.shape
    ff = up_weight.shape[1]
    chunks = ff // width
    total_rows = 2 * tok_rows

    piece = tok_rows // 2
    pick = lambda a, s: lax.dynamic_index_in_dim(a, s, 0, keepdims=False)
    other = pick(tokens, 1 - seq_at)
    id_rows = jnp.pad(segments.astype(bf16)[:, None, :], ((0, 0), (0, ID_ROWS - 1), (0, width - tok_rows)))
    own = jnp.concatenate([pick(tokens, seq_at), pick(id_rows, seq_at)], 0)
    other_b = jnp.concatenate([other[piece:], pick(id_rows, 1 - seq_at)], 0)
    far_a = links.swap(other[:piece], cross)
    far_b = links.swap(other_b, cross)
    near_block = links.swap(own, pair)
    last_a = links.swap(far_a, pair)
    last_b = links.swap(far_b, pair)
    cot_other = pick(cotangent, 1 - seq_at)
    cot_other, far_b, far_a = fence((cot_other, far_b, far_a))
    cot_far = links.swap(cot_other, cross)
    here, late = [own, far_a, far_b, near_block], [last_a, last_b]
    value_wide = value_bias.reshape(-1, 128)
    queries, keys, values, numer, totals = attn_some(
        here, query_weight, key_weight, value_weight, query_bias.reshape(-1, 128), value_wide, total_rows
    )
    cot_own = pick(cotangent, seq_at)
    cot_own, late, queries, keys, values, numer, totals = fence(
        (cot_own, late, queries, keys, values, numer, totals)
    )
    blocks = [*here, *late]
    keys, values, attended, inv_totals, seg_row = attn_last(
        here, late, queries, key_weight, value_weight, value_wide, numer, totals, keys, values
    )
    vectors = [
        v.reshape(-1, 128)
        for v in (out_bias, first_gain, first_shift, down_bias, second_gain, second_shift, up_bias)
    ]
    half = chunks // 2
    order = jnp.concatenate(
        [(1 - near_bit) * half + jnp.arange(half), near_bit * half + jnp.arange(half)]
    ).astype(jnp.int32)
    (
        seg_sums, small, d_resid, d_numer, d_total, out_own, out_away, grad_out,
        send_one, send_two, keep_one, keep_two,
    ) = mid(
        order, attended, (own, far_a, far_b), (cot_own, cot_far), inv_totals, seg_row,
        vectors, out_weight, up_weight, down_weight,
    )
    back_in = (queries, keys, values, d_numer, d_total)
    tc = Steps(links)
    bits = tc.bits
    first, *rest = links.far
    backward = rest[::-1] + [first]
    ffn_shape, attn_shape = ((ff, width), (width, ff)), ((width, width),) * 4
    vectors = UP_B + chunks + 2
    seg_at, row_end = vectors, vectors + 16
    pairs = width // 128

    near_end = pairs // 3
    recv_one = tc.swap(send_one, links.near)
    recv_two = tc.swap(send_two, links.near)
    grads_a = tc.run(attn_bwd, *back_in, seg_row, 0, near_end)
    recv_one, recv_two, grads_a, back_in, out_away = fence((recv_one, recv_two, grads_a, back_in, out_away))

    send_one, one = tc.cut((keep_one, recv_one), first)
    send_one, recv_two, back_in, out_away = fence((send_one, recv_two, back_in, out_away))
    one = one, tc.swap(send_one, first)
    send_two, two = tc.cut((keep_two, recv_two), first)
    send_two, back_in, out_away = fence((send_two, back_in, out_away))
    two = two, tc.swap(send_two, first)
    out_back = tc.swap(out_away, cross)
    grads_b = tc.run(attn_bwd, *back_in, seg_row, near_end, pairs - near_end)
    grads = (*grads_a, *grads_b)
    bias_sums, attn_send, attn_keep = tc.run(weight_grad, bits, grads, blocks, grad_out)
    one, two, out_back, grads, bias_sums, attn_send = fence((one, two, out_back, grads, bias_sums, attn_send))

    for stage in rest:
        one = tc.halve(one, stage)
    attn_recv = tc.swap(attn_send, links.near)
    small = jnp.concatenate([small[: UP_B + chunks], bias_sums, seg_sums], 0)
    small_recv = tc.swap(small, pair)
    one, attn_recv, small, small_recv = fence((one, attn_recv, small, small_recv))

    send_three, three = tc.cut((attn_keep, attn_recv), first)
    send_three, one, two = fence((send_three, one, two))
    three = three, tc.swap(send_three, first)
    for stage in rest:
        two = tc.halve(two, stage)
    one = tc.halve(one, pair)
    small = small + small_recv
    small_recv = tc.swap(small, cross)
    d_own, d_away, pair_own, pair_away = tc.run(token_grad, grads, query_weight, key_weight, value_weight, d_resid)
    one, two, three, small, small_recv, d_own, d_away, pair_own, pair_away = fence(
        (one, two, three, small, small_recv, d_own, d_away, pair_own, pair_away)
    )

    for stage in rest:
        three = tc.halve(three, stage)
    one = tc.halve(one, cross)
    two = tc.halve(two, pair)
    both_sums = ordered(seq_at, small[None, seg_at:row_end], small_recv[None, seg_at:row_end])
    small = small[:vectors] + small_recv[:vectors]
    small_recv = tc.swap(small, links.near)
    one, two, three, small, small_recv, both_sums = fence((one, two, three, small, small_recv, both_sums))

    one = tc.total(one, cross)
    three = tc.halve(three, pair)
    two = tc.halve(two, cross)
    for stage in links.plain_far:
        small = small + small_recv
        small_recv = tc.swap(small, stage)
    one, two, three, small, small_recv, both_sums = fence((one, two, three, small, small_recv, both_sums))

    one = tc.double(one, cross, pair)
    two = tc.total(two, cross)
    three = tc.halve(three, cross)
    small = small + small_recv
    pooled = matryoshka(both_sums[:, :NSEG] / both_sums[:, 8 : 8 + NSEG])
    vector_sums = [small[i] for i in range(UP_B)] + [small[UP_B : UP_B + chunks].reshape(-1)]
    vector_sums += [small[UP_B + chunks], small[UP_B + chunks + 1]]
    layer_output = ordered(seq_at, out_own[None], out_back[None])
    one, two, three, pooled, vector_sums, layer_output = fence((one, two, three, pooled, vector_sums, layer_output))

    one = tc.double(one, pair, backward[0])
    two = tc.double(two, cross, pair)
    three = tc.total(three, cross)
    one, two, three, pair_away = fence((one, two, three, pair_away))

    for stage, following in zip(backward[:-2], backward[1:-1]):
        one = tc.double(one, stage, following)
    one = tc.last(one, backward[-2], first)
    two = tc.double(two, pair, backward[0])
    three = tc.double(three, cross, pair)
    pair_away = tc.swap(pair_away, pair)
    one, two, three, d_away, pair_away = fence((one, two, three, d_away, pair_away))

    three = tc.double(three, pair, backward[0])
    for stage, following in zip(backward[:-2], backward[1:-1]):
        two = tc.double(two, stage, following)
    two = tc.last(two, backward[-2], first)
    d_back = tc.swap((d_away + pair_away.astype(f32)).astype(bf16), cross)
    one = tc.finish(one)
    two, three, one, d_back, pair_own = fence((two, three, one, d_back, pair_own))

    for stage, following in zip(backward[:-2], backward[1:-1]):
        three = tc.double(three, stage, following)
    three = tc.last(three, backward[-2], first)
    pair_own = tc.swap(pair_own, pair)
    two = tc.finish(two)
    ffn_sums = tc.run(emit, bits, one, (False, True), ffn_shape, 0)
    down_sum, up_sum = tc.run(emit, bits, two, (False, True), ffn_shape, 1, ffn_sums)
    attn_sums = tc.run(emit, bits, (three[0], three[2]), (False,), attn_shape)
    three, pair_own, down_sum, up_sum, attn_sums, d_back = fence((three, pair_own, down_sum, up_sum, attn_sums, d_back))

    three = tc.finish(three)
    d_own = d_own + pair_own.astype(f32)
    grad_tokens = ordered(seq_at, d_own.astype(bf16)[None], d_back[None])
    query_sum, key_sum, value_sum, out_sum = tc.run(emit, bits, three[2:], (True,), attn_shape, None, attn_sums)
    return (
        layer_output,
        pooled,
        grad_tokens,
        query_sum,
        vector_sums[7],
        key_sum,
        value_sum,
        vector_sums[8],
        out_sum,
        vector_sums[OUT_B],
        vector_sums[G1],
        vector_sums[B1],
        up_sum,
        vector_sums[UP_B],
        down_sum,
        vector_sums[DOWN_B],
        vector_sums[G2],
        vector_sums[B2],
    )


def solution(mesh):
    row_split = P("rows", "blk", None)
    return jax.shard_map(
        partial(local, mesh.shape["rows"], mesh.shape["blk"]),
        mesh=mesh,
        in_specs=(row_split, P("rows", "blk")) + (P(),) * 15 + (row_split,),
        out_specs=(row_split, P("rows", None, None), row_split) + (P(),) * 15,
        check_vma=False,
    )
```

time: 330 us -> 306 us (0.927)
  local copies, waits for them, and re-layouts: 30 us -> 7.1 us
  Pallas kernels: 106 us -> 119 us
  other arithmetic: 19.5 us -> 12 us
  waiting for transfers between devices: 111 us -> 107 us
  starting transfers between devices: 57.5 us -> 53.8 us
    unnamed x106 -> x68, local copies, waits for them, and re-layouts: 21.3 us -> 3.35 us
    pallas_call x10 -> x14, Pallas kernels: 106 us -> 119 us  [the longest x11 67.3 us: call(): pl.pallas_call(body, grid=grid, in_specs=[ANY] * n + list(in_specs), out_...]
    select_n x11 -> x12, other arithmetic: 7.52 us -> 3.44 us  [ordered(): jnp.where(first, mine[None], theirs[None]).reshape((-1,) + mine.shape[1:])]
    ppermute x50 -> x48, starting transfers between devices: 57.5 us -> 53.8 us  [swap(): return lax.ppermute(value, axis, pairs)]
    ppermute x50 -> x48, waiting for transfers between devices: 111 us -> 107 us  [swap(): return lax.ppermute(value, axis, pairs)]
  transfers between devices with their start and end apart: 50 -> 48, of which waited for: 23 -> 25; matrix products, arithmetic and copies ran while one was open for 8% -> 4% of each run, Pallas kernels for 19% -> 25%
where the time goes in v3:
time: 306 us; the launch traced here: 301 us
  Pallas kernels  119 us (39%)
  waiting for transfers between devices  107 us (35%)
  starting transfers between devices  53.8 us (18%)
  other arithmetic  12 us (4%)
  local copies, waits for them, and re-layouts  7.1 us (2%)
    ppermute x48, waiting for transfers between devices, swap(): return lax.ppermute(value, axis, pairs)  107 us
    pallas_call x11, Pallas kernels, call(): pl.pallas_call(body, grid=grid, in_specs=[ANY] * n + list(in_specs), out_...  67.3 us
    ppermute x48, starting transfers between devices, swap(): return lax.ppermute(value, axis, pairs)  53.8 us
    pallas_call x1, Pallas kernels, mid(): pl.pallas_call(mid_kernel, in_specs=[sm] + [vm] * 4 + [any_] * 3 + [vm] *...  30.6 us
    pallas_call x1, Pallas kernels, attn_some(): pl.pallas_call(partial(attn_some_kernel, len(parts)), grid=(W // GW,), in...  12.2 us
    pallas_call x1, Pallas kernels, attn_last(): pl.pallas_call(partial(attn_last_kernel, len(parts), n), grid=(W // GW,),...  9 us
  transfers between devices with their start and end apart: 48, of which 25 were waited for; matrix products, arithmetic and copies ran while one was open for 4% of the time, Pallas kernels for 25%

profile of v3, /device:TPU:0, one launch (start us, length us, event | category | flops | bytes accessed | tf_op | source)
XLA Modules:
  0.0 301.2 jit_solution(9818728104044143859)
XLA Ops:
  2.6 4.1 %collective-permute-start = (bf16[144,768]{1,0:T(8,128)(2,1)S(1)}, bf16[144,768]{1,0:T(8,128)(2,1)S(1)}, u32[]{:S(2)}, u32[]{:S(2)}) collective-permute-start(bf16[144,768]{1,0:T(8,128)(2,1)S(1)} %pad_maximum_fusion.1), channel_id=1, source_target_pairs={{0,2},{1,3},{2,0},{3,1},{4,6},{5,7},{6,4},{7,5},{8,10},{9,11},{10,... | collective-permute-start | bytes 663560 | tf_op jit(solution)/shard_map/ppermute | solution.py:653
  9.6 15.8 %collective-permute-done.1.refs_1_.xb_ref = bf16[128,768]{1,0:T(8,128)(2,1)S(1)} collective-permute-done((bf16[128,768]{1,0:T(8,128)(2,1)S(1)}, bf16[128,768]{1,0:T(8,128)(2,1)S(1)}, u32[]{:S(2)}, u32[]{:S(2)}) %collective-permute-start.1) | collective-permute-done | bytes 196640 | tf_op jit(solution)/shard_map/ppermute | solution.py:653
  25.5 4.1 %collective-permute-start.3 = (bf16[128,768]{1,0:T(8,128)(2,1)S(1)}, bf16[128,768]{1,0:T(8,128)(2,1)S(1)}, u32[]{:S(2)}, u32[]{:S(2)}) collective-permute-start(bf16[128,768]{1,0:T(8,128)(2,1)S(1)} %collective-permute-done.1.refs_1_.xb_ref), channel_id=1, source_target_pairs={{0,1},{1,0},{2,3},{3,2},{4,5},{5,4},{6,7},{7,6},{8,9},{9,8},{10,11... | collective-permute-start | bytes 589832 | tf_op jit(solution)/shard_map/ppermute | solution.py:653
  31.0 12.2 %attn_some.1 = (bf16[512,768]{1,0:T(8,128)(2,1)}, bf16[1024,768]{1,0:T(8,128)(2,1)}, bf16[1024,768]{1,0:T(8,128)(2,1)}, f32[512,768]{1,0:T(8,128)}, f32[512,768]{1,0:T(8,128)}) custom-call(bf16[272,768]{1,0:T(8,128)(2,1)} %copy-done, bf16[128,768]{1,0:T(8,128)(2,1)} %copy-done.3, bf16[144,768]{1,0:T(8,128)(2,1)} %copy-done.2, bf16[272,768]{1,0:T(8,128)(2,1)} %copy-done.1, ...), custom_call_target="tpu_custom_call" | custom-call | tf_op jit(solution)/shard_map/attn_some/pallas_call | solution.py:308
  46.5 9.0 %attn_last.1 = (bf16[1024,768]{1,0:T(8,128)(2,1)}, bf16[1024,768]{1,0:T(8,128)(2,1)}, f32[512,768]{1,0:T(8,128)}, f32[512,768]{1,0:T(8,128)}, f32[8,1024]{1,0:T(8,128)}) custom-call(bf16[272,768]{1,0:T(8,128)(2,1)} %copy-done, bf16[128,768]{1,0:T(8,128)(2,1)} %copy-done.3, ...), custom_call_target="tpu_custom_call", output_to_operand_aliasing={{0}: (12, {}), {1}: (13, {})} | custom-call | tf_op jit(solution)/shard_map/attn_last/pallas_call | solution.py:359
  56.2 30.6 %mid.1 = (f32[16,768]{1,0:T(8,128)}, f32[16,768]{1,0:T(8,128)}, f32[512,768]{1,0:T(8,128)}, bf16[512,768]{1,0:T(8,128)(2,1)}, f32[512,768]{1,0:T(8,128)}, /*inde...) custom-call(s32[4]{0:T(128)} %pad_add_fusion.order_ref, ...), custom_call_target="tpu_custom_call" | custom-call | tf_op jit(solution)/shard_map/mid/pallas_call | solution.py:219
  87.5 8.8 %attn_bwd.2 = (f32[8,128]{1,0:T(8,128)}, bf16[512,256]{1,0:T(8,128)(2,1)}, bf16[1024,256]{1,0:T(8,128)(2,1)}, bf16[1024,256]{1,0:T(8,128)(2,1)}) custom-call(bf16[512,768]{1,0:T(8,128)(2,1)} %get-tuple-element.265.refs_6_.refs_0_, bf16[1024,768]{1,0:T(8,128)(2,1)} %get-tuple-element.266.refs_1_, bf16[1024,768]{1,0:T(8,128)(2,1)} %get-tuple-element.267.refs_2_, ...), custom_call_target="tpu_custom_call" | custom-call | tf_op jit(solution)/shard_map/attn_bwd/pallas_call | solution.py:45
  96.3 4.3 %split_add.3 = (f32[8,128]{1,0:T(8,128)}, bf16[768,768]{1,0:T(8,128)(2,1)}, bf16[768,768]{1,0:T(8,128)(2,1)}) custom-call(s32[7]{0:T(128)S(1)} %stack.28.refs_0_.refs_12_, bf16[1536,768]{1,0:T(8,128)(2,1)} %get-tuple-element.247.refs_1_, bf16[1536,768]{1,0:T(8,128)(2,1)} %collective-permute-done.6.refs_2_), custom_call_target="tpu_custom_call" | custom-call | tf_op jit(solution)/shard_map/split_add/pallas_call | solution.py:45
  100.7 3.6 %split_add.4 = (f32[8,128]{1,0:T(8,128)}, bf16[768,768]{1,0:T(8,128)(2,1)}, bf16[768,768]{1,0:T(8,128)(2,1)}) custom-call(s32[7]{0:T(128)S(1)} %stack.28.refs_0_.refs_12_, bf16[1536,768]{1,0:T(8,128)(2,1)} %get-tuple-element.246.refs_1_, bf16[1536,768]{1,0:T(8,128)(2,1)S(1)} %collective-permute-done.7.refs_2_), custom_call_target="tpu_custom_call" | custom-call | tf_op jit(solution)/shard_map/split_add/pallas_call | solution.py:45
  108.4 14.6 %attn_bwd.3 = (f32[8,128]{1,0:T(8,128)}, bf16[512,512]{1,0:T(8,128)(2,1)}, bf16[1024,512]{1,0:T(8,128)(2,1)}, bf16[1024,512]{1,0:T(8,128)(2,1)}) custom-call(bf16[512,768]{1,0:T(8,128)(2,1)} %get-tuple-element.265.refs_6_.refs_0_, bf16[1024,768]{1,0:T(8,128)(2,1)} %get-tuple-element.266.refs_1_, bf16[1024,768]{1,0:T(8,128)(2,1)} %get-tuple-element.267.refs_2_, ...), custom_call_target="tpu_custom_call" | custom-call | tf_op jit(solution)/shard_map/attn_bwd/pallas_call | solution.py:45
  123.0 9.3 %weight_grad.1 = (f32[8,128]{1,0:T(8,128)}, f32[2,768]{1,0:T(2,128)}, bf16[1536,768]{1,0:T(8,128)(2,1)}, bf16[1536,768]{1,0:T(8,128)(2,1)}) custom-call(bf16[272,768]{1,0:T(8,128)(2,1)} %copy-done, bf16[128,768]{1,0:T(8,128)(2,1)} %copy-done.3, bf16[144,768]{1,0:T(8,128)(2,1)} %copy-done.2, bf16[272,768]{1,0:T(8,128)(2,1)} %copy-done.1, ...), custom_call_target="tpu_custom_call" | custom-call | tf_op jit(solution)/shard_map/weight_grad/pallas_call | solution.py:45
  142.4 3.7 %collective-permute-done.11 = bf16[384,768]{1,0:T(8,128)(2,1)S(1)} collective-permute-done((bf16[384,768]{1,0:T(8,128)(2,1)S(1)}, bf16[384,768]{1,0:T(8,128)(2,1)S(1)}, u32[]{:S(2)}, u32[]{:S(2)}) %collective-permute-start.11) | collective-permute-done | bytes 589856 | tf_op jit(solution)/shard_map/ppermute | solution.py:653
  146.1 3.9 %split_add.5 = (f32[8,128]{1,0:T(8,128)}, bf16[768,768]{1,0:T(8,128)(2,1)}, bf16[768,768]{1,0:T(8,128)(2,1)}) custom-call(s32[7]{0:T(128)S(1)} %stack.28.refs_0_.refs_12_, bf16[1536,768]{1,0:T(8,128)(2,1)} %get-tuple-element.274.refs_1_, bf16[1536,768]{1,0:T(8,128)(2,1)S(1)} %collective-permute-done.12.refs_2_), custom_call_target="tpu_custom_call" | custom-call | tf_op jit(solution)/shard_map/split_add/pallas_call | solution.py:45
  158.6 8.3 %token_grad.1 = (f32[8,128]{1,0:T(8,128)}, f32[256,768]{1,0:T(8,128)}, f32[256,768]{1,0:T(8,128)}, bf16[256,768]{1,0:T(8,128)(2,1)}, bf16[256,768]{1,0:T(8,128)(2,1)}) custom-call(bf16[512,256]{1,0:T(8,128)(2,1)} %get-tuple-element.302.refs_6_.refs_0_, bf16[1024,256]{1,0:T(8,128)(2,1)} %get-tuple-element.303.refs_7_.refs_1_, ...), custom_call_target="tpu_custom_call" | custom-call | tf_op jit(solution)/shard_map/token_grad/pallas_call | solution.py:45
  168.0 4.7 %collective-permute-done.16 = bf16[768,768]{1,0:T(8,128)(2,1)} collective-permute-done((bf16[768,768]{1,0:T(8,128)(2,1)}, bf16[768,768]{1,0:T(8,128)(2,1)}, u32[]{:S(2)}, u32[]{:S(2)}) %collective-permute-start.16) | collective-permute-done | bytes 1179680 | tf_op jit(solution)/shard_map/ppermute | solution.py:653
  180.6 5.2 %collective-permute-done.18 = bf16[96,768]{1,0:T(8,128)(2,1)S(1)} collective-permute-done((bf16[96,768]{1,0:T(8,128)(2,1)S(1)}, bf16[96,768]{1,0:T(8,128)(2,1)S(1)}, u32[]{:S(2)}, u32[]{:S(2)}) %collective-permute-start.18) | collective-permute-done | bytes 147488 | tf_op jit(solution)/shard_map/ppermute | solution.py:653
  210.2 3.4 %collective-permute-done.28 = bf16[96,768]{1,0:T(8,128)(2,1)S(1)} collective-permute-done((bf16[96,768]{1,0:T(8,128)(2,1)S(1)}, bf16[96,768]{1,0:T(8,128)(2,1)S(1)}, u32[]{:S(2)}, u32[]{:S(2)}) %collective-permute-start.28) | collective-permute-done | bytes 147488 | tf_op jit(solution)/shard_map/ppermute | solution.py:653
  213.6 5.8 %collective-permute-done.29 = bf16[96,768]{1,0:T(8,128)(2,1)S(1)} collective-permute-done((bf16[96,768]{1,0:T(8,128)(2,1)S(1)}, bf16[96,768]{1,0:T(8,128)(2,1)S(1)}, u32[]{:S(2)}, u32[]{:S(2)}) %collective-permute-start.29) | collective-permute-done | bytes 147488 | tf_op jit(solution)/shard_map/ppermute | solution.py:653
  223.2 4.3 %collective-permute-done.32 = bf16[96,768]{1,0:T(8,128)(2,1)S(1)} collective-permute-done((bf16[96,768]{1,0:T(8,128)(2,1)S(1)}, bf16[96,768]{1,0:T(8,128)(2,1)S(1)}, u32[]{:S(2)}, u32[]{:S(2)}) %collective-permute-start.32) | collective-permute-done | bytes 147488 | tf_op jit(solution)/shard_map/ppermute | solution.py:653
  237.1 15.4 %collective-permute-done.36 = bf16[192,768]{1,0:T(8,128)(2,1)S(1)} collective-permute-done((bf16[192,768]{1,0:T(8,128)(2,1)S(1)}, bf16[192,768]{1,0:T(8,128)(2,1)S(1)}, u32[]{:S(2)}, u32[]{:S(2)}) %collective-permute-start.36) | collective-permute-done | bytes 294944 | tf_op jit(solution)/shard_map/ppermute | solution.py:653
  258.4 17.5 %collective-permute-done.42 = bf16[256,768]{1,0:T(8,128)(2,1)S(1)} collective-permute-done((bf16[256,768]{1,0:T(8,128)(2,1)S(1)}, bf16[256,768]{1,0:T(8,128)(2,1)S(1)}, u32[]{:S(2)}, u32[]{:S(2)}) %collective-permute-start.42) | collective-permute-done | bytes 393248 | tf_op jit(solution)/shard_map/ppermute | solution.py:653
  278.8 4.4 %emit.4 = (f32[8,128]{1,0:T(8,128)}, f32[3072,768]{1,0:T(8,128)}, f32[768,3072]{1,0:T(8,128)}) custom-call(s32[7]{0:T(128)S(1)} %stack.28.refs_0_.refs_12_, bf16[768,768]{1,0:T(8,128)(2,1)S(1)} %bitcast_select_fusion.2.refs_1_, bf16[768,768]{1,0:T(8,128)(2,1)S(1)} %collective-permute-done.34.refs_2_, bf16[768,768]{1,0:T(8,128)(2,1)S(1)} %collective-permute-done.33.refs_3_, ...), custom_call_target="tpu_custom_call" | custom-call | tf_op jit(solution)/shard_map/emit/pallas_call | solution.py:45
  286.2 4.4 %emit.5 = (f32[8,128]{1,0:T(8,128)}, f32[3072,768]{1,0:T(8,128)}, f32[768,3072]{1,0:T(8,128)}) custom-call(s32[7]{0:T(128)S(1)} %stack.28.refs_0_.refs_12_, bf16[768,768]{1,0:T(8,128)(2,1)S(1)} %bitcast_select_fusion.1.refs_1_, bf16[768,768]{1,0:T(8,128)(2,1)S(1)} %collective-permute-done.39.refs_2_, ...), custom_call_target="tpu_custom_call", output_to_operand_aliasing={{1}: (5, {}), {2}: (6, {})} | custom-call | tf_op jit(solution)/shard_map/emit/pallas_call | solution.py:45
  290.6 4.4 %collective-permute-done.43.refs_1_ = bf16[768,768]{1,0:T(8,128)(2,1)S(1)} collective-permute-done((bf16[768,768]{1,0:T(8,128)(2,1)S(1)}, bf16[768,768]{1,0:T(8,128)(2,1)S(1)}, u32[]{:S(2)}, u32[]{:S(2)}) %collective-permute-start.43) | collective-permute-done | bytes 1179680 | tf_op jit(solution)/shard_map/ppermute | solution.py:653
  (236 shorter events, 97.4 us)
Async XLA Ops:
  2.6 22.8 %collective-permute-start = (bf16[144,768]{1,0:T(8,128)(2,1)S(1)}, bf16[144,768]{1,0:T(8,128)(2,1)S(1)}, u32[]{:S(2)}, u32[]{:S(2)}) collective-permute-start(bf16[144,768]{1,0:T(8,128)(2,1)S(1)} %pad_maximum_fusion.1), channel_id=1, source_target_pairs={{0,2},{1,3},{2,0},{3,1},{4,6},{5,7},{6,4},{7,5},{8,10},{9,11},{10,... | collective-permute-start | bytes 663560 | tf_op jit(solution)/shard_map/ppermute | solution.py:653
  6.7 18.7 %collective-permute-start.1 = (bf16[128,768]{1,0:T(8,128)(2,1)S(1)}, bf16[128,768]{1,0:T(8,128)(2,1)S(1)}, u32[]{:S(2)}, u32[]{:S(2)}) collective-permute-start(bf16[128,768]{1,0:T(8,128)(2,1)S(1)} %get-tuple-element.434), channel_id=1, source_target_pairs={{0,2},{1,3},{2,0},{3,1},{4,6},{5,7},{6,4},{7,5},{8,10},{9,11},{10,... | collective-permute-start | bytes 589832 | tf_op jit(solution)/shard_map/ppermute | solution.py:653
  6.9 23.3 %collective-permute-start.2 = (bf16[272,768]{1,0:T(8,128)(2,1)S(1)}, bf16[272,768]{1,0:T(8,128)(2,1)S(1)}, u32[]{:S(2)}, u32[]{:S(2)}) collective-permute-start(bf16[272,768]{1,0:T(8,128)(2,1)S(1)} %pad_maximum_fusion.refs_0_.xa_ref), channel_id=1, source_target_pairs={{0,1},{1,0},{2,3},{3,2},{4,5},{5,4},{6,7},{7,6},{8,9},{9,8},{10,11... | collective-permute-start | bytes 1253384 | tf_op jit(solution)/shard_map/ppermute | solution.py:653
  25.4 30.0 %collective-permute-start.5 = (bf16[256,768]{1,0:T(8,128)(2,1)S(1)}, bf16[256,768]{1,0:T(8,128)(2,1)S(1)}, u32[]{:S(2)}, u32[]{:S(2)}) collective-permute-start(bf16[256,768]{1,0:T(8,128)(2,1)S(1)} %get-tuple-element.230), channel_id=1, source_target_pairs={{0,2},{1,3},{2,0},{3,1},{4,6},{5,7},{6,4},{7,5},{8,10},{9,11},{10,... | collective-permute-start | bytes 1179656 | tf_op jit(solution)/shard_map/ppermute | solution.py:653
  25.5 17.6 %collective-permute-start.3 = (bf16[128,768]{1,0:T(8,128)(2,1)S(1)}, bf16[128,768]{1,0:T(8,128)(2,1)S(1)}, u32[]{:S(2)}, u32[]{:S(2)}) collective-permute-start(bf16[128,768]{1,0:T(8,128)(2,1)S(1)} %collective-permute-done.1.refs_1_.xb_ref), channel_id=1, source_target_pairs={{0,1},{1,0},{2,3},{3,2},{4,5},{5,4},{6,7},{7,6},{8,9},{9,8},{10,11... | collective-permute-start | bytes 589832 | tf_op jit(solution)/shard_map/ppermute | solution.py:653
  29.6 16.2 %collective-permute-start.4 = (bf16[144,768]{1,0:T(8,128)(2,1)S(1)}, bf16[144,768]{1,0:T(8,128)(2,1)S(1)}, u32[]{:S(2)}, u32[]{:S(2)}) collective-permute-start(bf16[144,768]{1,0:T(8,128)(2,1)S(1)} %collective-permute-done.refs_2_.xc_ref), channel_id=1, source_target_pairs={{0,1},{1,0},{2,3},{3,2},{4,5},{5,4},{6,7},{7,6},{8,9},{9,8},{10,11... | collective-permute-start | bytes 663560 | tf_op jit(solution)/shard_map/ppermute | solution.py:653
  104.2 28.1 %collective-permute-start.8 = (bf16[768,768]{1,0:T(8,128)(2,1)S(1)}, bf16[768,768]{1,0:T(8,128)(2,1)S(1)}, u32[]{:S(2)}, u32[]{:S(2)}) collective-permute-start(bf16[768,768]{1,0:T(8,128)(2,1)S(1)} %copy-done.29), channel_id=1, source_target_pairs={{0,8},{4,20},{8,0},{12,28},{16,24},{20,4},{24,16},{28,12},{1,9},{5... | collective-permute-start | bytes 3538952 | tf_op jit(solution)/shard_map/ppermute | solution.py:653
  105.6 27.6 %collective-permute-start.9 = (bf16[768,768]{1,0:T(8,128)(2,1)}, bf16[768,768]{1,0:T(8,128)(2,1)S(1)}, u32[]{:S(2)}, u32[]{:S(2)}) collective-permute-start(bf16[768,768]{1,0:T(8,128)(2,1)} %get-tuple-element.278), channel_id=1, source_target_pairs={{0,8},{4,20},{8,0},{12,28},{16,24},{20,4},{24,16},{28,12},{1,9},{5... | collective-permute-start | bytes 3538952 | tf_op jit(solution)/shard_map/ppermute | solution.py:653
  106.3 26.0 %collective-permute-start.10 = (bf16[256,768]{1,0:T(8,128)(2,1)S(1)}, bf16[256,768]{1,0:T(8,128)(2,1)S(1)}, u32[]{:S(2)}, u32[]{:S(2)}) collective-permute-start(bf16[256,768]{1,0:T(8,128)(2,1)S(1)} %copy-done.32), channel_id=1, source_target_pairs={{0,2},{1,3},{2,0},{3,1},{4,6},{5,7},{6,4},{7,5},{8,10},{9,11},{10,... | collective-permute-start | bytes 1179656 | tf_op jit(solution)/shard_map/ppermute | solution.py:653
  150.1 22.7 %collective-permute-start.16 = (bf16[768,768]{1,0:T(8,128)(2,1)}, bf16[768,768]{1,0:T(8,128)(2,1)}, u32[]{:S(2)}, u32[]{:S(2)}) collective-permute-start(bf16[768,768]{1,0:T(8,128)(2,1)} %get-tuple-element.299), channel_id=1, source_target_pairs={{0,8},{4,20},{8,0},{12,28},{16,24},{20,4},{24,16},{28,12},{1,9},{5... | collective-permute-start | bytes 3538952 | tf_op jit(solution)/shard_map/ppermute | solution.py:653
  151.7 16.3 %collective-permute-start.15 = (bf16[384,768]{1,0:T(8,128)(2,1)S(1)}, bf16[384,768]{1,0:T(8,128)(2,1)S(1)}, u32[]{:S(2)}, u32[]{:S(2)}) collective-permute-start(bf16[384,768]{1,0:T(8,128)(2,1)S(1)} %get-tuple-element.422), channel_id=1, source_target_pairs={{0,16},{4,12},{8,24},{12,4},{16,0},{20,28},{24,8},{28,20},{1,17},{... | collective-permute-start | bytes 1769480 | tf_op jit(solution)/shard_map/ppermute | solution.py:653
  202.0 17.4 %collective-permute-start.27 = (bf16[192,768]{1,0:T(8,128)(2,1)S(1)}, bf16[192,768]{1,0:T(8,128)(2,1)S(1)}, u32[]{:S(2)}, u32[]{:S(2)}) collective-permute-start(bf16[192,768]{1,0:T(8,128)(2,1)S(1)} %bitcast_select_fusion.8), channel_id=1, source_target_pairs={{0,1},{1,0},{2,3},{3,2},{4,5},{5,4},{6,7},{7,6},{8,9},{9,8},{10,11... | collective-permute-start | bytes 884744 | tf_op jit(solution)/shard_map/ppermute | solution.py:653
  219.5 12.9 %collective-permute-start.30 = (bf16[384,768]{1,0:T(8,128)(2,1)S(1)}, bf16[384,768]{1,0:T(8,128)(2,1)S(1)}, u32[]{:S(2)}, u32[]{:S(2)}) collective-permute-start(bf16[384,768]{1,0:T(8,128)(2,1)S(1)} %bitcast_select_fusion.5), channel_id=1, source_target_pairs={{0,16},{4,12},{8,24},{12,4},{16,0},{20,28},{24,8},{28,20},{1,17},{... | collective-permute-start | bytes 1769480 | tf_op jit(solution)/shard_map/ppermute | solution.py:653
  232.6 22.6 %collective-permute-start.33 = (bf16[768,768]{1,0:T(8,128)(2,1)S(1)}, bf16[768,768]{1,0:T(8,128)(2,1)S(1)}, u32[]{:S(2)}, u32[]{:S(2)}) collective-permute-start(bf16[768,768]{1,0:T(8,128)(2,1)S(1)} %bitcast_select_fusion.2.refs_1_), channel_id=1, source_target_pairs={{0,8},{4,20},{8,0},{12,28},{16,24},{20,4},{24,16},{28,12},{1,9},{5... | collective-permute-start | bytes 3538952 | tf_op jit(solution)/shard_map/ppermute | solution.py:653
  232.7 22.5 %collective-permute-start.34 = (bf16[768,768]{1,0:T(8,128)(2,1)S(1)}, bf16[768,768]{1,0:T(8,128)(2,1)S(1)}, u32[]{:S(2)}, u32[]{:S(2)}) collective-permute-start(bf16[768,768]{1,0:T(8,128)(2,1)S(1)} %bitcast_select_fusion.2.refs_1_), channel_id=1, source_target_pairs={{0,4},{4,0},{8,12},{12,8},{16,20},{20,16},{24,28},{28,24},{1,5},{5... | collective-permute-start | bytes 3538952 | tf_op jit(solution)/shard_map/ppermute | solution.py:653
  232.9 19.6 %collective-permute-start.35 = (bf16[384,768]{1,0:T(8,128)(2,1)S(1)}, bf16[384,768]{1,0:T(8,128)(2,1)S(1)}, u32[]{:S(2)}, u32[]{:S(2)}) collective-permute-start(bf16[384,768]{1,0:T(8,128)(2,1)S(1)} %bitcast_select_fusion.4), channel_id=1, source_target_pairs={{0,16},{4,12},{8,24},{12,4},{16,0},{20,28},{24,8},{28,20},{1,17},{... | collective-permute-start | bytes 1769480 | tf_op jit(solution)/shard_map/ppermute | solution.py:653
  234.9 17.6 %collective-permute-start.37 = (bf16[256,768]{1,0:T(8,128)(2,1)S(1)}, bf16[256,768]{1,0:T(8,128)(2,1)S(1)}, u32[]{:S(2)}, u32[]{:S(2)}) collective-permute-start(bf16[256,768]{1,0:T(8,128)(2,1)S(1)} %copy-done.31), channel_id=1, source_target_pairs={{0,1},{1,0},{2,3},{3,2},{4,5},{5,4},{6,7},{7,6},{8,9},{9,8},{10,11... | collective-permute-start | bytes 1179656 | tf_op jit(solution)/shard_map/ppermute | solution.py:653
  235.0 17.5 %collective-permute-start.36 = (bf16[192,768]{1,0:T(8,128)(2,1)S(1)}, bf16[192,768]{1,0:T(8,128)(2,1)S(1)}, u32[]{:S(2)}, u32[]{:S(2)}) collective-permute-start(bf16[192,768]{1,0:T(8,128)(2,1)S(1)} %bitcast_select_fusion.6), channel_id=1, source_target_pairs={{0,1},{1,0},{2,3},{3,2},{4,5},{5,4},{6,7},{7,6},{8,9},{9,8},{10,11... | collective-permute-start | bytes 884744 | tf_op jit(solution)/shard_map/ppermute | solution.py:653
  255.4 22.6 %collective-permute-start.38 = (bf16[768,768]{1,0:T(8,128)(2,1)S(1)}, bf16[768,768]{1,0:T(8,128)(2,1)S(1)}, u32[]{:S(2)}, u32[]{:S(2)}) collective-permute-start(bf16[768,768]{1,0:T(8,128)(2,1)S(1)} %bitcast_select_fusion.1.refs_1_), channel_id=1, source_target_pairs={{0,8},{4,20},{8,0},{12,28},{16,24},{20,4},{24,16},{28,12},{1,9},{5... | collective-permute-start | bytes 3538952 | tf_op jit(solution)/shard_map/ppermute | solution.py:653
  255.5 22.5 %collective-permute-start.39 = (bf16[768,768]{1,0:T(8,128)(2,1)S(1)}, bf16[768,768]{1,0:T(8,128)(2,1)S(1)}, u32[]{:S(2)}, u32[]{:S(2)}) collective-permute-start(bf16[768,768]{1,0:T(8,128)(2,1)S(1)} %bitcast_select_fusion.1.refs_1_), channel_id=1, source_target_pairs={{0,4},{4,0},{8,12},{12,8},{16,20},{20,16},{24,28},{28,24},{1,5},{5... | collective-permute-start | bytes 3538952 | tf_op jit(solution)/shard_map/ppermute | solution.py:653
  255.6 22.4 %collective-permute-start.41 = (bf16[768,768]{1,0:T(8,128)(2,1)S(1)}, bf16[768,768]{1,0:T(8,128)(2,1)S(1)}, u32[]{:S(2)}, u32[]{:S(2)}) collective-permute-start(bf16[768,768]{1,0:T(8,128)(2,1)S(1)} %collective-permute-done.33.refs_3_), channel_id=1, source_target_pairs={{0,4},{4,0},{8,12},{12,8},{16,20},{20,16},{24,28},{28,24},{1,5},{5... | collective-permute-start | bytes 3538952 | tf_op jit(solution)/shard_map/ppermute | solution.py:653
  256.2 19.7 %collective-permute-start.40 = (bf16[384,768]{1,0:T(8,128)(2,1)S(1)}, bf16[384,768]{1,0:T(8,128)(2,1)S(1)}, u32[]{:S(2)}, u32[]{:S(2)}) collective-permute-start(bf16[384,768]{1,0:T(8,128)(2,1)S(1)} %bitcast_select_fusion.3), channel_id=1, source_target_pairs={{0,16},{4,12},{8,24},{12,4},{16,0},{20,28},{24,8},{28,20},{1,17},{... | collective-permute-start | bytes 1769480 | tf_op jit(solution)/shard_map/ppermute | solution.py:653
  258.3 17.6 %collective-permute-start.42 = (bf16[256,768]{1,0:T(8,128)(2,1)S(1)}, bf16[256,768]{1,0:T(8,128)(2,1)S(1)}, u32[]{:S(2)}, u32[]{:S(2)}) collective-permute-start(bf16[256,768]{1,0:T(8,128)(2,1)S(1)} %add_convert_fusion.7), channel_id=1, source_target_pairs={{0,2},{1,3},{2,0},{3,1},{4,6},{5,7},{6,4},{7,5},{8,10},{9,11},{10,... | collective-permute-start | bytes 1179656 | tf_op jit(solution)/shard_map/ppermute | solution.py:653
  278.8 16.2 %collective-permute-start.43 = (bf16[768,768]{1,0:T(8,128)(2,1)S(1)}, bf16[768,768]{1,0:T(8,128)(2,1)S(1)}, u32[]{:S(2)}, u32[]{:S(2)}) collective-permute-start(bf16[768,768]{1,0:T(8,128)(2,1)S(1)} %bitcast_select_fusion.refs_1_), channel_id=1, source_target_pairs={{0,8},{4,20},{8,0},{12,28},{16,24},{20,4},{24,16},{28,12},{1,9},{5... | collective-permute-start | bytes 3538952 | tf_op jit(solution)/shard_map/ppermute | solution.py:653
  (57 other events, 410.8 us)

commit v4 on v3

--- a/solution.py
+++ b/solution.py
@@ -396,9 +396,10 @@
             ds = (e * pr).astype(bf16)
             dv = dot(e.astype(bf16), dnp)
             dk = dot(ds, qp)
-            dq = dot_tn(ds, kp)
+            dq = dot_tn(kp, ds)
             res.append((dq,dk,dv))
-        dq_ref[:,cs] = (jnp.where(first, res[0][0], res[1][0]).astype(bf16).astype(f32)*0.125).astype(bf16)
+        dq = jnp.concatenate([res[0][0][0:HD, :], res[1][0][HD:, :]], axis=0)
+        dq_ref[:,cs] = (jnp.transpose(dq).astype(bf16).astype(f32)*0.125).astype(bf16)
         dk_ref[:,cs] = jnp.where(first, res[0][1], res[1][1]).astype(bf16)
         dv_ref[:,cs] = jnp.where(first, res[0][2], res[1][2]).astype(bf16)
 
@@ -527,19 +528,23 @@
 
 def split_kernel(index, bits_ref, keep_hbm, recv_hbm, *refs):
     outs, (a, b, o, sem) = refs[:2], refs[2:]
-    n, W = outs[0].shape
+    n = outs[0].shape[0]
     bit = bits_ref[index]
+    steps = o.shape[0] // 2
+    rows = n // steps
     def load(i):
-        src = pl.ds((bit if i else 1 - bit)*n, n)
+        src = pl.ds((bit if i // steps else 1 - bit)*n + i % steps*rows, rows)
         return (pltpu.make_async_copy(keep_hbm.at[src, :], a.at[i], sem.at[0, i]),
                 pltpu.make_async_copy(recv_hbm.at[src, :], b.at[i], sem.at[1, i]))
-    for i in range(2):
+    def store(i):
+        return pltpu.make_async_copy(o.at[i], outs[i // steps].at[pl.ds(i % steps*rows, rows), :], sem.at[2, i])
+    for i in range(2*steps):
         for c in load(i): c.start()
-    for i in range(2):
+    for i in range(2*steps):
         for c in load(i): c.wait()
         o[i] = (a[i].astype(f32) + b[i].astype(f32)).astype(bf16)
-        pltpu.make_async_copy(o.at[i], outs[i], sem.at[2, i]).start()
-    for i in range(2): pltpu.make_async_copy(o.at[i], outs[i], sem.at[2, i]).wait()
+        store(i).start()
+    for i in range(2*steps): store(i).wait()
 
 def split_add(deps, bits, index, keep, recv):
     n, W = keep.shape[0] // 2, keep.shape[1]
@@ -548,9 +553,11 @@
         bit = bits[index]
         halves = [[lax.dynamic_slice_in_dim(a, b * n, n, 0).astype(f32) for a in (keep, recv)] for b in (1 - bit, bit)]
         return deps[0], [(a + b).astype(bf16) for a, b in halves]
+    steps = n // 192 if n % 192 == 0 else 1
     return call(
         partial(split_kernel, index), deps, (bits, *in_hbm(keep), recv), [SM, FAR, ANY], [FAR]*2,
-        [pltpu.HBM((n,W),bf16)]*2, [pltpu.VMEM((2,n,W),bf16)]*3+[pltpu.SemaphoreType.DMA((3,2))],
+        [pltpu.HBM((n,W),bf16)]*2,
+        [pltpu.VMEM((2*steps,n//steps,W),bf16)]*3+[pltpu.SemaphoreType.DMA((3,2*steps))],
         vmem=14*n*W/MIB+1, name="split_add",
     )
 
@@ -789,25 +796,29 @@
     two = two, tc.swap(send_two, first)
     out_back = tc.swap(out_away, cross)
     grads_b = tc.run(attn_bwd, *back_in, seg_row, near_end, pairs - near_end)
+    send_one, one = tc.cut(one, rest[0])
+    send_one, grads_a, grads_b, out_back = fence((send_one, grads_a, grads_b, out_back))
+    one = one, tc.swap(send_one, rest[0])
     grads = (*grads_a, *grads_b)
     bias_sums, attn_send, attn_keep = tc.run(weight_grad, bits, grads, blocks, grad_out)
-    one, two, out_back, grads, bias_sums, attn_send = fence((one, two, out_back, grads, bias_sums, attn_send))
+    one, two, grads, bias_sums, attn_send = fence((one, two, grads, bias_sums, attn_send))
 
     for stage in rest:
+        two = tc.halve(two, stage)
+    for stage in [*rest[1:], pair]:
         one = tc.halve(one, stage)
     attn_recv = tc.swap(attn_send, links.near)
     small = jnp.concatenate([small[: UP_B + chunks], bias_sums, seg_sums], 0)
-    small_recv = tc.swap(small, pair)
-    one, attn_recv, small, small_recv = fence((one, attn_recv, small, small_recv))
+    small_recv = tc.swap(small, cross)
+    one, two, attn_recv, small, small_recv = fence((one, two, attn_recv, small, small_recv))
 
     send_three, three = tc.cut((attn_keep, attn_recv), first)
     send_three, one, two = fence((send_three, one, two))
     three = three, tc.swap(send_three, first)
-    for stage in rest:
-        two = tc.halve(two, stage)
-    one = tc.halve(one, pair)
-    small = small + small_recv
-    small_recv = tc.swap(small, cross)
+    one = tc.halve(one, cross)
+    two = tc.halve(two, pair)
+    small = jnp.concatenate([small[:vectors] + small_recv[:vectors], small[vectors:], small_recv[vectors:]], 0)
+    small_recv = tc.swap(small, pair)
     d_own, d_away, pair_own, pair_away = tc.run(token_grad, grads, query_weight, key_weight, value_weight, d_resid)
     one, two, three, small, small_recv, d_own, d_away, pair_own, pair_away = fence(
         (one, two, three, small, small_recv, d_own, d_away, pair_own, pair_away)
@@ -815,22 +826,25 @@
 
     for stage in rest:
         three = tc.halve(three, stage)
-    one = tc.halve(one, cross)
-    two = tc.halve(two, pair)
-    both_sums = ordered(seq_at, small[None, seg_at:row_end], small_recv[None, seg_at:row_end])
-    small = small[:vectors] + small_recv[:vectors]
+    one = tc.total(one, cross)
+    small = small + small_recv
+    both_sums = ordered(seq_at, small[None, seg_at:row_end], small[None, row_end:])
+    small = small[:vectors]
     small_recv = tc.swap(small, links.near)
     one, two, three, small, small_recv, both_sums = fence((one, two, three, small, small_recv, both_sums))
 
-    one = tc.total(one, cross)
+    one = tc.double(one, cross, pair)
     three = tc.halve(three, pair)
     two = tc.halve(two, cross)
     for stage in links.plain_far:
         small = small + small_recv
         small_recv = tc.swap(small, stage)
-    one, two, three, small, small_recv, both_sums = fence((one, two, three, small, small_recv, both_sums))
-
-    one = tc.double(one, cross, pair)
+    one, two, three, small, small_recv, both_sums, pair_away = fence(
+        (one, two, three, small, small_recv, both_sums, pair_away)
+    )
+
+    pair_away = tc.swap(pair_away, pair)
+    one = tc.double(one, pair, backward[0])
     two = tc.total(two, cross)
     three = tc.halve(three, cross)
     small = small + small_recv
@@ -838,19 +852,20 @@
     vector_sums = [small[i] for i in range(UP_B)] + [small[UP_B : UP_B + chunks].reshape(-1)]
     vector_sums += [small[UP_B + chunks], small[UP_B + chunks + 1]]
     layer_output = ordered(seq_at, out_own[None], out_back[None])
-    one, two, three, pooled, vector_sums, layer_output = fence((one, two, three, pooled, vector_sums, layer_output))
-
-    one = tc.double(one, pair, backward[0])
-    two = tc.double(two, cross, pair)
-    three = tc.total(three, cross)
-    one, two, three, pair_away = fence((one, two, three, pair_away))
+    one, two, three, pooled, vector_sums, layer_output, pair_away = fence(
+        (one, two, three, pooled, vector_sums, layer_output, pair_away)
+    )
 
     for stage, following in zip(backward[:-2], backward[1:-1]):
         one = tc.double(one, stage, following)
     one = tc.last(one, backward[-2], first)
+    two = tc.double(two, cross, pair)
+    three = tc.total(three, cross)
+    one, two, three = fence((one, two, three))
+
+    one = tc.finish(one)
     two = tc.double(two, pair, backward[0])
     three = tc.double(three, cross, pair)
-    pair_away = tc.swap(pair_away, pair)
     one, two, three, d_away, pair_away = fence((one, two, three, d_away, pair_away))
 
     three = tc.double(three, pair, backward[0])
@@ -858,15 +873,14 @@
         two = tc.double(two, stage, following)
     two = tc.last(two, backward[-2], first)
     d_back = tc.swap((d_away + pair_away.astype(f32)).astype(bf16), cross)
-    one = tc.finish(one)
-    two, three, one, d_back, pair_own = fence((two, three, one, d_back, pair_own))
+    ffn_sums = tc.run(emit, bits, one, (False, True), ffn_shape, 0)
+    two, three, ffn_sums, d_back, pair_own = fence((two, three, ffn_sums, d_back, pair_own))
 
     for stage, following in zip(backward[:-2], backward[1:-1]):
         three = tc.double(three, stage, following)
     three = tc.last(three, backward[-2], first)
     pair_own = tc.swap(pair_own, pair)
     two = tc.finish(two)
-    ffn_sums = tc.run(emit, bits, one, (False, True), ffn_shape, 0)
     down_sum, up_sum = tc.run(emit, bits, two, (False, True), ffn_shape, 1, ffn_sums)
     attn_sums = tc.run(emit, bits, (three[0], three[2]), (False,), attn_shape)
     three, pair_own, down_sum, up_sum, attn_sums, d_back = fence((three, pair_own, down_sum, up_sum, attn_sums, d_back))

time: 306 us -> 300 us (0.980)
  waiting for transfers between devices: 107 us -> 99.6 us
    ppermute x48, waiting for transfers between devices: 107 us -> 99.6 us  [swap(): return lax.ppermute(value, axis, pairs)]
    pallas_call x11 -> x12, Pallas kernels: 67.3 us -> 67.2 us  [call(): pl.pallas_call(body, grid=grid, in_specs=[ANY] * n + list(in_specs), out_...]
  transfers between devices with their start and end apart: 48 -> 48, of which waited for: 25 -> 26; matrix products, arithmetic and copies ran while one was open for 4% -> 5% of each run, Pallas kernels for 25% -> 26%
where the time goes in v4:
time: 300 us; the launch traced here: 296 us
  Pallas kernels  119 us (40%)
  waiting for transfers between devices  99.6 us (33%)
  starting transfers between devices  54.8 us (18%)
  other arithmetic  13.9 us (5%)
  local copies, waits for them, and re-layouts  6.73 us (2%)
    ppermute x48, waiting for transfers between devices, swap(): return lax.ppermute(value, axis, pairs)  99.6 us
    pallas_call x12, Pallas kernels, call(): pl.pallas_call(body, grid=grid, in_specs=[ANY] * n + list(in_specs), out_...  67.2 us
    ppermute x48, starting transfers between devices, swap(): return lax.ppermute(value, axis, pairs)  54.8 us
    pallas_call x1, Pallas kernels, mid(): pl.pallas_call(mid_kernel, in_specs=[sm] + [vm] * 4 + [any_] * 3 + [vm] *...  30.6 us
    pallas_call x1, Pallas kernels, attn_some(): pl.pallas_call(partial(attn_some_kernel, len(parts)), grid=(W // GW,), in...  12.2 us
    pallas_call x1, Pallas kernels, attn_last(): pl.pallas_call(partial(attn_last_kernel, len(parts), n), grid=(W // GW,),...  8.99 us
    convert_element_type x11, other arithmetic, sum_of(): return total.astype(bf16)  6.05 us
  transfers between devices with their start and end apart: 48, of which 26 were waited for; matrix products, arithmetic and copies ran while one was open for 5% of the time, Pallas kernels for 26%

profile of v4, /device:TPU:0, one launch (start us, length us, event | category | flops | bytes accessed | tf_op | source)
XLA Modules:
  0.0 295.8 jit_solution(9510308046138724966)
XLA Ops:
  2.5 4.0 %collective-permute-start.1 = (bf16[128,768]{1,0:T(8,128)(2,1)}, bf16[128,768]{1,0:T(8,128)(2,1)S(1)}, u32[]{:S(2)}, u32[]{:S(2)}) collective-permute-start(bf16[128,768]{1,0:T(8,128)(2,1)} %get-tuple-element.456), channel_id=1, source_target_pairs={{0,2},{1,3},{2,0},{3,1},{4,6},{5,7},{6,4},{7,5},{8,10},{9,11},{10,... | collective-permute-start | bytes 589832 | tf_op jit(solution)/shard_map/ppermute | solution.py:660
  10.3 11.3 %collective-permute-done.1.refs_1_.xb_ref = bf16[128,768]{1,0:T(8,128)(2,1)S(1)} collective-permute-done((bf16[128,768]{1,0:T(8,128)(2,1)}, bf16[128,768]{1,0:T(8,128)(2,1)S(1)}, u32[]{:S(2)}, u32[]{:S(2)}) %collective-permute-start.1) | collective-permute-done | bytes 196640 | tf_op jit(solution)/shard_map/ppermute | solution.py:660
  21.5 3.9 %collective-permute-done.refs_2_.xc_ref = bf16[144,768]{1,0:T(8,128)(2,1)S(1)} collective-permute-done((bf16[144,768]{1,0:T(8,128)(2,1)S(1)}, bf16[144,768]{1,0:T(8,128)(2,1)S(1)}, u32[]{:S(2)}, u32[]{:S(2)}) %collective-permute-start) | collective-permute-done | bytes 221216 | tf_op jit(solution)/shard_map/ppermute | solution.py:660
  25.4 4.1 %collective-permute-start.3 = (bf16[128,768]{1,0:T(8,128)(2,1)S(1)}, bf16[128,768]{1,0:T(8,128)(2,1)S(1)}, u32[]{:S(2)}, u32[]{:S(2)}) collective-permute-start(bf16[128,768]{1,0:T(8,128)(2,1)S(1)} %collective-permute-done.1.refs_1_.xb_ref), channel_id=1, source_target_pairs={{0,1},{1,0},{2,3},{3,2},{4,5},{5,4},{6,7},{7,6},{8,9},{9,8},{10,11... | collective-permute-start | bytes 589832 | tf_op jit(solution)/shard_map/ppermute | solution.py:660
  30.9 12.2 %attn_some.1 = (bf16[512,768]{1,0:T(8,128)(2,1)}, bf16[1024,768]{1,0:T(8,128)(2,1)}, bf16[1024,768]{1,0:T(8,128)(2,1)}, f32[512,768]{1,0:T(8,128)}, f32[512,768]{1,0:T(8,128)}) custom-call(bf16[272,768]{1,0:T(8,128)(2,1)} %copy-done, bf16[128,768]{1,0:T(8,128)(2,1)} %copy-done.3, bf16[144,768]{1,0:T(8,128)(2,1)} %copy-done.2, bf16[272,768]{1,0:T(8,128)(2,1)} %copy-done.1, ...), custom_call_target="tpu_custom_call" | custom-call | tf_op jit(solution)/shard_map/attn_some/pallas_call | solution.py:308
  46.4 9.0 %attn_last.1 = (bf16[1024,768]{1,0:T(8,128)(2,1)}, bf16[1024,768]{1,0:T(8,128)(2,1)}, f32[512,768]{1,0:T(8,128)}, f32[512,768]{1,0:T(8,128)}, f32[8,1024]{1,0:T(8,128)}) custom-call(bf16[272,768]{1,0:T(8,128)(2,1)} %copy-done, bf16[128,768]{1,0:T(8,128)(2,1)} %copy-done.3, ...), custom_call_target="tpu_custom_call", output_to_operand_aliasing={{0}: (12, {}), {1}: (13, {})} | custom-call | tf_op jit(solution)/shard_map/attn_last/pallas_call | solution.py:359
  56.1 30.6 %mid.1 = (f32[16,768]{1,0:T(8,128)}, f32[16,768]{1,0:T(8,128)}, f32[512,768]{1,0:T(8,128)}, bf16[512,768]{1,0:T(8,128)(2,1)}, f32[512,768]{1,0:T(8,128)}, /*inde...) custom-call(s32[4]{0:T(128)} %pad_add_fusion.order_ref, ...), custom_call_target="tpu_custom_call" | custom-call | tf_op jit(solution)/shard_map/mid/pallas_call | solution.py:219
  87.4 8.2 %attn_bwd.2 = (f32[8,128]{1,0:T(8,128)}, bf16[512,256]{1,0:T(8,128)(2,1)}, bf16[1024,256]{1,0:T(8,128)(2,1)}, bf16[1024,256]{1,0:T(8,128)(2,1)}) custom-call(bf16[512,768]{1,0:T(8,128)(2,1)} %get-tuple-element.280.refs_6_.refs_0_, bf16[1024,768]{1,0:T(8,128)(2,1)} %get-tuple-element.281.refs_1_, bf16[1024,768]{1,0:T(8,128)(2,1)} %get-tuple-element.282.refs_2_, ...), custom_call_target="tpu_custom_call" | custom-call | tf_op jit(solution)/shard_map/attn_bwd/pallas_call | solution.py:45
  95.6 4.3 %split_add.4 = (f32[8,128]{1,0:T(8,128)}, bf16[768,768]{1,0:T(8,128)(2,1)}, bf16[768,768]{1,0:T(8,128)(2,1)}) custom-call(s32[7]{0:T(128)S(1)} %stack.28.refs_0_.refs_12_, bf16[1536,768]{1,0:T(8,128)(2,1)} %get-tuple-element.245.refs_1_, bf16[1536,768]{1,0:T(8,128)(2,1)} %collective-permute-done.6.refs_2_), custom_call_target="tpu_custom_call" | custom-call | tf_op jit(solution)/shard_map/split_add/pallas_call | solution.py:45
  107.3 13.5 %attn_bwd.3 = (f32[8,128]{1,0:T(8,128)}, bf16[512,512]{1,0:T(8,128)(2,1)}, bf16[1024,512]{1,0:T(8,128)(2,1)}, bf16[1024,512]{1,0:T(8,128)(2,1)}) custom-call(bf16[512,768]{1,0:T(8,128)(2,1)} %get-tuple-element.280.refs_6_.refs_0_, bf16[1024,768]{1,0:T(8,128)(2,1)} %get-tuple-element.281.refs_1_, bf16[1024,768]{1,0:T(8,128)(2,1)} %get-tuple-element.282.refs_2_, ...), custom_call_target="tpu_custom_call" | custom-call | tf_op jit(solution)/shard_map/attn_bwd/pallas_call | solution.py:45
  126.5 9.3 %weight_grad.1 = (f32[8,128]{1,0:T(8,128)}, f32[2,768]{1,0:T(2,128)}, bf16[1536,768]{1,0:T(8,128)(2,1)}, bf16[1536,768]{1,0:T(8,128)(2,1)}) custom-call(bf16[272,768]{1,0:T(8,128)(2,1)} %copy-done, bf16[128,768]{1,0:T(8,128)(2,1)} %copy-done.3, bf16[144,768]{1,0:T(8,128)(2,1)} %copy-done.2, bf16[272,768]{1,0:T(8,128)(2,1)} %copy-done.1, ...), custom_call_target="tpu_custom_call" | custom-call | tf_op jit(solution)/shard_map/weight_grad/pallas_call | solution.py:45
  141.6 3.6 %collective-permute-start.15 = (f32[28,768]{1,0:T(8,128)S(1)}, f32[28,768]{1,0:T(8,128)S(1)}, u32[]{:S(2)}, u32[]{:S(2)}) collective-permute-start(f32[28,768]{1,0:T(8,128)S(1)} %pad_maximum_fusion.3), channel_id=1, source_target_pairs={{0,2},{1,3},{2,0},{3,1},{4,6},{5,7},{6,4},{7,5},{8,10},{9,11},{10,... | collective-permute-start | bytes 258056 | tf_op jit(solution)/shard_map/ppermute | solution.py:660
  145.1 5.5 %collective-permute-done.15 = f32[28,768]{1,0:T(8,128)S(1)} collective-permute-done((f32[28,768]{1,0:T(8,128)S(1)}, f32[28,768]{1,0:T(8,128)S(1)}, u32[]{:S(2)}, u32[]{:S(2)}) %collective-permute-start.15) | collective-permute-done | bytes 86048 | tf_op jit(solution)/shard_map/ppermute | solution.py:660
  162.5 8.3 %token_grad.1 = (f32[8,128]{1,0:T(8,128)}, f32[256,768]{1,0:T(8,128)}, f32[256,768]{1,0:T(8,128)}, bf16[256,768]{1,0:T(8,128)(2,1)}, bf16[256,768]{1,0:T(8,128)(2,1)}) custom-call(bf16[512,256]{1,0:T(8,128)(2,1)} %get-tuple-element.325.refs_6_.refs_0_, bf16[1024,256]{1,0:T(8,128)(2,1)} %get-tuple-element.326.refs_7_.refs_1_, ...), custom_call_target="tpu_custom_call" | custom-call | tf_op jit(solution)/shard_map/token_grad/pallas_call | solution.py:45
  176.8 6.8 %collective-permute-done.20 = bf16[96,768]{1,0:T(8,128)(2,1)S(1)} collective-permute-done((bf16[96,768]{1,0:T(8,128)(2,1)S(1)}, bf16[96,768]{1,0:T(8,128)(2,1)S(1)}, u32[]{:S(2)}, u32[]{:S(2)}) %collective-permute-start.20) | collective-permute-done | bytes 147488 | tf_op jit(solution)/shard_map/ppermute | solution.py:660
  193.1 8.3 %collective-permute-done.24 = bf16[96,768]{1,0:T(8,128)(2,1)S(1)} collective-permute-done((bf16[96,768]{1,0:T(8,128)(2,1)S(1)}, bf16[96,768]{1,0:T(8,128)(2,1)S(1)}, u32[]{:S(2)}, u32[]{:S(2)}) %collective-permute-start.24) | collective-permute-done | bytes 147488 | tf_op jit(solution)/shard_map/ppermute | solution.py:660
  212.4 6.1 %collective-permute-done.29 = bf16[96,768]{1,0:T(8,128)(2,1)S(1)} collective-permute-done((bf16[96,768]{1,0:T(8,128)(2,1)S(1)}, bf16[96,768]{1,0:T(8,128)(2,1)S(1)}, u32[]{:S(2)}, u32[]{:S(2)}) %collective-permute-start.29) | collective-permute-done | bytes 147488 | tf_op jit(solution)/shard_map/ppermute | solution.py:660
  223.5 4.9 %collective-permute-start.35 = (bf16[96,768]{1,0:T(8,128)(2,1)S(1)}, bf16[96,768]{1,0:T(8,128)(2,1)S(1)}, u32[]{:S(2)}, u32[]{:S(2)}) collective-permute-start(bf16[96,768]{1,0:T(8,128)(2,1)S(1)} %add_convert_fusion.12), channel_id=1, source_target_pairs={{0,2},{1,3},{2,0},{3,1},{4,6},{5,7},{6,4},{7,5},{8,10},{9,11},{10,... | collective-permute-start | bytes 442376 | tf_op jit(solution)/shard_map/ppermute | solution.py:660
  228.5 5.2 %collective-permute-done.35 = bf16[96,768]{1,0:T(8,128)(2,1)S(1)} collective-permute-done((bf16[96,768]{1,0:T(8,128)(2,1)S(1)}, bf16[96,768]{1,0:T(8,128)(2,1)S(1)}, u32[]{:S(2)}, u32[]{:S(2)}) %collective-permute-start.35) | collective-permute-done | bytes 147488 | tf_op jit(solution)/shard_map/ppermute | solution.py:660
  240.2 8.7 %collective-permute-done.38 = bf16[192,768]{1,0:T(8,128)(2,1)S(1)} collective-permute-done((bf16[192,768]{1,0:T(8,128)(2,1)S(1)}, bf16[192,768]{1,0:T(8,128)(2,1)S(1)}, u32[]{:S(2)}, u32[]{:S(2)}) %collective-permute-start.38) | collective-permute-done | bytes 294944 | tf_op jit(solution)/shard_map/ppermute | solution.py:660
  255.0 4.4 %emit.4 = (f32[8,128]{1,0:T(8,128)}, f32[3072,768]{1,0:T(8,128)}, f32[768,3072]{1,0:T(8,128)}) custom-call(s32[7]{0:T(128)S(1)} %stack.28.refs_0_.refs_12_, bf16[768,768]{1,0:T(8,128)(2,1)S(1)} %bitcast_select_fusion.2.refs_1_, bf16[768,768]{1,0:T(8,128)(2,1)S(1)} %collective-permute-done.33.refs_2_, bf16[768,768]{1,0:T(8,128)(2,1)S(1)} %collective-permute-done.32.refs_3_, ...), custom_call_target="tpu_custom_call" | custom-call | tf_op jit(solution)/shard_map/emit/pallas_call | solution.py:45
  259.4 13.2 %collective-permute-done.42 = bf16[256,768]{1,0:T(8,128)(2,1)S(1)} collective-permute-done((bf16[256,768]{1,0:T(8,128)(2,1)S(1)}, bf16[256,768]{1,0:T(8,128)(2,1)S(1)}, u32[]{:S(2)}, u32[]{:S(2)}) %collective-permute-start.42) | collective-permute-done | bytes 393248 | tf_op jit(solution)/shard_map/ppermute | solution.py:660
  278.7 4.4 %emit.5 = (f32[8,128]{1,0:T(8,128)}, f32[3072,768]{1,0:T(8,128)}, f32[768,3072]{1,0:T(8,128)}) custom-call(s32[7]{0:T(128)S(1)} %stack.28.refs_0_.refs_12_, bf16[768,768]{1,0:T(8,128)(2,1)S(1)} %bitcast_select_fusion.1.refs_1_, bf16[768,768]{1,0:T(8,128)(2,1)S(1)} %collective-permute-done.40.refs_2_, ...), custom_call_target="tpu_custom_call", output_to_operand_aliasing={{1}: (5, {}), {2}: (6, {})} | custom-call | tf_op jit(solution)/shard_map/emit/pallas_call | solution.py:45
  284.8 4.8 %collective-permute-done.43.refs_1_ = bf16[768,768]{1,0:T(8,128)(2,1)S(1)} collective-permute-done((bf16[768,768]{1,0:T(8,128)(2,1)S(1)}, bf16[768,768]{1,0:T(8,128)(2,1)S(1)}, u32[]{:S(2)}, u32[]{:S(2)}) %collective-permute-start.43) | collective-permute-done | bytes 1179680 | tf_op jit(solution)/shard_map/ppermute | solution.py:660
  (217 shorter events, 99.6 us)
Async XLA Ops:
  2.5 19.0 %collective-permute-start.1 = (bf16[128,768]{1,0:T(8,128)(2,1)}, bf16[128,768]{1,0:T(8,128)(2,1)S(1)}, u32[]{:S(2)}, u32[]{:S(2)}) collective-permute-start(bf16[128,768]{1,0:T(8,128)(2,1)} %get-tuple-element.456), channel_id=1, source_target_pairs={{0,2},{1,3},{2,0},{3,1},{4,6},{5,7},{6,4},{7,5},{8,10},{9,11},{10,... | collective-permute-start | bytes 589832 | tf_op jit(solution)/shard_map/ppermute | solution.py:660
  7.3 18.1 %collective-permute-start = (bf16[144,768]{1,0:T(8,128)(2,1)S(1)}, bf16[144,768]{1,0:T(8,128)(2,1)S(1)}, u32[]{:S(2)}, u32[]{:S(2)}) collective-permute-start(bf16[144,768]{1,0:T(8,128)(2,1)S(1)} %pad_maximum_fusion.1), channel_id=1, source_target_pairs={{0,2},{1,3},{2,0},{3,1},{4,6},{5,7},{6,4},{7,5},{8,10},{9,11},{10,... | collective-permute-start | bytes 663560 | tf_op jit(solution)/shard_map/ppermute | solution.py:660
  7.5 22.6 %collective-permute-start.2 = (bf16[272,768]{1,0:T(8,128)(2,1)S(1)}, bf16[272,768]{1,0:T(8,128)(2,1)S(1)}, u32[]{:S(2)}, u32[]{:S(2)}) collective-permute-start(bf16[272,768]{1,0:T(8,128)(2,1)S(1)} %pad_maximum_fusion.refs_0_.xa_ref), channel_id=1, source_target_pairs={{0,1},{1,0},{2,3},{3,2},{4,5},{5,4},{6,7},{7,6},{8,9},{9,8},{10,11... | collective-permute-start | bytes 1253384 | tf_op jit(solution)/shard_map/ppermute | solution.py:660
  25.4 30.0 %collective-permute-start.5 = (bf16[256,768]{1,0:T(8,128)(2,1)S(1)}, bf16[256,768]{1,0:T(8,128)(2,1)S(1)}, u32[]{:S(2)}, u32[]{:S(2)}) collective-permute-start(bf16[256,768]{1,0:T(8,128)(2,1)S(1)} %get-tuple-element.242), channel_id=1, source_target_pairs={{0,2},{1,3},{2,0},{3,1},{4,6},{5,7},{6,4},{7,5},{8,10},{9,11},{10,... | collective-permute-start | bytes 1179656 | tf_op jit(solution)/shard_map/ppermute | solution.py:660
  25.4 17.7 %collective-permute-start.3 = (bf16[128,768]{1,0:T(8,128)(2,1)S(1)}, bf16[128,768]{1,0:T(8,128)(2,1)S(1)}, u32[]{:S(2)}, u32[]{:S(2)}) collective-permute-start(bf16[128,768]{1,0:T(8,128)(2,1)S(1)} %collective-permute-done.1.refs_1_.xb_ref), channel_id=1, source_target_pairs={{0,1},{1,0},{2,3},{3,2},{4,5},{5,4},{6,7},{7,6},{8,9},{9,8},{10,11... | collective-permute-start | bytes 589832 | tf_op jit(solution)/shard_map/ppermute | solution.py:660
  29.5 16.2 %collective-permute-start.4 = (bf16[144,768]{1,0:T(8,128)(2,1)S(1)}, bf16[144,768]{1,0:T(8,128)(2,1)S(1)}, u32[]{:S(2)}, u32[]{:S(2)}) collective-permute-start(bf16[144,768]{1,0:T(8,128)(2,1)S(1)} %collective-permute-done.refs_2_.xc_ref), channel_id=1, source_target_pairs={{0,1},{1,0},{2,3},{3,2},{4,5},{5,4},{6,7},{7,6},{8,9},{9,8},{10,11... | collective-permute-start | bytes 663560 | tf_op jit(solution)/shard_map/ppermute | solution.py:660
  99.8 20.9 %collective-permute-start.8 = (bf16[768,768]{1,0:T(8,128)(2,1)}, bf16[768,768]{1,0:T(8,128)(2,1)S(1)}, u32[]{:S(2)}, u32[]{:S(2)}) collective-permute-start(bf16[768,768]{1,0:T(8,128)(2,1)} %get-tuple-element.266), channel_id=1, source_target_pairs={{0,8},{4,20},{8,0},{12,28},{16,24},{20,4},{24,16},{28,12},{1,9},{5... | collective-permute-start | bytes 3538952 | tf_op jit(solution)/shard_map/ppermute | solution.py:660
  104.4 31.4 %collective-permute-start.11 = (bf16[768,768]{1,0:T(8,128)(2,1)}, bf16[768,768]{1,0:T(8,128)(2,1)}, u32[]{:S(2)}, u32[]{:S(2)}) collective-permute-start(bf16[768,768]{1,0:T(8,128)(2,1)} %get-tuple-element.300), channel_id=1, source_target_pairs={{0,8},{4,20},{8,0},{12,28},{16,24},{20,4},{24,16},{28,12},{1,9},{5... | collective-permute-start | bytes 3538952 | tf_op jit(solution)/shard_map/ppermute | solution.py:660
  105.2 20.0 %collective-permute-start.9 = (bf16[256,768]{1,0:T(8,128)(2,1)S(1)}, bf16[256,768]{1,0:T(8,128)(2,1)}, u32[]{:S(2)}, u32[]{:S(2)}) collective-permute-start(bf16[256,768]{1,0:T(8,128)(2,1)S(1)} %copy-done.21), channel_id=1, source_target_pairs={{0,2},{1,3},{2,0},{3,1},{4,6},{5,7},{6,4},{7,5},{8,10},{9,11},{10,... | collective-permute-start | bytes 1179656 | tf_op jit(solution)/shard_map/ppermute | solution.py:660
  135.8 17.0 %collective-permute-start.14 = (bf16[1536,768]{1,0:T(8,128)(2,1)}, bf16[1536,768]{1,0:T(8,128)(2,1)S(1)}, u32[]{:S(2)}, u32[]{:S(2)}) collective-permute-start(bf16[1536,768]{1,0:T(8,128)(2,1)} %get-tuple-element.307), channel_id=1, source_target_pairs={{0,4},{4,0},{8,12},{12,8},{16,20},{20,16},{24,28},{28,24},{1,5},{5... | collective-permute-start | bytes 7077896 | tf_op jit(solution)/shard_map/ppermute | solution.py:660
  138.6 14.2 %collective-permute-start.13 = (bf16[384,768]{1,0:T(8,128)(2,1)}, bf16[384,768]{1,0:T(8,128)(2,1)}, u32[]{:S(2)}, u32[]{:S(2)}) collective-permute-start(bf16[384,768]{1,0:T(8,128)(2,1)} %get-tuple-element.446), channel_id=1, source_target_pairs={{0,16},{4,12},{8,24},{12,4},{16,0},{20,28},{24,8},{28,20},{1,17},{... | collective-permute-start | bytes 1769480 | tf_op jit(solution)/shard_map/ppermute | solution.py:660
  156.0 16.5 %collective-permute-start.18 = (bf16[768,768]{1,0:T(8,128)(2,1)}, bf16[768,768]{1,0:T(8,128)(2,1)S(1)}, u32[]{:S(2)}, u32[]{:S(2)}) collective-permute-start(bf16[768,768]{1,0:T(8,128)(2,1)} %get-tuple-element.322), channel_id=1, source_target_pairs={{0,8},{4,20},{8,0},{12,28},{16,24},{20,4},{24,16},{28,12},{1,9},{5... | collective-permute-start | bytes 3538952 | tf_op jit(solution)/shard_map/ppermute | solution.py:660
  156.7 14.0 %collective-permute-start.19 = (f32[44,768]{1,0:T(8,128)S(1)}, f32[44,768]{1,0:T(8,128)S(1)}, u32[]{:S(2)}, u32[]{:S(2)}) collective-permute-start(f32[44,768]{1,0:T(8,128)S(1)} %pad_maximum_fusion.2), channel_id=1, source_target_pairs={{0,1},{1,0},{2,3},{3,2},{4,5},{5,4},{6,7},{7,6},{8,9},{9,8},{10,11... | collective-permute-start | bytes 405512 | tf_op jit(solution)/shard_map/ppermute | solution.py:660
  185.3 16.0 %collective-permute-start.23 = (bf16[192,768]{1,0:T(8,128)(2,1)S(1)}, bf16[192,768]{1,0:T(8,128)(2,1)S(1)}, u32[]{:S(2)}, u32[]{:S(2)}) collective-permute-start(bf16[192,768]{1,0:T(8,128)(2,1)S(1)} %bitcast_select_fusion.8), channel_id=1, source_target_pairs={{0,1},{1,0},{2,3},{3,2},{4,5},{5,4},{6,7},{7,6},{8,9},{9,8},{10,11... | collective-permute-start | bytes 884744 | tf_op jit(solution)/shard_map/ppermute | solution.py:660
  185.9 17.7 %collective-permute-start.25 = (bf16[192,768]{1,0:T(8,128)(2,1)S(1)}, bf16[192,768]{1,0:T(8,128)(2,1)S(1)}, u32[]{:S(2)}, u32[]{:S(2)}) collective-permute-start(bf16[192,768]{1,0:T(8,128)(2,1)S(1)} %get-tuple-element.448), channel_id=1, source_target_pairs={{0,1},{1,0},{2,3},{3,2},{4,5},{5,4},{6,7},{7,6},{8,9},{9,8},{10,11... | collective-permute-start | bytes 884744 | tf_op jit(solution)/shard_map/ppermute | solution.py:660
  187.7 13.6 %collective-permute-start.24 = (bf16[96,768]{1,0:T(8,128)(2,1)S(1)}, bf16[96,768]{1,0:T(8,128)(2,1)S(1)}, u32[]{:S(2)}, u32[]{:S(2)}) collective-permute-start(bf16[96,768]{1,0:T(8,128)(2,1)S(1)} %get-tuple-element.460), channel_id=1, source_target_pairs={{0,2},{1,3},{2,0},{3,1},{4,6},{5,7},{6,4},{7,5},{8,10},{9,11},{10,... | collective-permute-start | bytes 442376 | tf_op jit(solution)/shard_map/ppermute | solution.py:660
  206.3 13.8 %collective-permute-start.30 = (bf16[96,768]{1,0:T(8,128)(2,1)S(1)}, bf16[96,768]{1,0:T(8,128)(2,1)S(1)}, u32[]{:S(2)}, u32[]{:S(2)}) collective-permute-start(bf16[96,768]{1,0:T(8,128)(2,1)S(1)} %get-tuple-element.458), channel_id=1, source_target_pairs={{0,2},{1,3},{2,0},{3,1},{4,6},{5,7},{6,4},{7,5},{8,10},{9,11},{10,... | collective-permute-start | bytes 442376 | tf_op jit(solution)/shard_map/ppermute | solution.py:660
  208.2 14.3 %collective-permute-start.31 = (bf16[256,768]{1,0:T(8,128)(2,1)S(1)}, bf16[256,768]{1,0:T(8,128)(2,1)S(1)}, u32[]{:S(2)}, u32[]{:S(2)}) collective-permute-start(bf16[256,768]{1,0:T(8,128)(2,1)S(1)} %copy-done.20), channel_id=1, source_target_pairs={{0,1},{1,0},{2,3},{3,2},{4,5},{5,4},{6,7},{7,6},{8,9},{9,8},{10,11... | collective-permute-start | bytes 1179656 | tf_op jit(solution)/shard_map/ppermute | solution.py:660
  222.8 16.3 %collective-permute-start.32 = (bf16[768,768]{1,0:T(8,128)(2,1)S(1)}, bf16[768,768]{1,0:T(8,128)(2,1)S(1)}, u32[]{:S(2)}, u32[]{:S(2)}) collective-permute-start(bf16[768,768]{1,0:T(8,128)(2,1)S(1)} %bitcast_select_fusion.2.refs_1_), channel_id=1, source_target_pairs={{0,8},{4,20},{8,0},{12,28},{16,24},{20,4},{24,16},{28,12},{1,9},{5... | collective-permute-start | bytes 3538952 | tf_op jit(solution)/shard_map/ppermute | solution.py:660
  249.4 23.2 %collective-permute-start.40 = (bf16[768,768]{1,0:T(8,128)(2,1)S(1)}, bf16[768,768]{1,0:T(8,128)(2,1)S(1)}, u32[]{:S(2)}, u32[]{:S(2)}) collective-permute-start(bf16[768,768]{1,0:T(8,128)(2,1)S(1)} %bitcast_select_fusion.1.refs_1_), channel_id=1, source_target_pairs={{0,4},{4,0},{8,12},{12,8},{16,20},{20,16},{24,28},{28,24},{1,5},{5... | collective-permute-start | bytes 3538952 | tf_op jit(solution)/shard_map/ppermute | solution.py:660
  249.5 23.1 %collective-permute-start.39 = (bf16[768,768]{1,0:T(8,128)(2,1)S(1)}, bf16[768,768]{1,0:T(8,128)(2,1)S(1)}, u32[]{:S(2)}, u32[]{:S(2)}) collective-permute-start(bf16[768,768]{1,0:T(8,128)(2,1)S(1)} %bitcast_select_fusion.1.refs_1_), channel_id=1, source_target_pairs={{0,8},{4,20},{8,0},{12,28},{16,24},{20,4},{24,16},{28,12},{1,9},{5... | collective-permute-start | bytes 3538952 | tf_op jit(solution)/shard_map/ppermute | solution.py:660
  250.4 22.2 %collective-permute-start.41 = (bf16[384,768]{1,0:T(8,128)(2,1)S(1)}, bf16[384,768]{1,0:T(8,128)(2,1)S(1)}, u32[]{:S(2)}, u32[]{:S(2)}) collective-permute-start(bf16[384,768]{1,0:T(8,128)(2,1)S(1)} %bitcast_select_fusion.3), channel_id=1, source_target_pairs={{0,16},{4,12},{8,24},{12,4},{16,0},{20,28},{24,8},{28,20},{1,17},{... | collective-permute-start | bytes 1769480 | tf_op jit(solution)/shard_map/ppermute | solution.py:660
  251.9 20.7 %collective-permute-start.42 = (bf16[256,768]{1,0:T(8,128)(2,1)S(1)}, bf16[256,768]{1,0:T(8,128)(2,1)S(1)}, u32[]{:S(2)}, u32[]{:S(2)}) collective-permute-start(bf16[256,768]{1,0:T(8,128)(2,1)S(1)} %add_convert_fusion.5), channel_id=1, source_target_pairs={{0,2},{1,3},{2,0},{3,1},{4,6},{5,7},{6,4},{7,5},{8,10},{9,11},{10,... | collective-permute-start | bytes 1179656 | tf_op jit(solution)/shard_map/ppermute | solution.py:660
  273.4 16.2 %collective-permute-start.43 = (bf16[768,768]{1,0:T(8,128)(2,1)S(1)}, bf16[768,768]{1,0:T(8,128)(2,1)S(1)}, u32[]{:S(2)}, u32[]{:S(2)}) collective-permute-start(bf16[768,768]{1,0:T(8,128)(2,1)S(1)} %bitcast_select_fusion.refs_1_), channel_id=1, source_target_pairs={{0,8},{4,20},{8,0},{12,28},{16,24},{20,4},{24,16},{28,12},{1,9},{5... | collective-permute-start | bytes 3538952 | tf_op jit(solution)/shard_map/ppermute | solution.py:660
  (46 other events, 351.9 us)

commit v5 on v4

--- a/solution.py
+++ b/solution.py
@@ -808,12 +808,11 @@
     for stage in [*rest[1:], pair]:
         one = tc.halve(one, stage)
     attn_recv = tc.swap(attn_send, links.near)
+    send_three, three = tc.cut((attn_keep, attn_recv), first)
     small = jnp.concatenate([small[: UP_B + chunks], bias_sums, seg_sums], 0)
     small_recv = tc.swap(small, cross)
-    one, two, attn_recv, small, small_recv = fence((one, two, attn_recv, small, small_recv))
-
-    send_three, three = tc.cut((attn_keep, attn_recv), first)
-    send_three, one, two = fence((send_three, one, two))
+    one, two, three, send_three, small, small_recv = fence((one, two, three, send_three, small, small_recv))
+
     three = three, tc.swap(send_three, first)
     one = tc.halve(one, cross)
     two = tc.halve(two, pair)
@@ -861,18 +860,19 @@
     one = tc.last(one, backward[-2], first)
     two = tc.double(two, cross, pair)
     three = tc.total(three, cross)
-    one, two, three = fence((one, two, three))
+    d_away = (d_away + pair_away.astype(f32)).astype(bf16)
+    one, two, three, d_away = fence((one, two, three, d_away))
 
     one = tc.finish(one)
     two = tc.double(two, pair, backward[0])
     three = tc.double(three, cross, pair)
-    one, two, three, d_away, pair_away = fence((one, two, three, d_away, pair_away))
+    one, two, three, d_away = fence((one, two, three, d_away))
 
     three = tc.double(three, pair, backward[0])
     for stage, following in zip(backward[:-2], backward[1:-1]):
         two = tc.double(two, stage, following)
     two = tc.last(two, backward[-2], first)
-    d_back = tc.swap((d_away + pair_away.astype(f32)).astype(bf16), cross)
+    d_back = tc.swap(d_away, cross)
     ffn_sums = tc.run(emit, bits, one, (False, True), ffn_shape, 0)
     two, three, ffn_sums, d_back, pair_own = fence((two, three, ffn_sums, d_back, pair_own))
 

time: 300 us -> 297 us (0.990)
  waiting for transfers between devices: 99.6 us -> 96.1 us
    ppermute x48, waiting for transfers between devices: 99.6 us -> 96.1 us  [swap(): return lax.ppermute(value, axis, pairs)]
  transfers between devices with their start and end apart: 48 -> 48, of which waited for: 26 -> 26; matrix products, arithmetic and copies ran while one was open for 5% -> 5% of each run, Pallas kernels for 26% -> 28%
where the time goes in v5:
time: 297 us; the launch traced here: 293 us
  Pallas kernels  119 us (40%)
  waiting for transfers between devices  96.1 us (32%)
  starting transfers between devices  54.4 us (18%)
  other arithmetic  13.8 us (5%)
  local copies, waits for them, and re-layouts  7.78 us (3%)
    ppermute x48, waiting for transfers between devices, swap(): return lax.ppermute(value, axis, pairs)  96.1 us
    pallas_call x12, Pallas kernels, call(): pl.pallas_call(body, grid=grid, in_specs=[ANY] * n + list(in_specs), out_...  67.2 us
    ppermute x48, starting transfers between devices, swap(): return lax.ppermute(value, axis, pairs)  54.4 us
    pallas_call x1, Pallas kernels, mid(): pl.pallas_call(mid_kernel, in_specs=[sm] + [vm] * 4 + [any_] * 3 + [vm] *...  30.6 us
    pallas_call x1, Pallas kernels, attn_some(): pl.pallas_call(partial(attn_some_kernel, len(parts)), grid=(W // GW,), in...  12.2 us
    pallas_call x1, Pallas kernels, attn_last(): pl.pallas_call(partial(attn_last_kernel, len(parts), n), grid=(W // GW,),...  8.99 us
    convert_element_type x11, other arithmetic, sum_of(): return total.astype(bf16)  6.05 us
  transfers between devices with their start and end apart: 48, of which 26 were waited for; matrix products, arithmetic and copies ran while one was open for 5% of the time, Pallas kernels for 28%

profile of v5, /device:TPU:0, one launch (start us, length us, event | category | flops | bytes accessed | tf_op | source)
XLA Modules:
  0.0 292.9 jit_solution(10215900581217357841)
XLA Ops:
  1.8 4.1 %collective-permute-start.1 = (bf16[128,768]{1,0:T(8,128)(2,1)S(1)}, bf16[128,768]{1,0:T(8,128)(2,1)S(1)}, u32[]{:S(2)}, u32[]{:S(2)}) collective-permute-start(bf16[128,768]{1,0:T(8,128)(2,1)S(1)} %get-tuple-element.448), channel_id=1, source_target_pairs={{0,2},{1,3},{2,0},{3,1},{4,6},{5,7},{6,4},{7,5},{8,10},{9,11},{10,... | collective-permute-start | bytes 589832 | tf_op jit(solution)/shard_map/ppermute | solution.py:660
  9.7 11.1 %collective-permute-done.1.refs_1_.xb_ref = bf16[128,768]{1,0:T(8,128)(2,1)S(1)} collective-permute-done((bf16[128,768]{1,0:T(8,128)(2,1)S(1)}, bf16[128,768]{1,0:T(8,128)(2,1)S(1)}, u32[]{:S(2)}, u32[]{:S(2)}) %collective-permute-start.1) | collective-permute-done | bytes 196640 | tf_op jit(solution)/shard_map/ppermute | solution.py:660
  20.7 3.9 %collective-permute-done.refs_2_.xc_ref = bf16[144,768]{1,0:T(8,128)(2,1)S(1)} collective-permute-done((bf16[144,768]{1,0:T(8,128)(2,1)S(1)}, bf16[144,768]{1,0:T(8,128)(2,1)S(1)}, u32[]{:S(2)}, u32[]{:S(2)}) %collective-permute-start) | collective-permute-done | bytes 221216 | tf_op jit(solution)/shard_map/ppermute | solution.py:660
  24.6 4.1 %collective-permute-start.3 = (bf16[128,768]{1,0:T(8,128)(2,1)S(1)}, bf16[128,768]{1,0:T(8,128)(2,1)S(1)}, u32[]{:S(2)}, u32[]{:S(2)}) collective-permute-start(bf16[128,768]{1,0:T(8,128)(2,1)S(1)} %collective-permute-done.1.refs_1_.xb_ref), channel_id=1, source_target_pairs={{0,1},{1,0},{2,3},{3,2},{4,5},{5,4},{6,7},{7,6},{8,9},{9,8},{10,11... | collective-permute-start | bytes 589832 | tf_op jit(solution)/shard_map/ppermute | solution.py:660
  30.1 12.2 %attn_some.1 = (bf16[512,768]{1,0:T(8,128)(2,1)}, bf16[1024,768]{1,0:T(8,128)(2,1)}, bf16[1024,768]{1,0:T(8,128)(2,1)}, f32[512,768]{1,0:T(8,128)}, f32[512,768]{1,0:T(8,128)}) custom-call(bf16[272,768]{1,0:T(8,128)(2,1)} %copy-done, bf16[128,768]{1,0:T(8,128)(2,1)} %copy-done.3, bf16[144,768]{1,0:T(8,128)(2,1)} %copy-done.2, bf16[272,768]{1,0:T(8,128)(2,1)} %copy-done.1, ...), custom_call_target="tpu_custom_call" | custom-call | tf_op jit(solution)/shard_map/attn_some/pallas_call | solution.py:308
  45.6 9.0 %attn_last.1 = (bf16[1024,768]{1,0:T(8,128)(2,1)}, bf16[1024,768]{1,0:T(8,128)(2,1)}, f32[512,768]{1,0:T(8,128)}, f32[512,768]{1,0:T(8,128)}, f32[8,1024]{1,0:T(8,128)}) custom-call(bf16[272,768]{1,0:T(8,128)(2,1)} %copy-done, bf16[128,768]{1,0:T(8,128)(2,1)} %copy-done.3, ...), custom_call_target="tpu_custom_call", output_to_operand_aliasing={{0}: (12, {}), {1}: (13, {})} | custom-call | tf_op jit(solution)/shard_map/attn_last/pallas_call | solution.py:359
  55.3 30.6 %mid.1 = (f32[16,768]{1,0:T(8,128)}, f32[16,768]{1,0:T(8,128)}, f32[512,768]{1,0:T(8,128)}, bf16[512,768]{1,0:T(8,128)(2,1)}, f32[512,768]{1,0:T(8,128)}, /*inde...) custom-call(s32[4]{0:T(128)} %pad_add_fusion.order_ref, ...), custom_call_target="tpu_custom_call" | custom-call | tf_op jit(solution)/shard_map/mid/pallas_call | solution.py:219
  86.6 8.2 %attn_bwd.2 = (f32[8,128]{1,0:T(8,128)}, bf16[512,256]{1,0:T(8,128)(2,1)}, bf16[1024,256]{1,0:T(8,128)(2,1)}, bf16[1024,256]{1,0:T(8,128)(2,1)}) custom-call(bf16[512,768]{1,0:T(8,128)(2,1)} %get-tuple-element.277.refs_6_.refs_0_, bf16[1024,768]{1,0:T(8,128)(2,1)} %get-tuple-element.278.refs_1_, bf16[1024,768]{1,0:T(8,128)(2,1)} %get-tuple-element.279.refs_2_, ...), custom_call_target="tpu_custom_call" | custom-call | tf_op jit(solution)/shard_map/attn_bwd/pallas_call | solution.py:45
  94.8 4.3 %split_add.4 = (f32[8,128]{1,0:T(8,128)}, bf16[768,768]{1,0:T(8,128)(2,1)}, bf16[768,768]{1,0:T(8,128)(2,1)}) custom-call(s32[7]{0:T(128)S(1)} %stack.28.refs_0_.refs_12_, bf16[1536,768]{1,0:T(8,128)(2,1)} %get-tuple-element.241.refs_1_, bf16[1536,768]{1,0:T(8,128)(2,1)} %collective-permute-done.6.refs_2_), custom_call_target="tpu_custom_call" | custom-call | tf_op jit(solution)/shard_map/split_add/pallas_call | solution.py:45
  106.5 13.5 %attn_bwd.3 = (f32[8,128]{1,0:T(8,128)}, bf16[512,512]{1,0:T(8,128)(2,1)}, bf16[1024,512]{1,0:T(8,128)(2,1)}, bf16[1024,512]{1,0:T(8,128)(2,1)}) custom-call(bf16[512,768]{1,0:T(8,128)(2,1)} %get-tuple-element.277.refs_6_.refs_0_, bf16[1024,768]{1,0:T(8,128)(2,1)} %get-tuple-element.278.refs_1_, bf16[1024,768]{1,0:T(8,128)(2,1)} %get-tuple-element.279.refs_2_, ...), custom_call_target="tpu_custom_call" | custom-call | tf_op jit(solution)/shard_map/attn_bwd/pallas_call | solution.py:45
  125.7 9.3 %weight_grad.1 = (f32[8,128]{1,0:T(8,128)}, f32[2,768]{1,0:T(2,128)}, bf16[1536,768]{1,0:T(8,128)(2,1)}, bf16[1536,768]{1,0:T(8,128)(2,1)}) custom-call(bf16[272,768]{1,0:T(8,128)(2,1)} %copy-done, bf16[128,768]{1,0:T(8,128)(2,1)} %copy-done.3, bf16[144,768]{1,0:T(8,128)(2,1)} %copy-done.2, bf16[272,768]{1,0:T(8,128)(2,1)} %copy-done.1, ...), custom_call_target="tpu_custom_call" | custom-call | tf_op jit(solution)/shard_map/weight_grad/pallas_call | solution.py:45
  141.8 3.6 %collective-permute-start.15 = (f32[28,768]{1,0:T(8,128)S(1)}, f32[28,768]{1,0:T(8,128)S(1)}, u32[]{:S(2)}, u32[]{:S(2)}) collective-permute-start(f32[28,768]{1,0:T(8,128)S(1)} %pad_maximum_fusion.3), channel_id=1, source_target_pairs={{0,2},{1,3},{2,0},{3,1},{4,6},{5,7},{6,4},{7,5},{8,10},{9,11},{10,... | collective-permute-start | bytes 258056 | tf_op jit(solution)/shard_map/ppermute | solution.py:660
  160.0 8.3 %token_grad.1 = (f32[8,128]{1,0:T(8,128)}, f32[256,768]{1,0:T(8,128)}, f32[256,768]{1,0:T(8,128)}, bf16[256,768]{1,0:T(8,128)(2,1)}, bf16[256,768]{1,0:T(8,128)(2,1)}) custom-call(bf16[512,256]{1,0:T(8,128)(2,1)} %get-tuple-element.317.refs_6_.refs_0_, bf16[1024,256]{1,0:T(8,128)(2,1)} %get-tuple-element.318.refs_7_.refs_1_, ...), custom_call_target="tpu_custom_call" | custom-call | tf_op jit(solution)/shard_map/token_grad/pallas_call | solution.py:45
  174.4 6.8 %collective-permute-done.20 = bf16[96,768]{1,0:T(8,128)(2,1)S(1)} collective-permute-done((bf16[96,768]{1,0:T(8,128)(2,1)S(1)}, bf16[96,768]{1,0:T(8,128)(2,1)S(1)}, u32[]{:S(2)}, u32[]{:S(2)}) %collective-permute-start.20) | collective-permute-done | bytes 147488 | tf_op jit(solution)/shard_map/ppermute | solution.py:660
  190.8 8.1 %collective-permute-done.24 = bf16[96,768]{1,0:T(8,128)(2,1)S(1)} collective-permute-done((bf16[96,768]{1,0:T(8,128)(2,1)S(1)}, bf16[96,768]{1,0:T(8,128)(2,1)S(1)}, u32[]{:S(2)}, u32[]{:S(2)}) %collective-permute-start.24) | collective-permute-done | bytes 147488 | tf_op jit(solution)/shard_map/ppermute | solution.py:660
  210.0 6.2 %collective-permute-done.29 = bf16[96,768]{1,0:T(8,128)(2,1)S(1)} collective-permute-done((bf16[96,768]{1,0:T(8,128)(2,1)S(1)}, bf16[96,768]{1,0:T(8,128)(2,1)S(1)}, u32[]{:S(2)}, u32[]{:S(2)}) %collective-permute-start.29) | collective-permute-done | bytes 147488 | tf_op jit(solution)/shard_map/ppermute | solution.py:660
  221.0 4.6 %collective-permute-start.35 = (bf16[96,768]{1,0:T(8,128)(2,1)S(1)}, bf16[96,768]{1,0:T(8,128)(2,1)S(1)}, u32[]{:S(2)}, u32[]{:S(2)}) collective-permute-start(bf16[96,768]{1,0:T(8,128)(2,1)S(1)} %add_convert_fusion.12), channel_id=1, source_target_pairs={{0,2},{1,3},{2,0},{3,1},{4,6},{5,7},{6,4},{7,5},{8,10},{9,11},{10,... | collective-permute-start | bytes 442376 | tf_op jit(solution)/shard_map/ppermute | solution.py:660
  225.7 5.4 %collective-permute-done.35 = bf16[96,768]{1,0:T(8,128)(2,1)S(1)} collective-permute-done((bf16[96,768]{1,0:T(8,128)(2,1)S(1)}, bf16[96,768]{1,0:T(8,128)(2,1)S(1)}, u32[]{:S(2)}, u32[]{:S(2)}) %collective-permute-start.35) | collective-permute-done | bytes 147488 | tf_op jit(solution)/shard_map/ppermute | solution.py:660
  233.3 3.4 %collective-permute-done.32.refs_3_ = bf16[768,768]{1,0:T(8,128)(2,1)S(1)} collective-permute-done((bf16[768,768]{1,0:T(8,128)(2,1)S(1)}, bf16[768,768]{1,0:T(8,128)(2,1)S(1)}, u32[]{:S(2)}, u32[]{:S(2)}) %collective-permute-start.32) | collective-permute-done | bytes 1179680 | tf_op jit(solution)/shard_map/ppermute | solution.py:660
  237.8 8.8 %collective-permute-done.38 = bf16[192,768]{1,0:T(8,128)(2,1)S(1)} collective-permute-done((bf16[192,768]{1,0:T(8,128)(2,1)S(1)}, bf16[192,768]{1,0:T(8,128)(2,1)S(1)}, u32[]{:S(2)}, u32[]{:S(2)}) %collective-permute-start.38) | collective-permute-done | bytes 294944 | tf_op jit(solution)/shard_map/ppermute | solution.py:660
  252.1 4.4 %emit.4 = (f32[8,128]{1,0:T(8,128)}, f32[3072,768]{1,0:T(8,128)}, f32[768,3072]{1,0:T(8,128)}) custom-call(s32[7]{0:T(128)S(1)} %stack.28.refs_0_.refs_12_, bf16[768,768]{1,0:T(8,128)(2,1)S(1)} %bitcast_select_fusion.2.refs_1_, bf16[768,768]{1,0:T(8,128)(2,1)S(1)} %collective-permute-done.33.refs_2_, bf16[768,768]{1,0:T(8,128)(2,1)S(1)} %collective-permute-done.32.refs_3_, ...), custom_call_target="tpu_custom_call" | custom-call | tf_op jit(solution)/shard_map/emit/pallas_call | solution.py:45
  256.5 13.2 %collective-permute-done.42 = bf16[256,768]{1,0:T(8,128)(2,1)S(1)} collective-permute-done((bf16[256,768]{1,0:T(8,128)(2,1)S(1)}, bf16[256,768]{1,0:T(8,128)(2,1)S(1)}, u32[]{:S(2)}, u32[]{:S(2)}) %collective-permute-start.42) | collective-permute-done | bytes 393248 | tf_op jit(solution)/shard_map/ppermute | solution.py:660
  275.7 4.4 %emit.5 = (f32[8,128]{1,0:T(8,128)}, f32[3072,768]{1,0:T(8,128)}, f32[768,3072]{1,0:T(8,128)}) custom-call(s32[7]{0:T(128)S(1)} %stack.28.refs_0_.refs_12_, bf16[768,768]{1,0:T(8,128)(2,1)S(1)} %bitcast_select_fusion.1.refs_1_, bf16[768,768]{1,0:T(8,128)(2,1)S(1)} %collective-permute-done.40.refs_2_, ...), custom_call_target="tpu_custom_call", output_to_operand_aliasing={{1}: (5, {}), {2}: (6, {})} | custom-call | tf_op jit(solution)/shard_map/emit/pallas_call | solution.py:45
  281.8 4.9 %collective-permute-done.43.refs_1_ = bf16[768,768]{1,0:T(8,128)(2,1)S(1)} collective-permute-done((bf16[768,768]{1,0:T(8,128)(2,1)S(1)}, bf16[768,768]{1,0:T(8,128)(2,1)S(1)}, u32[]{:S(2)}, u32[]{:S(2)}) %collective-permute-start.43) | collective-permute-done | bytes 1179680 | tf_op jit(solution)/shard_map/ppermute | solution.py:660
  (219 shorter events, 99.0 us)
Async XLA Ops:
  1.8 18.9 %collective-permute-start.1 = (bf16[128,768]{1,0:T(8,128)(2,1)S(1)}, bf16[128,768]{1,0:T(8,128)(2,1)S(1)}, u32[]{:S(2)}, u32[]{:S(2)}) collective-permute-start(bf16[128,768]{1,0:T(8,128)(2,1)S(1)} %get-tuple-element.448), channel_id=1, source_target_pairs={{0,2},{1,3},{2,0},{3,1},{4,6},{5,7},{6,4},{7,5},{8,10},{9,11},{10,... | collective-permute-start | bytes 589832 | tf_op jit(solution)/shard_map/ppermute | solution.py:660
  6.7 17.9 %collective-permute-start = (bf16[144,768]{1,0:T(8,128)(2,1)S(1)}, bf16[144,768]{1,0:T(8,128)(2,1)S(1)}, u32[]{:S(2)}, u32[]{:S(2)}) collective-permute-start(bf16[144,768]{1,0:T(8,128)(2,1)S(1)} %pad_maximum_fusion.1), channel_id=1, source_target_pairs={{0,2},{1,3},{2,0},{3,1},{4,6},{5,7},{6,4},{7,5},{8,10},{9,11},{10,... | collective-permute-start | bytes 663560 | tf_op jit(solution)/shard_map/ppermute | solution.py:660
  6.9 22.4 %collective-permute-start.2 = (bf16[272,768]{1,0:T(8,128)(2,1)S(1)}, bf16[272,768]{1,0:T(8,128)(2,1)S(1)}, u32[]{:S(2)}, u32[]{:S(2)}) collective-permute-start(bf16[272,768]{1,0:T(8,128)(2,1)S(1)} %pad_maximum_fusion.refs_0_.xa_ref), channel_id=1, source_target_pairs={{0,1},{1,0},{2,3},{3,2},{4,5},{5,4},{6,7},{7,6},{8,9},{9,8},{10,11... | collective-permute-start | bytes 1253384 | tf_op jit(solution)/shard_map/ppermute | solution.py:660
  24.6 30.0 %collective-permute-start.5 = (bf16[256,768]{1,0:T(8,128)(2,1)S(1)}, bf16[256,768]{1,0:T(8,128)(2,1)S(1)}, u32[]{:S(2)}, u32[]{:S(2)}) collective-permute-start(bf16[256,768]{1,0:T(8,128)(2,1)S(1)} %get-tuple-element.238), channel_id=1, source_target_pairs={{0,2},{1,3},{2,0},{3,1},{4,6},{5,7},{6,4},{7,5},{8,10},{9,11},{10,... | collective-permute-start | bytes 1179656 | tf_op jit(solution)/shard_map/ppermute | solution.py:660
  24.6 17.7 %collective-permute-start.3 = (bf16[128,768]{1,0:T(8,128)(2,1)S(1)}, bf16[128,768]{1,0:T(8,128)(2,1)S(1)}, u32[]{:S(2)}, u32[]{:S(2)}) collective-permute-start(bf16[128,768]{1,0:T(8,128)(2,1)S(1)} %collective-permute-done.1.refs_1_.xb_ref), channel_id=1, source_target_pairs={{0,1},{1,0},{2,3},{3,2},{4,5},{5,4},{6,7},{7,6},{8,9},{9,8},{10,11... | collective-permute-start | bytes 589832 | tf_op jit(solution)/shard_map/ppermute | solution.py:660
  28.7 16.2 %collective-permute-start.4 = (bf16[144,768]{1,0:T(8,128)(2,1)S(1)}, bf16[144,768]{1,0:T(8,128)(2,1)S(1)}, u32[]{:S(2)}, u32[]{:S(2)}) collective-permute-start(bf16[144,768]{1,0:T(8,128)(2,1)S(1)} %collective-permute-done.refs_2_.xc_ref), channel_id=1, source_target_pairs={{0,1},{1,0},{2,3},{3,2},{4,5},{5,4},{6,7},{7,6},{8,9},{9,8},{10,11... | collective-permute-start | bytes 663560 | tf_op jit(solution)/shard_map/ppermute | solution.py:660
  99.1 20.9 %collective-permute-start.8 = (bf16[768,768]{1,0:T(8,128)(2,1)}, bf16[768,768]{1,0:T(8,128)(2,1)S(1)}, u32[]{:S(2)}, u32[]{:S(2)}) collective-permute-start(bf16[768,768]{1,0:T(8,128)(2,1)} %get-tuple-element.262), channel_id=1, source_target_pairs={{0,8},{4,20},{8,0},{12,28},{16,24},{20,4},{24,16},{28,12},{1,9},{5... | collective-permute-start | bytes 3538952 | tf_op jit(solution)/shard_map/ppermute | solution.py:660
  103.6 31.4 %collective-permute-start.11 = (bf16[768,768]{1,0:T(8,128)(2,1)}, bf16[768,768]{1,0:T(8,128)(2,1)S(1)}, u32[]{:S(2)}, u32[]{:S(2)}) collective-permute-start(bf16[768,768]{1,0:T(8,128)(2,1)} %get-tuple-element.288), channel_id=1, source_target_pairs={{0,8},{4,20},{8,0},{12,28},{16,24},{20,4},{24,16},{28,12},{1,9},{5... | collective-permute-start | bytes 3538952 | tf_op jit(solution)/shard_map/ppermute | solution.py:660
  104.5 20.0 %collective-permute-start.9 = (bf16[256,768]{1,0:T(8,128)(2,1)S(1)}, bf16[256,768]{1,0:T(8,128)(2,1)}, u32[]{:S(2)}, u32[]{:S(2)}) collective-permute-start(bf16[256,768]{1,0:T(8,128)(2,1)S(1)} %copy-done.22), channel_id=1, source_target_pairs={{0,2},{1,3},{2,0},{3,1},{4,6},{5,7},{6,4},{7,5},{8,10},{9,11},{10,... | collective-permute-start | bytes 1179656 | tf_op jit(solution)/shard_map/ppermute | solution.py:660
  138.7 14.2 %collective-permute-start.13 = (bf16[384,768]{1,0:T(8,128)(2,1)}, bf16[384,768]{1,0:T(8,128)(2,1)}, u32[]{:S(2)}, u32[]{:S(2)}) collective-permute-start(bf16[384,768]{1,0:T(8,128)(2,1)} %get-tuple-element.438), channel_id=1, source_target_pairs={{0,16},{4,12},{8,24},{12,4},{16,0},{20,28},{24,8},{28,20},{1,17},{... | collective-permute-start | bytes 1769480 | tf_op jit(solution)/shard_map/ppermute | solution.py:660
  153.7 16.4 %collective-permute-start.18 = (bf16[768,768]{1,0:T(8,128)(2,1)}, bf16[768,768]{1,0:T(8,128)(2,1)S(1)}, u32[]{:S(2)}, u32[]{:S(2)}) collective-permute-start(bf16[768,768]{1,0:T(8,128)(2,1)} %get-tuple-element.314), channel_id=1, source_target_pairs={{0,8},{4,20},{8,0},{12,28},{16,24},{20,4},{24,16},{28,12},{1,9},{5... | collective-permute-start | bytes 3538952 | tf_op jit(solution)/shard_map/ppermute | solution.py:660
  154.3 14.0 %collective-permute-start.19 = (f32[44,768]{1,0:T(8,128)S(1)}, f32[44,768]{1,0:T(8,128)S(1)}, u32[]{:S(2)}, u32[]{:S(2)}) collective-permute-start(f32[44,768]{1,0:T(8,128)S(1)} %pad_maximum_fusion.2), channel_id=1, source_target_pairs={{0,1},{1,0},{2,3},{3,2},{4,5},{5,4},{6,7},{7,6},{8,9},{9,8},{10,11... | collective-permute-start | bytes 405512 | tf_op jit(solution)/shard_map/ppermute | solution.py:660
  182.9 16.0 %collective-permute-start.23 = (bf16[192,768]{1,0:T(8,128)(2,1)S(1)}, bf16[192,768]{1,0:T(8,128)(2,1)S(1)}, u32[]{:S(2)}, u32[]{:S(2)}) collective-permute-start(bf16[192,768]{1,0:T(8,128)(2,1)S(1)} %bitcast_select_fusion.8), channel_id=1, source_target_pairs={{0,1},{1,0},{2,3},{3,2},{4,5},{5,4},{6,7},{7,6},{8,9},{9,8},{10,11... | collective-permute-start | bytes 884744 | tf_op jit(solution)/shard_map/ppermute | solution.py:660
  183.4 17.7 %collective-permute-start.25 = (bf16[192,768]{1,0:T(8,128)(2,1)S(1)}, bf16[192,768]{1,0:T(8,128)(2,1)S(1)}, u32[]{:S(2)}, u32[]{:S(2)}) collective-permute-start(bf16[192,768]{1,0:T(8,128)(2,1)S(1)} %get-tuple-element.440), channel_id=1, source_target_pairs={{0,1},{1,0},{2,3},{3,2},{4,5},{5,4},{6,7},{7,6},{8,9},{9,8},{10,11... | collective-permute-start | bytes 884744 | tf_op jit(solution)/shard_map/ppermute | solution.py:660
  185.3 13.6 %collective-permute-start.24 = (bf16[96,768]{1,0:T(8,128)(2,1)S(1)}, bf16[96,768]{1,0:T(8,128)(2,1)S(1)}, u32[]{:S(2)}, u32[]{:S(2)}) collective-permute-start(bf16[96,768]{1,0:T(8,128)(2,1)S(1)} %get-tuple-element.452), channel_id=1, source_target_pairs={{0,2},{1,3},{2,0},{3,1},{4,6},{5,7},{6,4},{7,5},{8,10},{9,11},{10,... | collective-permute-start | bytes 442376 | tf_op jit(solution)/shard_map/ppermute | solution.py:660
  202.6 13.6 %collective-permute-start.29 = (bf16[96,768]{1,0:T(8,128)(2,1)S(1)}, bf16[96,768]{1,0:T(8,128)(2,1)S(1)}, u32[]{:S(2)}, u32[]{:S(2)}) collective-permute-start(bf16[96,768]{1,0:T(8,128)(2,1)S(1)} %add_convert_fusion.15), channel_id=1, source_target_pairs={{0,2},{1,3},{2,0},{3,1},{4,6},{5,7},{6,4},{7,5},{8,10},{9,11},{10,... | collective-permute-start | bytes 442376 | tf_op jit(solution)/shard_map/ppermute | solution.py:660
  204.0 13.8 %collective-permute-start.30 = (bf16[96,768]{1,0:T(8,128)(2,1)S(1)}, bf16[96,768]{1,0:T(8,128)(2,1)S(1)}, u32[]{:S(2)}, u32[]{:S(2)}) collective-permute-start(bf16[96,768]{1,0:T(8,128)(2,1)S(1)} %get-tuple-element.450), channel_id=1, source_target_pairs={{0,2},{1,3},{2,0},{3,1},{4,6},{5,7},{6,4},{7,5},{8,10},{9,11},{10,... | collective-permute-start | bytes 442376 | tf_op jit(solution)/shard_map/ppermute | solution.py:660
  205.8 14.4 %collective-permute-start.31 = (bf16[256,768]{1,0:T(8,128)(2,1)S(1)}, bf16[256,768]{1,0:T(8,128)(2,1)S(1)}, u32[]{:S(2)}, u32[]{:S(2)}) collective-permute-start(bf16[256,768]{1,0:T(8,128)(2,1)S(1)} %copy-done.21), channel_id=1, source_target_pairs={{0,1},{1,0},{2,3},{3,2},{4,5},{5,4},{6,7},{7,6},{8,9},{9,8},{10,11... | collective-permute-start | bytes 1179656 | tf_op jit(solution)/shard_map/ppermute | solution.py:660
  220.4 16.3 %collective-permute-start.32 = (bf16[768,768]{1,0:T(8,128)(2,1)S(1)}, bf16[768,768]{1,0:T(8,128)(2,1)S(1)}, u32[]{:S(2)}, u32[]{:S(2)}) collective-permute-start(bf16[768,768]{1,0:T(8,128)(2,1)S(1)} %bitcast_select_fusion.2.refs_1_), channel_id=1, source_target_pairs={{0,8},{4,20},{8,0},{12,28},{16,24},{20,4},{24,16},{28,12},{1,9},{5... | collective-permute-start | bytes 3538952 | tf_op jit(solution)/shard_map/ppermute | solution.py:660
  247.0 22.7 %collective-permute-start.40 = (bf16[768,768]{1,0:T(8,128)(2,1)S(1)}, bf16[768,768]{1,0:T(8,128)(2,1)S(1)}, u32[]{:S(2)}, u32[]{:S(2)}) collective-permute-start(bf16[768,768]{1,0:T(8,128)(2,1)S(1)} %bitcast_select_fusion.1.refs_1_), channel_id=1, source_target_pairs={{0,4},{4,0},{8,12},{12,8},{16,20},{20,16},{24,28},{28,24},{1,5},{5... | collective-permute-start | bytes 3538952 | tf_op jit(solution)/shard_map/ppermute | solution.py:660
  247.1 22.6 %collective-permute-start.39 = (bf16[768,768]{1,0:T(8,128)(2,1)S(1)}, bf16[768,768]{1,0:T(8,128)(2,1)S(1)}, u32[]{:S(2)}, u32[]{:S(2)}) collective-permute-start(bf16[768,768]{1,0:T(8,128)(2,1)S(1)} %bitcast_select_fusion.1.refs_1_), channel_id=1, source_target_pairs={{0,8},{4,20},{8,0},{12,28},{16,24},{20,4},{24,16},{28,12},{1,9},{5... | collective-permute-start | bytes 3538952 | tf_op jit(solution)/shard_map/ppermute | solution.py:660
  248.0 21.7 %collective-permute-start.41 = (bf16[384,768]{1,0:T(8,128)(2,1)S(1)}, bf16[384,768]{1,0:T(8,128)(2,1)S(1)}, u32[]{:S(2)}, u32[]{:S(2)}) collective-permute-start(bf16[384,768]{1,0:T(8,128)(2,1)S(1)} %bitcast_select_fusion.3), channel_id=1, source_target_pairs={{0,16},{4,12},{8,24},{12,4},{16,0},{20,28},{24,8},{28,20},{1,17},{... | collective-permute-start | bytes 1769480 | tf_op jit(solution)/shard_map/ppermute | solution.py:660
  249.2 20.5 %collective-permute-start.42 = (bf16[256,768]{1,0:T(8,128)(2,1)S(1)}, bf16[256,768]{1,0:T(8,128)(2,1)S(1)}, u32[]{:S(2)}, u32[]{:S(2)}) collective-permute-start(bf16[256,768]{1,0:T(8,128)(2,1)S(1)} %add_convert_fusion.5), channel_id=1, source_target_pairs={{0,2},{1,3},{2,0},{3,1},{4,6},{5,7},{6,4},{7,5},{8,10},{9,11},{10,... | collective-permute-start | bytes 1179656 | tf_op jit(solution)/shard_map/ppermute | solution.py:660
  270.5 16.2 %collective-permute-start.43 = (bf16[768,768]{1,0:T(8,128)(2,1)S(1)}, bf16[768,768]{1,0:T(8,128)(2,1)S(1)}, u32[]{:S(2)}, u32[]{:S(2)}) collective-permute-start(bf16[768,768]{1,0:T(8,128)(2,1)S(1)} %bitcast_select_fusion.refs_1_), channel_id=1, source_target_pairs={{0,8},{4,20},{8,0},{12,28},{16,24},{20,4},{24,16},{28,12},{1,9},{5... | collective-permute-start | bytes 3538952 | tf_op jit(solution)/shard_map/ppermute | solution.py:660
  (47 other events, 347.6 us)
